TPU v7x, 32 devices: a whole 2x2x4 slice. The times are simulated.
32 devices in a mesh: groups: 2 (over x), seq: 16 (over z, y, core).
Axes of the slice: x: 2, y: 2, z: 4, core: 2. Of those that a mesh axis runs over, the one named last changes fastest.
Arguments:
- mixer_in: bfloat16 [2048, 4608], P(('groups', 'seq')), parts along dimension 0, may hold values from -6 to 6
- gate_in: bfloat16 [2048, 4096], P(('groups', 'seq')), parts along dimension 0, may hold values from -6 to 6
- step_raw: bfloat16 [2048, 64], P(('groups', 'seq')), parts along dimension 0, may hold values from -3 to 3
- step_bias: float32 [64], replicated, may hold values from -1.5 to 0
- rate_log: float32 [64], replicated, as said below
- conv_weight: float32 [4, 4608], replicated, may hold values from -3 to 3
- conv_bias: float32 [4608], replicated, may hold values from -0.5 to 0.5
- skip_gain: float32 [64], replicated, may hold values from 0.5 to 1.5
- norm_gain: float32 [4096], replicated, may hold values from 0.1 to 1.9
- doc_lengths: int32 [12], P('groups'), parts along dimension 0, may hold values from 1 to 512, 1024 in all
Outputs:
- mixed_out: bfloat16 [2048, 4096], P(('groups', 'seq')), parts along dimension 0
There are 2 independent parts, one for each index of `groups`. A program takes and returns all parts, laid end to end along the dimension named above; an argument that names none is the same for every part. Nothing has to cross between parts.
Inputs may be any that keep to these rules, and one draw needn't show every extreme that they name: `doc_lengths`: the 6 lengths of a part sum to 1024, and the longest is exactly 512. exp(rate_log) lies between 0.3 / 1024 and 0.08.
All inputs are finite; a program needn't handle non-finite values.
Results may differ from a plain program's by a relative error of at most 0.0043.
Values may be sent and summed in bfloat16 or wider, within the bound.
No kernel may reach another device: no remote copies, remote signals or barrier semaphores. Data moves between devices by JAX's collectives and lax.ppermute only.
A program may use at most 320 MiB of HBM per device.

v0:
```python
import jax
import jax.numpy as jnp
from jax import lax
from jax.sharding import PartitionSpec as P

GROUPS = 4


epsilon = 1e-05


def from_behind(block, axis, distance):
    devices = range(lax.axis_size(axis))
    route = [(i - distance, i) for i in devices if i - distance in devices]
    return lax.ppermute(block, axis, route)


def doc_index(doc_lengths, positions):
    doc_ends = jnp.cumsum(doc_lengths)
    inside = jnp.sum((positions[:, None] >= doc_ends[None, :]).astype(jnp.int32), axis=1)
    return jnp.where(positions >= 0, inside, -1)


def convolve(tok_block, rim_rows, positions, doc_lengths, conv_weight, conv_bias):
    rim_width = rim_rows.shape[0]
    length = tok_block.shape[0]
    padded = jnp.concatenate([rim_rows, tok_block], axis=0).astype(jnp.float32)
    all_positions = jnp.concatenate([positions[:rim_width] - rim_width, positions])
    doc_ids = doc_index(doc_lengths, all_positions)
    own_doc = doc_ids[rim_width:]
    summed = jnp.zeros(tok_block.shape, jnp.float32) + conv_bias[None, :]
    for offset in range(rim_width + 1):
        same_doc = (doc_ids[offset : offset + length] == own_doc)[:, None]
        summed = summed + conv_weight[offset][None, :] * jnp.where(
            same_doc, padded[offset : offset + length], 0.0
        )
    return (jax.nn.silu(summed).astype(jnp.bfloat16), own_doc, doc_ids[rim_width - 1])


def group_terms(
    conv_x,
    conv_b,
    conv_c,
    step_size,
    log_sums,
    own_doc,
    prior_doc,
    skip_gain,
    member,
    group_heads,
    state_size,
):
    length = conv_x.shape[0]
    head_size = conv_x.shape[1] // skip_gain.shape[0]
    first = member * group_heads
    picked = slice(first, first + group_heads)
    x_group = conv_x[:, first * head_size : (first + group_heads) * head_size].reshape(
        length, group_heads, head_size
    )
    b_group = conv_b[:, member * state_size : (member + 1) * state_size]
    c_group = conv_c[:, member * state_size : (member + 1) * state_size]
    scores = jnp.einsum("tn,sn->ts", c_group, b_group, preferred_element_type=jnp.float32)
    places = jnp.arange(length, dtype=jnp.int32)
    causal = (places[:, None] >= places[None, :]) & (own_doc[:, None] == own_doc[None, :])
    head_logs = log_sums[:, picked].T
    log_gaps = head_logs[:, :, None] - head_logs[:, None, :]
    decays = jnp.exp(jnp.where(causal[None], log_gaps, -jnp.inf))
    head_steps = step_size[:, picked].T
    weights = (decays * scores[None] * head_steps[:, None, :]).astype(jnp.bfloat16)
    within = jnp.einsum("hts,shp->thp", weights, x_group, preferred_element_type=jnp.float32)
    within = within + skip_gain[picked][None, :, None] * x_group.astype(jnp.float32)
    final_log = log_sums[-1, picked]
    tail_scale = (
        jnp.exp(final_log[None, :] - log_sums[:, picked])
        * step_size[:, picked]
        * (own_doc == own_doc[-1]).astype(jnp.float32)[:, None]
    )
    weighted = (x_group * tail_scale[:, :, None]).astype(jnp.bfloat16)
    local_state = jnp.einsum("shp,sn->hpn", weighted, b_group, preferred_element_type=jnp.float32)
    inward = jnp.exp(log_sums[:, picked]) * (own_doc == prior_doc).astype(jnp.float32)[:, None]
    passing = jnp.exp(final_log) * (own_doc[-1] == prior_doc).astype(jnp.float32)
    return (within, local_state, inward, passing)


def carry_term(c_group, state_in, inward):
    rounded = state_in.astype(jnp.bfloat16)
    term = jnp.einsum("tn,hpn->thp", c_group, rounded, preferred_element_type=jnp.float32)
    return term * inward[:, :, None]


def finish(mixed_out, gate_rows, norm_gain):
    length, head_count, head_size = mixed_out.shape
    gated = mixed_out * jax.nn.silu(gate_rows.astype(jnp.float32)).reshape(
        length, head_count, head_size
    )
    inv_rms = lax.rsqrt(jnp.mean(gated * gated, axis=2, keepdims=True) + epsilon)
    return ((gated * inv_rms).reshape(length, head_count * head_size) * norm_gain[None, :]).astype(
        jnp.bfloat16
    )


def linked(earlier, later):
    return (earlier[0] * later[0], later[0][..., None] * earlier[1] + later[1])


def on_device(
    mixer_in,
    gate_in,
    step_raw,
    step_bias,
    rate_log,
    conv_weight,
    conv_bias,
    skip_gain,
    norm_gain,
    doc_lengths,
):
    tok_rows = mixer_in.shape[0]
    rim_width = conv_weight.shape[0] - 1
    head_count = rate_log.shape[0]
    inner_width = gate_in.shape[1]
    head_width = inner_width // head_count
    state_size = (mixer_in.shape[1] - inner_width) // (2 * GROUPS)
    group_heads = head_count // GROUPS
    rim_rows = from_behind(mixer_in[tok_rows - rim_width :], "seq", 1)
    positions = lax.axis_index("seq") * tok_rows + jnp.arange(tok_rows, dtype=jnp.int32)
    mixed, own_doc, prior_doc = convolve(
        mixer_in, rim_rows, positions, doc_lengths, conv_weight, conv_bias
    )
    conv_x = mixed[:, :inner_width]
    conv_b = mixed[:, inner_width : inner_width + GROUPS * state_size]
    conv_c = mixed[:, inner_width + GROUPS * state_size :]
    step_size = jax.nn.softplus(step_raw.astype(jnp.float32) + step_bias[None, :])
    log_sums = jnp.cumsum(-jnp.exp(rate_log)[None, :] * step_size, axis=0)
    pieces = [
        group_terms(
            conv_x,
            conv_b,
            conv_c,
            step_size,
            log_sums,
            own_doc,
            prior_doc,
            skip_gain,
            member,
            group_heads,
            state_size,
        )
        for member in range(GROUPS)
    ]
    passings = jnp.concatenate([piece_set[3] for piece_set in pieces], axis=0)
    local_states = jnp.concatenate([piece_set[1] for piece_set in pieces], axis=0)
    row_count = head_count * head_width
    row_pass = jnp.repeat(passings, head_width)[None, :]
    row_states = local_states.reshape(1, row_count, state_size)
    block_states, block_pass = (
        lax.all_to_all(row_states, "seq", split_axis=1, concat_axis=0, tiled=True),
        lax.all_to_all(row_pass, "seq", split_axis=1, concat_axis=0, tiled=True),
    )
    inclusive = lax.associative_scan(linked, (block_pass, block_states), axis=0)
    exclusive = jnp.concatenate([jnp.zeros_like(block_states[:1]), inclusive[1][:-1]], axis=0)
    returned = lax.all_to_all(
        exclusive.astype(jnp.bfloat16), "seq", split_axis=0, concat_axis=1, tiled=True
    ).astype(exclusive.dtype)
    whole_state = returned.reshape(head_count, head_width, state_size)
    arrivals = [
        whole_state[member * group_heads : (member + 1) * group_heads] for member in range(GROUPS)
    ]
    results = []
    for member in range(GROUPS):
        c_group = conv_c[:, member * state_size : (member + 1) * state_size]
        results.append(pieces[member][0] + carry_term(c_group, arrivals[member], pieces[member][2]))
    mixed_out = jnp.concatenate(results, axis=1)
    return finish(mixed_out, gate_in, norm_gain)


def solution(mesh):
    return jax.shard_map(
        on_device,
        mesh=mesh,
        in_specs=(
            P(("groups", "seq"), None),
            P(("groups", "seq"), None),
            P(("groups", "seq"), None),
            P(),
            P(),
            P(),
            P(),
            P(),
            P(),
            P("groups"),
        ),
        out_specs=P(("groups", "seq"), None),
        check_vma=False,
    )
```

profile of v0, /device:TPU:0, one launch (start us, length us, event | category | flops | bytes accessed | tf_op | source)
XLA Modules:
  0.0 141.2 jit_solution(8743664559068083938)
XLA Ops:
  1.0 2.4 %collective-permute-start = (bf16[3,4608]{1,0:T(4,128)(2,1)S(1)}, bf16[3,4608]{1,0:T(4,128)(2,1)S(1)}, u32[]{:S(2)}, u32[]{:S(2)}) collective-permute-start(bf16[3,4608]{1,0:T(4,128)(2,1)S(1)} %slice.290), channel_id=1, source_target_pairs={{0,1},{1,2},{2,3},{3,4},{4,5},{5,6},{6,7},{7,8},{8,9},{9,10},{10,1... | collective-permute-start | bytes 82952 | tf_op jit(solution)/shard_map/ppermute | solution.py:15
  10.0 7.2 %all-to-all-start.1 = ((f32[1,16,256]{2,0,1:T(1,128)}), f32[1,16,256]{2,0,1:T(1,128)S(1)}, u32[]{:S(2)}, u32[]{:S(2)}) async-start(f32[1,16,256]{2,0,1:T(1,128)} %broadcast_in_dim.68), calls=%async_computation.1 | async-start | bytes 32768 | tf_op jit(solution)/shard_map/all_to_all | solution.py:158
  17.2 1.3 compare_convert_fusion
  24.7 19.3 %reduce.24 = f32[4096,64]{1,0:T(8,128)} reduce(f32[4096,1,64]{2,1,0:T(1,128)S(1)} %bitcast.110, f32[]{:T(128)} %broadcast.143), dimensions={1}, to_apply=%bitcast.95.reduce_sub_computation | reduce | bytes 2097156
  44.1 3.4 %reshape.249 = f32[16,1,16384]{2,1,0:T(1,128)} reshape(f32[4096,64]{1,0:T(8,128)} %reduce.24) | data formatting | bytes 2097152
  47.5 6.2 %all-to-all-start = ((f32[16,1,16384]{2,1,0:T(1,128)}), f32[16,1,16384]{2,1,0:T(1,128)S(1)}, u32[]{:S(2)}, u32[]{:S(2)}) async-start(f32[16,1,16384]{2,1,0:T(1,128)} %reshape.249), calls=%async_computation | async-start | bytes 2097152 | tf_op jit(solution)/shard_map/all_to_all | solution.py:157
  57.6 19.0 %all-to-all-done = f32[16,1,16384]{2,1,0:T(1,128)S(1)} async-done(((f32[16,1,16384]{2,1,0:T(1,128)}), f32[16,1,16384]{2,1,0:T(1,128)S(1)}, u32[]{:S(2)}, u32[]{:S(2)}) %all-to-all-start) | async-done | bytes 1048608 | tf_op jit(solution)/shard_map/all_to_all | solution.py:157
  76.5 3.1 %reduce.25 = f32[16,16384]{1,0:T(8,128)S(1)} reduce(f32[16,1,16384]{2,1,0:T(1,128)S(1)} %all-to-all-done, f32[]{:T(128)} %broadcast.143), dimensions={1}, to_apply=%all_to_all.13.reduce_sub_computation | reduce | bytes 2097156 | tf_op jit(solution)/shard_map/all_to_all | solution.py:157
  79.7 2.6 %reshape.250 = f32[4096,1,64]{2,1,0:T(1,128)S(1)} reshape(f32[16,16384]{1,0:T(8,128)S(1)} %reduce.25) | data formatting | bytes 2097152
  84.4 2.3 %copy.183 = f32[8,256,64]{1,2,0:T(8,128)} copy(f32[8,256,64]{2,1,0:T(8,128)} %get-tuple-element.16) | data formatting | bytes 1048576
  87.9 1.4 multiply_add_fusion
  95.2 1.8 %pad.32 = f32[8,256,64]{1,2,0:T(8,128)S(1)} pad(f32[4,256,64]{1,2,0:T(8,128)} %add.148, f32[]{:T(128)} %constant.34.clone.1), padding=1_0_1x0_0_0x0_0_0 | pad | bytes 786436 | tf_op jit(solution)/shard_map/pad | solution.py:160
  101.4 6.9 %all-to-all-start.2 = ((bf16[16,256,64]{1,2,0:T(8,128)(2,1)}), bf16[16,256,64]{1,2,0:T(8,128)(2,1)}, u32[]{:S(2)}, u32[]{:S(2)}) async-start(bf16[16,256,64]{1,2,0:T(8,128)(2,1)} %concatenate.37), calls=%async_computation.2 | async-start | bytes 1048576 | tf_op jit(solution)/shard_map/all_to_all | solution.py:162
  109.5 1.6 %fusion.73 = f32[64,64]{1,0:T(8,128)} fusion(bf16[64,4608]{1,0:T(8,128)(2,1)} %copy-done.3), kind=kOutput, calls=%fused_computation.123 | convolution fusion | flops 524288 | bytes 49152 | tf_op jit(solution)/shard_map/tn,sn->ts/dot_general | solution.py:62
  111.0 1.5 %fusion.76 = f32[64,64]{1,0:T(8,128)} fusion(bf16[64,4608]{1,0:T(8,128)(2,1)} %copy-done.3), kind=kOutput, calls=%fused_computation.126 | convolution fusion | flops 524288 | bytes 49152 | tf_op jit(solution)/shard_map/tn,sn->ts/dot_general | solution.py:62
  112.5 1.5 %fusion.79 = f32[64,64]{1,0:T(8,128)} fusion(bf16[64,4608]{1,0:T(8,128)(2,1)} %copy-done.3), kind=kOutput, calls=%fused_computation.129 | convolution fusion | flops 524288 | bytes 49152 | tf_op jit(solution)/shard_map/tn,sn->ts/dot_general | solution.py:62
  114.1 1.5 %fusion.88 = f32[64,64]{1,0:T(8,128)} fusion(bf16[64,4608]{1,0:T(8,128)(2,1)} %copy-done.3), kind=kOutput, calls=%fused_computation.138 | convolution fusion | flops 524288 | bytes 49152 | tf_op jit(solution)/shard_map/tn,sn->ts/dot_general | solution.py:62
  115.5 7.0 %all-to-all-done.2 = bf16[16,256,64]{1,2,0:T(8,128)(2,1)} async-done(((bf16[16,256,64]{1,2,0:T(8,128)(2,1)}), bf16[16,256,64]{1,2,0:T(8,128)(2,1)}, u32[]{:S(2)}, u32[]{:S(2)}) %all-to-all-start.2) | async-done | bytes 524320 | tf_op jit(solution)/shard_map/all_to_all | solution.py:162
  122.6 1.3 copy.168
  130.9 1.9 %pad_maximum_fusion.1 = (f32[64,64,64]{0,2,1:T(8,128)}, f32[64,64]{0,1:T(8,128)S(1)}) fusion(f32[64,16,64]{0,2,1:T(8,128)S(1)} %fusion.7, f32[64,16,64]{0,2,1:T(8,128)S(1)} %fusion.5, f32[64,16,64]{0,2,1:T(8,128)S(1)} %fusion.3, f32[64,16,64]{0,2,1:T(8,128)S(1)} %fusion.1, f32[64,4096]{0,1:T(8,128)S(1)} %copy.174), kind=kLoop, calls=%fused_computation.1 | loop fusion | flops 1568768 | bytes 3162112 | tf_op jit(solution)/shard_map/concatenate | solution.py:173
  132.9 1.9 %mul.516 = f32[64,64,64]{2,1,0:T(8,128)} broadcast(f32[64,64]{1,0:T(8,128)S(1)} %copy.175), dimensions={0,1} | broadcast | bytes 1064960 | tf_op jit(solution)/shard_map/mul | solution.py:97
  134.8 2.3 %mul.517 = f32[64,4096]{1,0:T(8,128)S(1)} reshape(f32[64,64,64]{2,1,0:T(8,128)} %mul.516) | data formatting | bytes 2097152 | tf_op jit(solution)/shard_map/mul | solution.py:97
  137.1 1.6 %copy.173 = f32[64,4096]{1,0:T(8,128)} copy(f32[64,4096]{0,1:T(8,128)S(1)} %bitcast.109) | data formatting | bytes 2097152 | tf_op jit(solution)/shard_map/concatenate | solution.py:173
  138.7 2.5 %multiply_convert_fusion.1 = bf16[64,4096]{1,0:T(8,128)(2,1)} fusion(f32[64,4096]{1,0:T(8,128)S(1)} %mul.517, f32[64,4096]{1,0:T(8,128)} %copy.173, f32[4096]{0:T(1024)S(1)} %copy-done.35, bf16[64,4096]{1,0:T(8,128)(2,1)} %param.11), kind=kLoop, calls=%fused_computation.36 | loop fusion | flops 2359296 | bytes 3162112 | tf_op jit(solution)/shard_map/convert_element_type | solution.py:97
  (203 shorter events, 37.6 us)
Async XLA Ops:
  0.0 20.8 %copy-start.16 = (bf16[64,4608]{1,0:T(8,128)(2,1)S(1)}, bf16[64,4608]{1,0:T(8,128)(2,1)}, u32[]{:S(2)}) copy-start(bf16[64,4608]{1,0:T(8,128)(2,1)} %param.10) | copy-start | bytes 1769476
  1.0 19.9 %collective-permute-start = (bf16[3,4608]{1,0:T(4,128)(2,1)S(1)}, bf16[3,4608]{1,0:T(4,128)(2,1)S(1)}, u32[]{:S(2)}, u32[]{:S(2)}) collective-permute-start(bf16[3,4608]{1,0:T(4,128)(2,1)S(1)} %slice.290), channel_id=1, source_target_pairs={{0,1},{1,2},{2,3},{3,4},{4,5},{5,6},{6,7},{7,8},{8,9},{9,10},{10,1... | collective-permute-start | bytes 82952 | tf_op jit(solution)/shard_map/ppermute | solution.py:15
  10.0 37.5 %all-to-all-start.1 = ((f32[1,16,256]{2,0,1:T(1,128)}), f32[1,16,256]{2,0,1:T(1,128)S(1)}, u32[]{:S(2)}, u32[]{:S(2)}) async-start(f32[1,16,256]{2,0,1:T(1,128)} %broadcast_in_dim.68), calls=%async_computation.1 | async-start | bytes 32768 | tf_op jit(solution)/shard_map/all_to_all | solution.py:158
  18.5 2.5 %copy-start.34 = (f32[4608]{0:T(1024)S(1)}, f32[4608]{0:T(1024)}, u32[]{:S(2)}) copy-start(f32[4608]{0:T(1024)} %param.16) | copy-start | bytes 55300
  47.5 6.9 %copy-start.5 = (bf16[64,4096]{1,0:T(8,128)(2,1)S(1)}, bf16[64,4096]{1,0:T(8,128)(2,1)}, u32[]{:S(2)}) copy-start(bf16[64,4096]{1,0:T(8,128)(2,1)} %param.11) | copy-start | bytes 1572868
  47.5 29.0 %all-to-all-start = ((f32[16,1,16384]{2,1,0:T(1,128)}), f32[16,1,16384]{2,1,0:T(1,128)S(1)}, u32[]{:S(2)}, u32[]{:S(2)}) async-start(f32[16,1,16384]{2,1,0:T(1,128)} %reshape.249), calls=%async_computation | async-start | bytes 2097152 | tf_op jit(solution)/shard_map/all_to_all | solution.py:157
  55.8 20.7 %copy-start.36 = (f32[2,256]{1,0:T(2,128)}, f32[2,256]{1,0:T(2,128)S(1)}, u32[]{:S(2)}) copy-start(f32[2,256]{1,0:T(2,128)S(1)} %slice.339) | copy-start | bytes 6148
  87.9 2.7 %copy-start.2 = (f32[7,256,64]{2,1,0:T(8,128)S(1)}, f32[7,256,64]{2,1,0:T(8,128)}, u32[]{:S(2)}) copy-start(f32[7,256,64]{2,1,0:T(8,128)} %slice.351) | copy-start | bytes 1376260
  89.2 3.4 %copy-start.44 = (f32[1,256]{1,0:T(1,128)S(1)}, f32[1,256]{1,0:T(1,128)}, u32[]{:S(2)}) copy-start(f32[1,256]{1,0:T(1,128)} %slice_multiply_fusion.1) | copy-start | bytes 3076
  90.0 2.7 %copy-start.45 = (f32[1,256]{1,0:T(1,128)S(1)}, f32[1,256]{1,0:T(1,128)}, u32[]{:S(2)}) copy-start(f32[1,256]{1,0:T(1,128)} %slice.391) | copy-start | bytes 3076
  94.4 3.5 %copy-start.17 = (f32[1,256,64]{1,2,0:T(8,128)S(1)}, f32[1,256,64]{1,2,0:T(8,128)}, u32[]{:S(2)}) copy-start(f32[1,256,64]{1,2,0:T(8,128)} %slice.389) | copy-start | bytes 196612
  100.5 7.7 %copy-start.39 = (f32[64]{0:T(128)S(1)}, f32[64]{0:T(128)}, u32[]{:S(2)}) copy-start(f32[64]{0:T(128)} %param.17) | copy-start | bytes 772
  100.5 8.3 %copy-start.1 = (f32[64,4096]{1,0:T(8,128)S(1)}, f32[64,4096]{1,0:T(8,128)}, u32[]{:S(2)}) copy-start(f32[64,4096]{1,0:T(8,128)} %convert_multiply_fusion) | copy-start | bytes 3145732
  101.4 21.2 %all-to-all-start.2 = ((bf16[16,256,64]{1,2,0:T(8,128)(2,1)}), bf16[16,256,64]{1,2,0:T(8,128)(2,1)}, u32[]{:S(2)}, u32[]{:S(2)}) async-start(bf16[16,256,64]{1,2,0:T(8,128)(2,1)} %concatenate.37), calls=%async_computation.2 | async-start | bytes 1048576 | tf_op jit(solution)/shard_map/all_to_all | solution.py:162
  124.4 2.6 %copy-start.20 = (f32[64,16]{0,1:T(8,128)S(1)}, f32[64,16]{0,1:T(8,128)}, u32[]{:S(2)}) copy-start(f32[64,16]{0,1:T(8,128)} %get-tuple-element.51) | copy-start | bytes 12292
  124.7 3.4 %copy-start.19 = (f32[64,16]{0,1:T(8,128)S(1)}, f32[64,16]{0,1:T(8,128)}, u32[]{:S(2)}) copy-start(f32[64,16]{0,1:T(8,128)} %get-tuple-element.54) | copy-start | bytes 12292
  125.9 3.1 %copy-start.15 = (bf16[64,1024]{0,1:T(8,128)(2,1)S(1)}, bf16[64,1024]{0,1:T(8,128)(2,1)}, u32[]{:S(2)}) copy-start(bf16[64,1024]{0,1:T(8,128)(2,1)} %copy-done.14) | copy-start | bytes 393220
  125.9 3.1 %copy-start.25 = (f32[64,64]{1,0:T(8,128)S(1)}, f32[64,64]{1,0:T(8,128)}, u32[]{:S(2)}) copy-start(f32[64,64]{1,0:T(8,128)} %fusion.73) | copy-start | bytes 49156
  126.0 3.1 %copy-start.33 = (f32[64,16]{0,1:T(8,128)S(1)}, f32[64,16]{0,1:T(8,128)}, u32[]{:S(2)}) copy-start(f32[64,16]{0,1:T(8,128)} %copy-done.32) | copy-start | bytes 12292
  126.0 3.1 %copy-start.38 = (pred[64,64]{1,0:T(8,128)(4,1)S(1)}, pred[64,64]{1,0:T(8,128)(4,1)}, u32[]{:S(2)}) copy-start(pred[64,64]{1,0:T(8,128)(4,1)} %fusion.63) | copy-start | bytes 12292
  126.0 3.1 %copy-start.43 = (f32[16,64]{1,0:T(8,128)S(1)}, f32[16,64]{1,0:T(8,128)}, u32[]{:S(2)}) copy-start(f32[16,64]{1,0:T(8,128)} %get-tuple-element.36) | copy-start | bytes 12292
  126.0 3.1 %copy-start.49 = (f32[16]{0:T(128)S(1)}, f32[16]{0:T(128)}, u32[]{:S(2)}) copy-start(f32[16]{0:T(128)} %get-tuple-element.57) | copy-start | bytes 196
  127.0 2.5 %copy-start.13 = (bf16[64,1024]{0,1:T(8,128)(2,1)S(1)}, bf16[64,1024]{0,1:T(8,128)(2,1)}, u32[]{:S(2)}) copy-start(bf16[64,1024]{0,1:T(8,128)(2,1)} %copy-done.12) | copy-start | bytes 393220
  127.0 2.5 %copy-start.24 = (f32[64,64]{1,0:T(8,128)S(1)}, f32[64,64]{1,0:T(8,128)}, u32[]{:S(2)}) copy-start(f32[64,64]{1,0:T(8,128)} %fusion.76) | copy-start | bytes 49156
  (30 other events, 43.5 us)
where the time goes:
time: 143 us; the launch traced here: 141 us
  other arithmetic  42.4 us (30%)
  local copies, waits for them, and re-layouts  35.6 us (25%)
  waiting for transfers between devices  26 us (18%)
  starting transfers between devices  22.6 us (16%)
  matrix products  12.4 us (9%)
  between operations  2.27 us (2%)
    unnamed x1, other arithmetic  19.3 us
    all_to_all x1, waiting for transfers between devices, on_device(): lax.all_to_all(row_states, 'seq', split_axis=1, concat_axis=0, tiled=True)  19 us
    unnamed x114, local copies, waits for them, and re-layouts  14.4 us
    all_to_all x1, starting transfers between devices, on_device(): lax.all_to_all(row_pass, 'seq', split_axis=1, concat_axis=0, tiled=True)  7.21 us
    all_to_all x1, waiting for transfers between devices, on_device(): lax.all_to_all(exclusive.astype(jnp.bfloat16), 'seq', split_axis=0, conca...  7.03 us
    all_to_all x1, starting transfers between devices, on_device(): lax.all_to_all(exclusive.astype(jnp.bfloat16), 'seq', split_axis=0, conca...  6.85 us
    all_to_all x1, starting transfers between devices, on_device(): lax.all_to_all(row_states, 'seq', split_axis=1, concat_axis=0, tiled=True)  6.15 us
    dot_general x4, matrix products, group_terms(): jnp.einsum('tn,sn->ts', c_group, b_group, preferred_element_type=jnp.floa...  6.04 us
  transfers between devices with their start and end apart: 4, of which 2 were waited for; matrix products, arithmetic and copies ran while one was open for 33% of the time, Pallas kernels for 0%

commit v1 on v0

v1 whole, which is shorter than its diff:
```python
import functools

import jax
import jax.numpy as jnp
from jax import lax
from jax.experimental import pallas as pl
from jax.experimental.pallas import tpu as pltpu
from jax.sharding import PartitionSpec as P

GROUPS = 4
PAIR = 2
RIM = 8
EPSILON = 1e-05
F32 = jnp.float32
BF16 = jnp.bfloat16
VMEM = pl.BlockSpec(memory_space=pltpu.VMEM)
SMEM = pl.BlockSpec(memory_space=pltpu.SMEM)
ANY = pl.BlockSpec(memory_space=pl.ANY)


def dot(a, b, dims=((1,), (0,))):
    return lax.dot_general(a, b, (dims, ((), ())), preferred_element_type=F32)


def silu(v):
    half = 0.5 * v
    return half + half * jnp.tanh(half)


def split(a, parts):
    out = []
    for _ in range(parts):
        top = a.astype(BF16)
        out.append(top)
        a = a - top.astype(F32)
    return out


def doc_of(lengths, position):
    end, found = jnp.int32(0), jnp.zeros_like(position)
    for i in range(lengths.shape[0]):
        end = end + lengths[i]
        found = found + jnp.where(position >= end, 1, 0)
    return jnp.where(position >= 0, found, -1)


def log_sums(raw, bias, rate_log):
    v = raw.astype(F32) + bias
    step = jnp.maximum(v, 0.0) + jnp.log(1.0 + jnp.exp(-jnp.abs(v)))
    change = -jnp.exp(rate_log) * step
    rows = raw.shape[0]
    shape = (rows, 3 * rows)
    behind = lax.broadcasted_iota(jnp.int32, shape, 1) % rows
    lower = jnp.where(behind <= lax.broadcasted_iota(jnp.int32, shape, 0), 1.0, 0.0)
    sums = dot(lower.astype(BF16), jnp.concatenate(split(change, 3), axis=0))
    return step, sums


def selector(heads, columns, width, first):
    shape = (3 * heads, columns)
    head = lax.broadcasted_iota(jnp.int32, shape, 0) % heads
    owner = lax.broadcasted_iota(jnp.int32, shape, 1) // width + first
    return jnp.where(head == owner, 1.0, 0.0).astype(BF16)


def widen(compact, chosen):
    return dot(jnp.concatenate([p.astype(F32) for p in split(compact, 3)], axis=1).astype(BF16), chosen)


def convolve(padded, taps, bias, same):
    width = len(same)
    total = bias + taps[width : width + 1] * padded
    for back in range(1, width + 1):
        moved = pltpu.roll(padded, back, 0)
        total = total + taps[width - back : width - back + 1] * jnp.where(same[back - 1], moved, 0.0)
    return silu(total[RIM:]).astype(BF16)


def same_docs(lengths, first, rows, width):
    position = lax.broadcasted_iota(jnp.int32, (rows + RIM, 128), 0) + (first - RIM)
    doc = doc_of(lengths, position)
    return doc, [pltpu.roll(doc, back, 0) == doc for back in range(1, width + 1)]


def pick(first, a, b):
    return jnp.where(first, a, b)


def states_kernel(keep, dims, lengths, own_hbm, other_hbm, rim_own, rim_other, raw_own, raw_other,
                  step_bias, rate_log, taps, bias, out, out_pass, own, other, own_b, other_b, weighted, sems):
    heads, width, inner, tok = dims
    index = lax.axis_index("seq")
    core, row = index % 2, (index // 2) % 2
    columns = inner // GROUPS
    wanted = row if keep else 1 - row
    group = PAIR * core + wanted
    at = pl.multiple_of(group * columns, columns)
    at_b = pl.multiple_of(inner + core * 128, 128)
    copies = [
        pltpu.make_async_copy(own_hbm.at[:, pl.ds(at, columns)], own, sems.at[0]),
        pltpu.make_async_copy(other_hbm.at[:, pl.ds(at, columns)], other, sems.at[1]),
        pltpu.make_async_copy(own_hbm.at[:, pl.ds(at_b, 128)], own_b, sems.at[2]),
        pltpu.make_async_copy(other_hbm.at[:, pl.ds(at_b, 128)], other_b, sems.at[3]),
    ]
    for copy in copies:
        copy.start()
    is_first = core == 0
    chip_first = (index - core) * tok
    lens = [lengths[i] for i in range(lengths.shape[0])]
    lens = _Lengths(lens)
    doc, same = same_docs(lens, chip_first, 2 * tok, taps.shape[0] - 1)
    prior = doc_of(lens, chip_first - 1)
    end_a = doc_of(lens, chip_first + tok - 1)
    end_b = doc_of(lens, chip_first + 2 * tok - 1)
    raw_a = pick(is_first, raw_own[...].astype(F32), raw_other[...].astype(F32))
    raw_b = pick(is_first, raw_other[...].astype(F32), raw_own[...].astype(F32))
    scales, ends = [], []
    for part, (raw, end) in enumerate(((raw_a, end_a), (raw_b, end_b))):
        step, sums = log_sums(raw, step_bias[...], rate_log[...])
        last = sums[tok - 1 :]
        here = doc[RIM + part * tok : RIM + (part + 1) * tok, :heads] == end
        scales.append(jnp.where(here, jnp.exp(last - sums) * step, 0.0))
        ends.append(jnp.exp(last))
    pass_a = jnp.where(end_a == prior, ends[0], 0.0)
    pass_b = jnp.where(end_b == end_a, ends[1], 0.0)
    rest = jnp.concatenate([pass_b, pass_a * pass_b, jnp.zeros((6, heads), F32)], axis=0)
    scale = widen(jnp.concatenate(scales + [rest], axis=0), selector(heads, columns, width, group * (heads // GROUPS)))
    for copy in copies:
        copy.wait()
    rim_at = pl.ds(at, columns)

    def padded(o, p, rim_columns, lanes):
        a, b = o[:, lanes].astype(F32), p[:, lanes].astype(F32)
        rim = pick(is_first, rim_own[:, rim_columns].astype(F32), rim_other[:, rim_columns].astype(F32))
        return jnp.concatenate([rim, pick(is_first, a, b), pick(is_first, b, a)], axis=0)

    everything = slice(0, 128)
    b_pair = convolve(padded(own_b, other_b, pl.ds(at_b, 128), everything), taps[:, pl.ds(at_b, 128)], bias[:, pl.ds(at_b, 128)], same)
    b_pair = b_pair.astype(F32)
    half = b_pair.shape[1] // 2
    b_rows = pick(wanted == 0, b_pair[:, :half], b_pair[:, half:]).astype(BF16)
    for j in range(columns // 128):
        lanes = slice(j * 128, (j + 1) * 128)
        lanes_at = pl.ds(pl.multiple_of(at + j * 128, 128), 128)
        x = convolve(padded(own, other, lanes_at, lanes), taps[:, lanes_at], bias[:, lanes_at], same)
        weighted[:, lanes] = (x.astype(F32) * scale[: 2 * tok, lanes]).astype(BF16)
    state_a = dot(b_rows[:tok], weighted[:tok], ((0,), (0,)))
    state_b = dot(b_rows[tok:], weighted[tok:], ((0,), (0,)))
    passes = scale[2 * tok + 1 : 2 * tok + 2]
    total = scale[2 * tok : 2 * tok + 1] * state_a + state_b
    out[...] = total.astype(out.dtype)
    if keep:
        out_pass[...] = jnp.broadcast_to(passes, out_pass.shape).astype(out_pass.dtype)
    else:
        out_pass[...] = two_rows(passes, out_pass.shape)


class _Lengths:
    def __init__(self, values):
        self.values, self.shape = values, (len(values),)

    def __getitem__(self, i):
        return self.values[i]


def two_rows(passes, shape):
    top = passes.astype(BF16).astype(F32)
    which = lax.broadcasted_iota(jnp.int32, shape, 0)
    both = jnp.where(which == 0, top, jnp.where(which == 1, passes - top, 0.0))
    return both.astype(BF16)


def one_row(rows):
    wide = rows[...].astype(F32)
    return wide[0:1] + wide[1:2]


def plane_kernel(own, own_pass, got, got_pass, out, out_pass):
    upper = (lax.axis_index("seq") // 2) % 2 == 1
    mine, theirs = own[...], got[...].astype(F32)
    my_pass, their_pass = own_pass[0:1], one_row(got_pass)
    later_pass = pick(upper, my_pass, their_pass)
    total = later_pass * pick(upper, theirs, mine) + pick(upper, mine, theirs)
    out[...] = total.astype(BF16)
    out_pass[...] = two_rows(my_pass * their_pass, out_pass.shape)


def arrive_kernel(reach, own, own_pass, got, got_pass, *rest):
    parts, (out_own, out_sent) = rest[:-2], rest[-2:]
    index = lax.axis_index("seq")
    plane = index // GROUPS
    upper = (index // 2) % 2 == 1
    state = None
    for back in range(reach, 0, -1):
        even, even_pass, odd, odd_pass = parts[4 * (back - 1) : 4 * back]
        source = plane - back
        is_even = (source + 2 * back) // back % 2 == 0
        there = source >= 0
        arrived = pick(is_even, even[...].astype(F32), odd[...].astype(F32))
        arrived = jnp.where(there, arrived, 0.0)
        if state is None:
            state = arrived
        else:
            passes = pick(is_even, one_row(even_pass), one_row(odd_pass))
            state = arrived + jnp.where(there, passes, 0.0) * state
    first_state = pick(upper, got[...].astype(F32), own[...])
    first_pass = pick(upper, one_row(got_pass), own_pass[0:1])
    later = first_pass * state + first_state
    out_own[...] = pick(upper, later, state).astype(BF16)
    out_sent[...] = pick(upper, state, later).astype(BF16)


def local_kernel(dims, lengths, x_ref, bc_ref, before, before_bc, rim, rim_bc, gate, raw, step_bias, rate_log, taps, bias,
                 taps_bc, bias_bc, skip, a_out, b_out, c_out, s_out, p_out, b_all, compact):
    heads, width, state, tok = dims
    g = pl.program_id(0)
    index = lax.axis_index("seq")
    core = index % 2
    is_first = core == 0
    first = index * tok
    lens = _Lengths([lengths[i] for i in range(lengths.shape[0])])
    doc, same = same_docs(lens, first, tok, taps.shape[0] - 1)
    prior = doc_of(lens, first - 1)
    final = doc_of(lens, first + tok - 1)

    def padded(ref, rim_ref, before_ref, lanes):
        top = pick(is_first, rim_ref[:, lanes].astype(F32), before_ref[:, lanes].astype(F32))
        return jnp.concatenate([top, ref[:, lanes].astype(F32)], axis=0)

    @pl.when(g == 0)
    def _():
        for j in range(bc_ref.shape[1] // 128):
            lanes = slice(j * 128, (j + 1) * 128)
            mixed = convolve(padded(bc_ref, rim_bc, before_bc, lanes), taps_bc[:, lanes], bias_bc[:, lanes], same)
            for k in range(128 // state):
                which = j * (128 // state) + k
                value = mixed.astype(F32)[:, k * state : (k + 1) * state].astype(BF16)
                if which < GROUPS:
                    b_all[which] = value
                else:
                    c_out[which - GROUPS] = value
        step, sums = log_sums(raw[...], step_bias[...], rate_log[...])
        last = sums[tok - 1 :]
        rest = jnp.concatenate(
            [jnp.exp(last), jnp.where(final == prior, jnp.exp(last), 0.0), skip[...], jnp.zeros((5, heads), F32)], axis=0)
        whole = jnp.concatenate([jnp.exp(sums), jnp.exp(-sums) * step, rest], axis=0)
        compact[...] = jnp.concatenate([p.astype(F32) for p in split(whole, 3)], axis=1).astype(BF16)

    columns = x_ref.shape[1]
    wide = dot(compact[...], selector(heads, columns, width, g * (heads // GROUPS)))
    inward, outward = wide[:tok], wide[tok : 2 * tok]
    end_decay, passes, gains = (wide[2 * tok + k : 2 * tok + k + 1] for k in range(3))
    b_rows, c_rows = b_all[g], c_out[g]
    scores = dot(c_rows, b_rows, ((1,), (1,)))
    down, across = (lax.broadcasted_iota(jnp.int32, (tok, tok), k) for k in range(2))
    causal = (down >= across) & (doc[RIM:, :tok] == doc_of(lens, across + first))
    mask = jnp.where(causal, scores, 0.0)
    m_top, m_rest = split(mask, 2)
    here = doc[RIM:, :state] == final
    ending = jnp.where(here, b_rows.astype(F32), 0.0).astype(BF16)
    lhs = jnp.concatenate([m_top.astype(F32), m_rest.astype(F32)], axis=1).astype(BF16)
    entered = doc[RIM:] == prior
    for j in range(columns // 128):
        lanes = slice(j * 128, (j + 1) * 128)
        x = convolve(padded(x_ref, rim, before, lanes), taps[:, lanes], bias[:, lanes], same).astype(F32)
        scaled = x * outward[:, lanes]
        s_top, s_rest = split(scaled, 2)
        within = dot(lhs, jnp.concatenate([s_top, s_top], axis=0)) + dot(m_top, s_rest)
        local = dot(ending, s_top, ((0,), (0,))) + dot(ending, s_rest, ((0,), (0,)))
        opened = silu(gate[:, lanes].astype(F32))
        a_out[:, lanes] = (inward[:, lanes] * within + gains[:, lanes] * x) * opened
        b_out[:, lanes] = jnp.where(entered, inward[:, lanes] * opened, 0.0)
        s_out[:, lanes] = (end_decay[:, lanes] * local).astype(BF16)
    p_out[...] = two_rows(passes, p_out.shape)


def finish_kernel(width, a_ref, b_ref, c_ref, prior_state, prior_pass, x0, x1, x2, x3, gain, out):
    index = lax.axis_index("seq")
    core, row = index % 2, (index // 2) % 2
    second = core == 1
    columns = x0.shape[1]
    block = 256
    shape = (2 * block, block)
    r, c = lax.broadcasted_iota(jnp.int32, shape, 0) % block // width, lax.broadcasted_iota(jnp.int32, shape, 1) // width
    means = jnp.where(r == c, 1.0 / width, 0.0).astype(BF16)
    order = ((x0, core, row), (x1, core, 1 - row), (x2, 1 - core, row), (x3, 1 - core, 1 - row))
    for arrived, half, other in order:
        group = PAIR * half + other
        c_rows = c_ref[group]
        for j in range(columns // block):
            lanes = slice(j * block, (j + 1) * block)
            at = pl.ds(pl.multiple_of(group * columns + j * block, block), block)
            state = arrived[:, lanes].astype(F32)
            passes = prior_pass[:, at].astype(F32)
            stepped = (passes[0:1] + passes[1:2]) * state + prior_state[:, at].astype(F32)
            state = pick(second, stepped, state).astype(BF16)
            gated = a_ref[:, at] + b_ref[:, at] * dot(c_rows, state)
            top, rest = split(gated * gated, 2)
            mean = dot(jnp.concatenate([top, rest], axis=1), means)
            out[:, at] = (gated * lax.rsqrt(mean + EPSILON) * gain[:, at]).astype(BF16)


def swap(block, pairs):
    return lax.ppermute(block, "seq", [*pairs, *((b, a) for a, b in pairs)])


def on_device(mixer_in, gate_in, step_raw, step_bias, rate_log, conv_weight, conv_bias, skip_gain, norm_gain, doc_lengths):
    tok, channels = mixer_in.shape
    heads, inner = rate_log.shape[0], gate_in.shape[1]
    width = inner // heads
    state = (channels - inner) // (2 * GROUPS)
    devices = lax.axis_size("seq")
    planes = devices // GROUPS
    columns = inner // GROUPS
    taps_n = conv_weight.shape[0]
    longest = devices * tok // 2
    reach = -(-(longest - 1) // (GROUPS * tok))
    row = lambda a: a.reshape(1, -1)
    step_bias, rate_log, skip_gain, norm_gain, conv_bias = map(row, (step_bias, rate_log, skip_gain, norm_gain, conv_bias))
    cores = [(i, i + 1) for i in range(0, devices, 2)]
    rows = [(i, i + 2) for i in range(0, devices, 4) for i in (i, i + 1)]
    chips = [(i, i + 1) for i in range(1, devices - 1, 2)]

    other = swap(mixer_in, cores)
    other_raw = swap(step_raw, cores)
    rim = swap(mixer_in[tok - RIM :], chips)
    other_rim = swap(rim, cores)

    params = pltpu.CompilerParams(vmem_limit_bytes=48 << 20)

    def states(keep):
        kind = F32 if keep else BF16
        return pl.pallas_call(
            functools.partial(states_kernel, keep, (heads, width, inner, tok)),
            out_shape=(jax.ShapeDtypeStruct((state, columns), kind), jax.ShapeDtypeStruct((8, columns), kind)),
            in_specs=[SMEM, ANY, ANY] + [VMEM] * 8,
            out_specs=(VMEM, VMEM),
            scratch_shapes=[pltpu.VMEM((tok, columns), BF16)] * 2 + [pltpu.VMEM((tok, 128), BF16)] * 2
            + [pltpu.VMEM((2 * tok, columns), BF16), pltpu.SemaphoreType.DMA((4,))],
            compiler_params=params,
            name="states_kept" if keep else "states_sent",
        )(doc_lengths, mixer_in, other, rim, other_rim, step_raw, other_raw, step_bias, rate_log, conv_weight, conv_bias)

    sent, sent_pass = states(False)
    got = swap(sent, rows)
    got_pass = swap(sent_pass, rows)
    kept, kept_pass = states(True)
    piece = jax.ShapeDtypeStruct((state, columns), BF16)
    piece_pass = jax.ShapeDtypeStruct((8, columns), BF16)
    plane, plane_pass = pl.pallas_call(
        plane_kernel, out_shape=(piece, piece_pass), in_specs=[VMEM] * 4, out_specs=(VMEM, VMEM), name="plane_total",
    )(kept, kept_pass, got, got_pass)
    parts = []
    for back in range(1, reach + 1):
        for parity in range(2):
            pairs = [
                (GROUPS * p + q, GROUPS * (p + back) + q)
                for p in range(planes - back) if p // back % 2 == parity
                for q in range(GROUPS)
            ]
            if pairs:
                parts += [swap(plane, pairs), swap(plane_pass, pairs)]
            else:
                parts += parts[-2:]

    def whole(height, length):
        return pl.BlockSpec((height, length), lambda g: (0, 0))

    def by_group(height):
        return pl.BlockSpec((height, columns), lambda g: (0, g))

    rest = channels - inner
    bc = pl.BlockSpec((tok, rest), lambda g: (0, inner // rest))
    last = pl.BlockSpec((RIM, columns), lambda g: (tok // RIM - 1, g))
    last_bc = pl.BlockSpec((RIM, rest), lambda g: (tok // RIM - 1, inner // rest))
    a, b, c, own_state, own_pass = pl.pallas_call(
        functools.partial(local_kernel, (heads, width, state, tok)),
        grid=(GROUPS,),
        out_shape=(
            jax.ShapeDtypeStruct((tok, inner), F32),
            jax.ShapeDtypeStruct((tok, inner), F32),
            jax.ShapeDtypeStruct((GROUPS, tok, state), BF16),
            jax.ShapeDtypeStruct((state, inner), BF16),
            jax.ShapeDtypeStruct((8, inner), BF16),
        ),
        in_specs=[
            SMEM, by_group(tok), bc, last, last_bc, by_group(RIM), pl.BlockSpec((RIM, rest), lambda g: (0, inner // rest)),
            by_group(tok), whole(tok, heads), whole(1, heads), whole(1, heads), by_group(taps_n), by_group(1),
            pl.BlockSpec((taps_n, rest), lambda g: (0, inner // rest)), pl.BlockSpec((1, rest), lambda g: (0, inner // rest)),
            whole(1, heads),
        ],
        out_specs=(by_group(tok), by_group(tok), pl.BlockSpec((GROUPS, tok, state), lambda g: (0, 0, 0)), by_group(state), by_group(8)),
        scratch_shapes=[pltpu.VMEM((GROUPS, tok, state), BF16), pltpu.VMEM((2 * tok + 8, 3 * heads), BF16)],
        compiler_params=params,
        name="local_block",
        cost_estimate=pl.CostEstimate(flops=2 * 10**9, bytes_accessed=8 << 20, transcendentals=10**6),
    )(doc_lengths, mixer_in, mixer_in, other, other, rim, rim, gate_in, step_raw, step_bias, rate_log, conv_weight, conv_bias,
      conv_weight, conv_bias, skip_gain)
    prior_state, prior_pass = swap(own_state, cores), swap(own_pass, cores)

    x0, mine = pl.pallas_call(
        functools.partial(arrive_kernel, reach), out_shape=(piece, piece), in_specs=[VMEM] * (4 + 4 * reach), out_specs=(VMEM, VMEM),
        name="arrive",
    )(kept, kept_pass, got, got_pass, *parts)
    x1 = swap(mine, rows)
    x2 = swap(x0, cores)
    x3 = swap(x1, cores)
    return pl.pallas_call(
        functools.partial(finish_kernel, width),
        out_shape=jax.ShapeDtypeStruct((tok, inner), BF16),
        in_specs=[VMEM] * 10,
        out_specs=VMEM,
        compiler_params=params,
        name="finish",
    )(a, b, c, prior_state, prior_pass, x0, x1, x2, x3, norm_gain)


def solution(mesh):
    split_rows = P(("groups", "seq"), None)
    return jax.shard_map(
        on_device,
        mesh=mesh,
        in_specs=(split_rows, split_rows, split_rows, P(), P(), P(), P(), P(), P(), P("groups")),
        out_specs=split_rows,
        check_vma=False,
    )
```

time: 143 us -> 62.1 us (0.43); the launches traced: 141 us -> 61.8 us
  other arithmetic: 42.4 us -> 0 us
  local copies, waits for them, and re-layouts: 35.6 us -> 6.72 us
  Pallas kernels: 0 us -> 14.8 us
  matrix products: 12.4 us -> 0 us
  waiting for transfers between devices: 26 us -> 14.2 us
  starting transfers between devices: 22.6 us -> 25.9 us
  between operations: 2.27 us -> 0.21 us
    all_to_all x3 -> x0, waiting for transfers between devices: 26 us -> none  [the longest x1 19 us: on_device(): lax.all_to_all(row_states, 'seq', split_axis=1, concat_axis=0, tiled=True)]
    ppermute x1 -> x17, starting transfers between devices: 2.4 us -> 25.9 us  [swap(): return lax.ppermute(block, 'seq', [*pairs, *((b, a) for a, b in pairs)])]
    all_to_all x3 -> x0, starting transfers between devices: 20.2 us -> none  [the longest x1 7.21 us: on_device(): lax.all_to_all(row_pass, 'seq', split_axis=1, concat_axis=0, tiled=True)]
    unnamed x1 -> x0, other arithmetic: 19.3 us -> none
    pallas_call x0 -> x6, Pallas kernels: none -> 14.8 us  [the longest x1 4.33 us: on_device(): pl.pallas_call(functools.partial(local_kernel, (heads, width, state, tok)...]
    ppermute x1 -> x17, waiting for transfers between devices: 0.01 us -> 14.2 us  [swap(): return lax.ppermute(block, 'seq', [*pairs, *((b, a) for a, b in pairs)])]
    dot_general x16 -> x0, matrix products: 12.4 us -> none  [the longest x4 6.04 us: group_terms(): jnp.einsum('tn,sn->ts', c_group, b_group, preferred_element_type=jnp.floa...]
    unnamed x114 -> x40, local copies, waits for them, and re-layouts: 14.4 us -> 5.82 us
  transfers between devices with their start and end apart: 4 -> 17, of which waited for: 2 -> 5; matrix products, arithmetic and copies ran while one was open for 33% -> 1% of each run, Pallas kernels for 0% -> 17%
where the time goes in v1:
time: 62.1 us; the launch traced here: 61.8 us
  starting transfers between devices  25.9 us (42%)
  Pallas kernels  14.8 us (24%)
  waiting for transfers between devices  14.2 us (23%)
  local copies, waits for them, and re-layouts  6.72 us (11%)
    ppermute x17, starting transfers between devices, swap(): return lax.ppermute(block, 'seq', [*pairs, *((b, a) for a, b in pairs)])  25.9 us
    ppermute x17, waiting for transfers between devices, swap(): return lax.ppermute(block, 'seq', [*pairs, *((b, a) for a, b in pairs)])  14.2 us
    unnamed x40, local copies, waits for them, and re-layouts  5.82 us
    pallas_call x1, Pallas kernels, on_device(): pl.pallas_call(functools.partial(local_kernel, (heads, width, state, tok)...  4.33 us
    pallas_call x2, Pallas kernels, states(): pl.pallas_call(functools.partial(states_kernel, keep, (heads, width, inne...  3.93 us
    pallas_call x1, Pallas kernels, on_device(): pl.pallas_call(functools.partial(finish_kernel, width), out_shape=jax.Sha...  2.63 us
    pallas_call x1, Pallas kernels, on_device(): pl.pallas_call(functools.partial(arrive_kernel, reach), out_shape=(piece,...  2.17 us
    pallas_call x1, Pallas kernels, on_device(): pl.pallas_call(plane_kernel, out_shape=(piece, piece_pass), in_specs=[VME...  1.74 us
  transfers between devices with their start and end apart: 17, of which 5 were waited for; matrix products, arithmetic and copies ran while one was open for 1% of the time, Pallas kernels for 17%

profile of v1, /device:TPU:0, one launch (start us, length us, event | category | flops | bytes accessed | tf_op | source)
XLA Modules:
  0.0 61.8 jit_solution(18284813014862297017)
XLA Ops:
  0.6 0.9 %slice.3 = bf16[8,4608]{1,0:T(8,128)(2,1)S(1)} slice(bf16[64,4608]{1,0:T(8,128)(2,1)} %own_hbm.3), slice={[56:64], [0:4608]} | slice | bytes 147456 | tf_op jit(solution)/shard_map/slice | solution.py:326
  1.5 0.7 %collective-permute-start.1 = (bf16[8,4608]{1,0:T(8,128)(2,1)S(1)}, bf16[8,4608]{1,0:T(8,128)(2,1)S(1)}, u32[]{:S(2)}, u32[]{:S(2)}) collective-permute-start(bf16[8,4608]{1,0:T(8,128)(2,1)S(1)} %slice.3), channel_id=1, source_target_pairs={{1,2},{3,4},{5,6},{7,8},{9,10},{11,12},{13,14},{2,1},{4,3},{6,5},{... | collective-permute-start | bytes 221192 | tf_op jit(solution)/shard_map/ppermute | solution.py:304
  2.1 5.9 %collective-permute-start.4 = (bf16[8,4608]{1,0:T(8,128)(2,1)S(1)}, bf16[8,4608]{1,0:T(8,128)(2,1)S(1)}, u32[]{:S(2)}, u32[]{:S(2)}) collective-permute-start(bf16[8,4608]{1,0:T(8,128)(2,1)S(1)} %collective-permute-done.1.rim.rim_bc.rim_own), channel_id=1, source_target_pairs={{0,1},{2,3},{4,5},{6,7},{8,9},{10,11},{12,13},{14,15},{1,0},{3,2},... | collective-permute-start | bytes 221192 | tf_op jit(solution)/shard_map/ppermute | solution.py:304
  8.1 1.2 %collective-permute-done.5.raw_other = bf16[64,64]{1,0:T(8,128)(2,1)S(1)} collective-permute-done((bf16[64,64]{1,0:T(8,128)(2,1)S(1)}, bf16[64,64]{1,0:T(8,128)(2,1)S(1)}, u32[]{:S(2)}, u32[]{:S(2)}) %collective-permute-start.5) | collective-permute-done | bytes 8224 | tf_op jit(solution)/shard_map/ppermute | solution.py:304
  9.9 1.1 %copy-done = bf16[64,4608]{1,0:T(8,128)(2,1)S(1)} copy-done((bf16[64,4608]{1,0:T(8,128)(2,1)S(1)}, bf16[64,4608]{1,0:T(8,128)(2,1)}, u32[]{:S(2)}) %copy-start) | copy-done | bytes 589848
  11.0 2.0 %states_sent.1 = (bf16[64,1024]{1,0:T(8,128)(2,1)S(1)}, bf16[8,1024]{1,0:T(8,128)(2,1)S(1)}) custom-call(s32[6]{0:T(128)S(1)} %copy-done.7, bf16[64,4608]{1,0:T(8,128)(2,1)S(1)} %copy-done, bf16[64,4608]{1,0:T(8,128)(2,1)S(1)} %collective-permute-done.before.before_bc.other_hbm, bf16[8,4608]{1,0:T(8,128)(2,1)S(1)} %collective-permute-done.1.rim.rim_bc.rim_own, ...), custom_call_target="tpu_custom_call" | custom-call | tf_op jit(solution)/shard_map/states_sent/pallas_call | solution.py:333
  13.0 3.1 %collective-permute-start.6 = (bf16[64,1024]{1,0:T(8,128)(2,1)S(1)}, bf16[64,1024]{1,0:T(8,128)(2,1)S(1)}, u32[]{:S(2)}, u32[]{:S(2)}) collective-permute-start(bf16[64,1024]{1,0:T(8,128)(2,1)S(1)} %get-tuple-element.25), channel_id=1, source_target_pairs={{0,2},{1,3},{4,6},{5,7},{8,10},{9,11},{12,14},{13,15},{2,0},{3,1},... | collective-permute-start | bytes 393224 | tf_op jit(solution)/shard_map/ppermute | solution.py:304
  16.0 4.3 %local_block.1 = (f32[64,4096]{1,0:T(8,128)S(1)}, f32[64,4096]{1,0:T(8,128)S(1)}, bf16[4,64,64]{2,1,0:T(8,128)(2,1)S(1)}, bf16[64,4096]{1,0:T(8,128)(2,1)S(1)}, bf16[8,4096]{1,0:T(8,128)(2,1)S(1)}) custom-call(s32[6]{0:T(128)S(1)} %copy-done.7, bf16[64,4608]{1,0:T(8,128)(2,1)S(1)} %copy-done, bf16[64,4608]{1,0:T(8,128)(2,1)S(1)} %copy-done, ...), custom_call_target="tpu_custom_call" | custom-call | flops 2000000000 | bytes 8388608 | tf_op jit(solution)/shard_map/local_block/pallas_call | solution.py:376
  20.5 0.7 %collective-permute-start.7 = (bf16[8,1024]{1,0:T(8,128)(2,1)S(1)}, bf16[8,1024]{1,0:T(8,128)(2,1)S(1)}, u32[]{:S(2)}, u32[]{:S(2)}) collective-permute-start(bf16[8,1024]{1,0:T(8,128)(2,1)S(1)} %get-tuple-element.26), channel_id=1, source_target_pairs={{0,2},{1,3},{4,6},{5,7},{8,10},{9,11},{12,14},{13,15},{2,0},{3,1},... | collective-permute-start | bytes 49160 | tf_op jit(solution)/shard_map/ppermute | solution.py:304
  21.2 2.0 %states_kept.1 = (f32[64,1024]{1,0:T(8,128)S(1)}, f32[8,1024]{1,0:T(8,128)S(1)}) custom-call(s32[6]{0:T(128)S(1)} %copy-done.7, bf16[64,4608]{1,0:T(8,128)(2,1)S(1)} %copy-done, bf16[64,4608]{1,0:T(8,128)(2,1)S(1)} %collective-permute-done.before.before_bc.other_hbm, bf16[8,4608]{1,0:T(8,128)(2,1)S(1)} %collective-permute-done.1.rim.rim_bc.rim_own, ...), custom_call_target="tpu_custom_call" | custom-call | tf_op jit(solution)/shard_map/states_kept/pallas_call | solution.py:333
  23.1 0.7 %copy-done.1 = f32[64,1024]{1,0:T(8,128)} copy-done((f32[64,1024]{1,0:T(8,128)}, f32[64,1024]{1,0:T(8,128)S(1)}, u32[]{:S(2)}) %copy-start.1) | copy-done | bytes 262168
  25.1 1.7 %plane_total.1 = (bf16[64,1024]{1,0:T(8,128)(2,1)}, bf16[8,1024]{1,0:T(8,128)(2,1)}) custom-call(f32[64,1024]{1,0:T(8,128)} %copy-done.1, f32[8,1024]{1,0:T(8,128)} %copy-done.3, bf16[64,1024]{1,0:T(8,128)(2,1)} %copy-done.12, bf16[8,1024]{1,0:T(8,128)(2,1)} %copy-done.16), custom_call_target="tpu_custom_call" | custom-call | tf_op jit(solution)/shard_map/plane_total/pallas_call | solution.py:350
  26.9 2.6 %collective-permute-start.12 = (bf16[64,1024]{1,0:T(8,128)(2,1)}, bf16[64,1024]{1,0:T(8,128)(2,1)S(1)}, u32[]{:S(2)}, u32[]{:S(2)}) collective-permute-start(bf16[64,1024]{1,0:T(8,128)(2,1)} %get-tuple-element.27), channel_id=1, source_target_pairs={{0,8},{1,9},{2,10},{3,11},{4,12},{5,13},{6,14},{7,15},{8,0},{9,1},... | collective-permute-start | bytes 393224 | tf_op jit(solution)/shard_map/ppermute | solution.py:304
  29.5 0.7 %collective-permute-start.10 = (bf16[64,1024]{1,0:T(8,128)(2,1)}, bf16[64,1024]{1,0:T(8,128)(2,1)S(1)}, u32[]{:S(2)}, u32[]{:S(2)}) collective-permute-start(bf16[64,1024]{1,0:T(8,128)(2,1)} %get-tuple-element.27), channel_id=1, source_target_pairs={{4,8},{5,9},{6,10},{7,11},{8,4},{9,5},{10,6},{11,7},{20,24},{21,25... | collective-permute-start | bytes 393224 | tf_op jit(solution)/shard_map/ppermute | solution.py:304
  30.1 2.6 %collective-permute-start.8 = (bf16[64,1024]{1,0:T(8,128)(2,1)}, bf16[64,1024]{1,0:T(8,128)(2,1)}, u32[]{:S(2)}, u32[]{:S(2)}) collective-permute-start(bf16[64,1024]{1,0:T(8,128)(2,1)} %get-tuple-element.27), channel_id=1, source_target_pairs={{0,4},{1,5},{2,6},{3,7},{8,12},{9,13},{10,14},{11,15},{4,0},{5,1},... | collective-permute-start | bytes 393224 | tf_op jit(solution)/shard_map/ppermute | solution.py:304
  32.7 1.5 %collective-permute-start.13 = (bf16[8,1024]{1,0:T(8,128)(2,1)}, bf16[8,1024]{1,0:T(8,128)(2,1)S(1)}, u32[]{:S(2)}, u32[]{:S(2)}) collective-permute-start(bf16[8,1024]{1,0:T(8,128)(2,1)} %get-tuple-element.28), channel_id=1, source_target_pairs={{0,8},{1,9},{2,10},{3,11},{4,12},{5,13},{6,14},{7,15},{8,0},{9,1},... | collective-permute-start | bytes 49160 | tf_op jit(solution)/shard_map/ppermute | solution.py:304
  34.3 5.5 %collective-permute-done.13.rest_5_.rest_7_ = bf16[8,1024]{1,0:T(8,128)(2,1)S(1)} collective-permute-done((bf16[8,1024]{1,0:T(8,128)(2,1)}, bf16[8,1024]{1,0:T(8,128)(2,1)S(1)}, u32[]{:S(2)}, u32[]{:S(2)}) %collective-permute-start.13) | collective-permute-done | bytes 16416 | tf_op jit(solution)/shard_map/ppermute | solution.py:304
  40.4 5.8 %collective-permute-start.9 = (bf16[8,1024]{1,0:T(8,128)(2,1)}, bf16[8,1024]{1,0:T(8,128)(2,1)S(1)}, u32[]{:S(2)}, u32[]{:S(2)}) collective-permute-start(bf16[8,1024]{1,0:T(8,128)(2,1)} %get-tuple-element.28), channel_id=1, source_target_pairs={{0,4},{1,5},{2,6},{3,7},{8,12},{9,13},{10,14},{11,15},{4,0},{5,1},... | collective-permute-start | bytes 49160 | tf_op jit(solution)/shard_map/ppermute | solution.py:304
  46.3 1.9 %collective-permute-done.9.rest_1_ = bf16[8,1024]{1,0:T(8,128)(2,1)S(1)} collective-permute-done((bf16[8,1024]{1,0:T(8,128)(2,1)}, bf16[8,1024]{1,0:T(8,128)(2,1)S(1)}, u32[]{:S(2)}, u32[]{:S(2)}) %collective-permute-start.9) | collective-permute-done | bytes 16416 | tf_op jit(solution)/shard_map/ppermute | solution.py:304
  49.4 2.2 %arrive.1 = (bf16[64,1024]{1,0:T(8,128)(2,1)}, bf16[64,1024]{1,0:T(8,128)(2,1)}) custom-call(f32[64,1024]{1,0:T(8,128)} %copy-done.1, f32[8,1024]{1,0:T(8,128)} %copy-done.3, bf16[64,1024]{1,0:T(8,128)(2,1)} %copy-done.12, bf16[8,1024]{1,0:T(8,128)(2,1)} %copy-done.16, bf16[64,1024]{1,0:T(8,128)(2,1)} %collective-permute-done.8.rest_0_, ...), custom_call_target="tpu_custom_call" | custom-call | tf_op jit(solution)/shard_map/arrive/pallas_call | solution.py:401
  52.1 4.6 %collective-permute-done.14.x1 = bf16[64,1024]{1,0:T(8,128)(2,1)S(1)} collective-permute-done((bf16[64,1024]{1,0:T(8,128)(2,1)}, bf16[64,1024]{1,0:T(8,128)(2,1)S(1)}, u32[]{:S(2)}, u32[]{:S(2)}) %collective-permute-start.14) | collective-permute-done | bytes 131104 | tf_op jit(solution)/shard_map/ppermute | solution.py:304
  57.3 0.9 %collective-permute-done.3.prior_pass = bf16[8,4096]{1,0:T(8,128)(2,1)S(1)} collective-permute-done((bf16[8,4096]{1,0:T(8,128)(2,1)S(1)}, bf16[8,4096]{1,0:T(8,128)(2,1)S(1)}, u32[]{:S(2)}, u32[]{:S(2)}) %collective-permute-start.3) | collective-permute-done | bytes 65568 | tf_op jit(solution)/shard_map/ppermute | solution.py:304
  58.3 0.9 %copy-done.4 = bf16[64,1024]{1,0:T(8,128)(2,1)S(1)} copy-done((bf16[64,1024]{1,0:T(8,128)(2,1)S(1)}, bf16[64,1024]{1,0:T(8,128)(2,1)}, u32[]{:S(2)}) %copy-start.4) | copy-done | bytes 131096
  59.2 2.6 %finish.1 = bf16[64,4096]{1,0:T(8,128)(2,1)} custom-call(f32[64,4096]{1,0:T(8,128)S(1)} %get-tuple-element.18.a_ref, f32[64,4096]{1,0:T(8,128)S(1)} %get-tuple-element.19.b_ref, bf16[4,64,64]{2,1,0:T(8,128)(2,1)S(1)} %get-tuple-element.20.c_ref, bf16[64,4096]{1,0:T(8,128)(2,1)S(1)} %collective-permute-done.2.prior_state, ...), custom_call_target="tpu_custom_call" | custom-call | tf_op jit(solution)/shard_map/finish/pallas_call | solution.py:408
  (58 shorter events, 5.5 us)
Async XLA Ops:
  0.0 8.0 %copy-start.5 = (bf16[64,64]{1,0:T(8,128)(2,1)S(1)}, bf16[64,64]{1,0:T(8,128)(2,1)}, u32[]{:S(2)}) copy-start(bf16[64,64]{1,0:T(8,128)(2,1)} %raw_own.3) | copy-start | bytes 24580
  0.0 8.0 %copy-start.17 = (f32[4608]{0:T(1024)S(1)}, f32[4608]{0:T(1024)}, u32[]{:S(2)}) copy-start(f32[4608]{0:T(1024)} %param.16) | copy-start | bytes 55300
  0.0 9.2 %copy-start.2 = (f32[4,4608]{1,0:T(4,128)S(1)}, f32[4,4608]{1,0:T(4,128)}, u32[]{:S(2)}) copy-start(f32[4,4608]{1,0:T(4,128)} %taps.5) | copy-start | bytes 221188
  0.0 9.2 %collective-permute-start = (bf16[64,4608]{1,0:T(8,128)(2,1)}, bf16[64,4608]{1,0:T(8,128)(2,1)S(1)}, u32[]{:S(2)}, u32[]{:S(2)}) collective-permute-start(bf16[64,4608]{1,0:T(8,128)(2,1)} %own_hbm.3), channel_id=1, source_target_pairs={{0,1},{2,3},{4,5},{6,7},{8,9},{10,11},{12,13},{14,15},{1,0},{3,2},... | collective-permute-start | bytes 1769480 | tf_op jit(solution)/shard_map/ppermute | solution.py:304
  1.5 0.7 %collective-permute-start.1 = (bf16[8,4608]{1,0:T(8,128)(2,1)S(1)}, bf16[8,4608]{1,0:T(8,128)(2,1)S(1)}, u32[]{:S(2)}, u32[]{:S(2)}) collective-permute-start(bf16[8,4608]{1,0:T(8,128)(2,1)S(1)} %slice.3), channel_id=1, source_target_pairs={{1,2},{3,4},{5,6},{7,8},{9,10},{11,12},{13,14},{2,1},{4,3},{6,5},{... | collective-permute-start | bytes 221192 | tf_op jit(solution)/shard_map/ppermute | solution.py:304
  2.1 7.1 %collective-permute-start.4 = (bf16[8,4608]{1,0:T(8,128)(2,1)S(1)}, bf16[8,4608]{1,0:T(8,128)(2,1)S(1)}, u32[]{:S(2)}, u32[]{:S(2)}) collective-permute-start(bf16[8,4608]{1,0:T(8,128)(2,1)S(1)} %collective-permute-done.1.rim.rim_bc.rim_own), channel_id=1, source_target_pairs={{0,1},{2,3},{4,5},{6,7},{8,9},{10,11},{12,13},{14,15},{1,0},{3,2},... | collective-permute-start | bytes 221192 | tf_op jit(solution)/shard_map/ppermute | solution.py:304
  8.0 1.2 %collective-permute-start.5 = (bf16[64,64]{1,0:T(8,128)(2,1)S(1)}, bf16[64,64]{1,0:T(8,128)(2,1)S(1)}, u32[]{:S(2)}, u32[]{:S(2)}) collective-permute-start(bf16[64,64]{1,0:T(8,128)(2,1)S(1)} %copy-done.5), channel_id=1, source_target_pairs={{0,1},{2,3},{4,5},{6,7},{8,9},{10,11},{12,13},{14,15},{1,0},{3,2},... | collective-permute-start | bytes 24584 | tf_op jit(solution)/shard_map/ppermute | solution.py:304
  11.0 5.1 %copy-start.10 = (bf16[64,4096]{1,0:T(8,128)(2,1)S(1)}, bf16[64,4096]{1,0:T(8,128)(2,1)}, u32[]{:S(2)}) copy-start(bf16[64,4096]{1,0:T(8,128)(2,1)} %gate.1) | copy-start | bytes 1572868
  13.0 11.5 %collective-permute-start.6 = (bf16[64,1024]{1,0:T(8,128)(2,1)S(1)}, bf16[64,1024]{1,0:T(8,128)(2,1)S(1)}, u32[]{:S(2)}, u32[]{:S(2)}) collective-permute-start(bf16[64,1024]{1,0:T(8,128)(2,1)S(1)} %get-tuple-element.25), channel_id=1, source_target_pairs={{0,2},{1,3},{4,6},{5,7},{8,10},{9,11},{12,14},{13,15},{2,0},{3,1},... | collective-permute-start | bytes 393224 | tf_op jit(solution)/shard_map/ppermute | solution.py:304
  20.4 37.9 %collective-permute-start.2 = (bf16[64,4096]{1,0:T(8,128)(2,1)S(1)}, bf16[64,4096]{1,0:T(8,128)(2,1)S(1)}, u32[]{:S(2)}, u32[]{:S(2)}) collective-permute-start(bf16[64,4096]{1,0:T(8,128)(2,1)S(1)} %get-tuple-element.21), channel_id=1, source_target_pairs={{0,1},{2,3},{4,5},{6,7},{8,9},{10,11},{12,13},{14,15},{1,0},{3,2},... | collective-permute-start | bytes 1572872 | tf_op jit(solution)/shard_map/ppermute | solution.py:304
  20.5 4.0 %collective-permute-start.7 = (bf16[8,1024]{1,0:T(8,128)(2,1)S(1)}, bf16[8,1024]{1,0:T(8,128)(2,1)S(1)}, u32[]{:S(2)}, u32[]{:S(2)}) collective-permute-start(bf16[8,1024]{1,0:T(8,128)(2,1)S(1)} %get-tuple-element.26), channel_id=1, source_target_pairs={{0,2},{1,3},{4,6},{5,7},{8,10},{9,11},{12,14},{13,15},{2,0},{3,1},... | collective-permute-start | bytes 49160 | tf_op jit(solution)/shard_map/ppermute | solution.py:304
  26.9 21.3 %collective-permute-start.12 = (bf16[64,1024]{1,0:T(8,128)(2,1)}, bf16[64,1024]{1,0:T(8,128)(2,1)S(1)}, u32[]{:S(2)}, u32[]{:S(2)}) collective-permute-start(bf16[64,1024]{1,0:T(8,128)(2,1)} %get-tuple-element.27), channel_id=1, source_target_pairs={{0,8},{1,9},{2,10},{3,11},{4,12},{5,13},{6,14},{7,15},{8,0},{9,1},... | collective-permute-start | bytes 393224 | tf_op jit(solution)/shard_map/ppermute | solution.py:304
  29.5 18.7 %collective-permute-start.10 = (bf16[64,1024]{1,0:T(8,128)(2,1)}, bf16[64,1024]{1,0:T(8,128)(2,1)S(1)}, u32[]{:S(2)}, u32[]{:S(2)}) collective-permute-start(bf16[64,1024]{1,0:T(8,128)(2,1)} %get-tuple-element.27), channel_id=1, source_target_pairs={{4,8},{5,9},{6,10},{7,11},{8,4},{9,5},{10,6},{11,7},{20,24},{21,25... | collective-permute-start | bytes 393224 | tf_op jit(solution)/shard_map/ppermute | solution.py:304
  30.1 18.7 %collective-permute-start.8 = (bf16[64,1024]{1,0:T(8,128)(2,1)}, bf16[64,1024]{1,0:T(8,128)(2,1)}, u32[]{:S(2)}, u32[]{:S(2)}) collective-permute-start(bf16[64,1024]{1,0:T(8,128)(2,1)} %get-tuple-element.27), channel_id=1, source_target_pairs={{0,4},{1,5},{2,6},{3,7},{8,12},{9,13},{10,14},{11,15},{4,0},{5,1},... | collective-permute-start | bytes 393224 | tf_op jit(solution)/shard_map/ppermute | solution.py:304
  32.7 7.0 %collective-permute-start.13 = (bf16[8,1024]{1,0:T(8,128)(2,1)}, bf16[8,1024]{1,0:T(8,128)(2,1)S(1)}, u32[]{:S(2)}, u32[]{:S(2)}) collective-permute-start(bf16[8,1024]{1,0:T(8,128)(2,1)} %get-tuple-element.28), channel_id=1, source_target_pairs={{0,8},{1,9},{2,10},{3,11},{4,12},{5,13},{6,14},{7,15},{8,0},{9,1},... | collective-permute-start | bytes 49160 | tf_op jit(solution)/shard_map/ppermute | solution.py:304
  39.8 8.4 %copy-start.15 = (bf16[8,1024]{1,0:T(8,128)(2,1)}, bf16[8,1024]{1,0:T(8,128)(2,1)S(1)}, u32[]{:S(2)}) copy-start(bf16[8,1024]{1,0:T(8,128)(2,1)S(1)} %collective-permute-done.13.rest_5_.rest_7_) | copy-start | bytes 49156
  39.8 0.7 %collective-permute-start.11 = (bf16[8,1024]{1,0:T(8,128)(2,1)}, bf16[8,1024]{1,0:T(8,128)(2,1)S(1)}, u32[]{:S(2)}, u32[]{:S(2)}) collective-permute-start(bf16[8,1024]{1,0:T(8,128)(2,1)} %get-tuple-element.28), channel_id=1, source_target_pairs={{4,8},{5,9},{6,10},{7,11},{8,4},{9,5},{10,6},{11,7},{20,24},{21,25... | collective-permute-start | bytes 49160 | tf_op jit(solution)/shard_map/ppermute | solution.py:304
  40.4 7.8 %copy-start.18 = (bf16[8,1024]{1,0:T(8,128)(2,1)}, bf16[8,1024]{1,0:T(8,128)(2,1)S(1)}, u32[]{:S(2)}) copy-start(bf16[8,1024]{1,0:T(8,128)(2,1)S(1)} %collective-permute-done.11.rest_3_) | copy-start | bytes 49156
  40.4 7.7 %collective-permute-start.9 = (bf16[8,1024]{1,0:T(8,128)(2,1)}, bf16[8,1024]{1,0:T(8,128)(2,1)S(1)}, u32[]{:S(2)}, u32[]{:S(2)}) collective-permute-start(bf16[8,1024]{1,0:T(8,128)(2,1)} %get-tuple-element.28), channel_id=1, source_target_pairs={{0,4},{1,5},{2,6},{3,7},{8,12},{9,13},{10,14},{11,15},{4,0},{5,1},... | collective-permute-start | bytes 49160 | tf_op jit(solution)/shard_map/ppermute | solution.py:304
  49.4 8.8 %copy-start.6 = (f32[4096]{0:T(1024)S(1)}, f32[4096]{0:T(1024)}, u32[]{:S(2)}) copy-start(f32[4096]{0:T(1024)} %param.18) | copy-start | bytes 49156
  51.6 5.2 %collective-permute-start.14 = (bf16[64,1024]{1,0:T(8,128)(2,1)}, bf16[64,1024]{1,0:T(8,128)(2,1)S(1)}, u32[]{:S(2)}, u32[]{:S(2)}) collective-permute-start(bf16[64,1024]{1,0:T(8,128)(2,1)} %get-tuple-element.30), channel_id=1, source_target_pairs={{0,2},{1,3},{4,6},{5,7},{8,10},{9,11},{12,14},{13,15},{2,0},{3,1},... | collective-permute-start | bytes 393224 | tf_op jit(solution)/shard_map/ppermute | solution.py:304
  52.1 6.1 %collective-permute-start.15 = (bf16[64,1024]{1,0:T(8,128)(2,1)}, bf16[64,1024]{1,0:T(8,128)(2,1)S(1)}, u32[]{:S(2)}, u32[]{:S(2)}) collective-permute-start(bf16[64,1024]{1,0:T(8,128)(2,1)} %get-tuple-element.29.x0), channel_id=1, source_target_pairs={{0,1},{2,3},{4,5},{6,7},{8,9},{10,11},{12,13},{14,15},{1,0},{3,2},... | collective-permute-start | bytes 393224 | tf_op jit(solution)/shard_map/ppermute | solution.py:304
  56.8 1.4 %collective-permute-start.16 = (bf16[64,1024]{1,0:T(8,128)(2,1)S(1)}, bf16[64,1024]{1,0:T(8,128)(2,1)S(1)}, u32[]{:S(2)}, u32[]{:S(2)}) collective-permute-start(bf16[64,1024]{1,0:T(8,128)(2,1)S(1)} %collective-permute-done.14.x1), channel_id=1, source_target_pairs={{0,1},{2,3},{4,5},{6,7},{8,9},{10,11},{12,13},{14,15},{1,0},{3,2},... | collective-permute-start | bytes 393224 | tf_op jit(solution)/shard_map/ppermute | solution.py:304
  56.8 1.4 %collective-permute-start.3 = (bf16[8,4096]{1,0:T(8,128)(2,1)S(1)}, bf16[8,4096]{1,0:T(8,128)(2,1)S(1)}, u32[]{:S(2)}, u32[]{:S(2)}) collective-permute-start(bf16[8,4096]{1,0:T(8,128)(2,1)S(1)} %get-tuple-element.22), channel_id=1, source_target_pairs={{0,1},{2,3},{4,5},{6,7},{8,9},{10,11},{12,13},{14,15},{1,0},{3,2},... | collective-permute-start | bytes 196616 | tf_op jit(solution)/shard_map/ppermute | solution.py:304
  (13 other events, 11.5 us)

commit v2 on v1

v2 whole, which is shorter than its diff:
```python
import functools

import jax
import jax.numpy as jnp
from jax import lax
from jax.experimental import pallas as pl
from jax.experimental.pallas import tpu as pltpu
from jax.sharding import PartitionSpec as P

GROUPS = 4
PAIR = 2
RIM = 8
EPSILON = 1e-05
F32 = jnp.float32
BF16 = jnp.bfloat16
VMEM = pl.BlockSpec(memory_space=pltpu.VMEM)
SMEM = pl.BlockSpec(memory_space=pltpu.SMEM)
ANY = pl.BlockSpec(memory_space=pl.ANY)
HBM = pl.BlockSpec(memory_space=pltpu.HBM)


def dot(a, b, dims=((1,), (0,))):
    return lax.dot_general(a, b, (dims, ((), ())), preferred_element_type=F32)


def silu(v):
    half = 0.5 * v
    return half + half * jnp.tanh(half)


def split(a, parts):
    out = []
    for _ in range(parts):
        top = a.astype(BF16)
        out.append(top)
        a = a - top.astype(F32)
    return out


def doc_of(lengths, position):
    end, found = jnp.int32(0), jnp.zeros_like(position)
    for i in range(lengths.shape[0]):
        end = end + lengths[i]
        found = found + jnp.where(position >= end, 1, 0)
    return jnp.where(position >= 0, found, -1)


def log_sums(raw, bias, rate_log):
    v = raw.astype(F32) + bias
    step = jnp.maximum(v, 0.0) + jnp.log(1.0 + jnp.exp(-jnp.abs(v)))
    change = -jnp.exp(rate_log) * step
    rows = raw.shape[0]
    shape = (rows, 3 * rows)
    behind = lax.broadcasted_iota(jnp.int32, shape, 1) % rows
    lower = jnp.where(behind <= lax.broadcasted_iota(jnp.int32, shape, 0), 1.0, 0.0)
    sums = dot(lower.astype(BF16), jnp.concatenate(split(change, 3), axis=0))
    return step, sums


def selector(heads, columns, width, first):
    shape = (3 * heads, columns)
    head = lax.broadcasted_iota(jnp.int32, shape, 0) % heads
    owner = lax.broadcasted_iota(jnp.int32, shape, 1) // width + first
    return jnp.where(head == owner, 1.0, 0.0).astype(BF16)


def widen(compact, chosen):
    return dot(jnp.concatenate([p.astype(F32) for p in split(compact, 3)], axis=1).astype(BF16), chosen)


def convolve(padded, taps, bias, same):
    width = len(same)
    total = bias + taps[width : width + 1] * padded
    for back in range(1, width + 1):
        moved = pltpu.roll(padded, back, 0)
        total = total + taps[width - back : width - back + 1] * jnp.where(same[back - 1], moved, 0.0)
    return silu(total[RIM:]).astype(BF16)


def same_docs(lengths, first, rows, width):
    position = lax.broadcasted_iota(jnp.int32, (rows + RIM, 128), 0) + (first - RIM)
    doc = doc_of(lengths, position)
    return doc, [pltpu.roll(doc, back, 0) == doc for back in range(1, width + 1)]


def pick(first, a, b):
    return jnp.where(first, a, b)


def prepare_kernel(rows, raw, step_bias, rate_log, rim, tail, inner, sem):
    tok = raw.shape[0]
    copy = pltpu.make_async_copy(rows.at[tok - RIM :], rim, sem)
    copy.start()
    step, sums = log_sums(raw[...], step_bias[...], rate_log[...])
    last = sums[tok - 1 :]
    tail[:tok] = jnp.exp(last - sums) * step
    tail[tok:] = jnp.broadcast_to(jnp.exp(last), (8, raw.shape[1]))
    inner[:tok] = jnp.exp(sums)
    inner[tok:] = jnp.exp(-sums) * step
    copy.wait()


def states_kernel(keep, dims, state, lengths, own_hbm, other, tail_own, tail_other,
                  taps, bias, out, own, own_b, weighted, sems):
    heads, width, inner, tok = dims
    index = lax.axis_index("seq")
    core, row = index % 2, (index // 2) % 2
    columns = inner // GROUPS
    wanted = row if keep else 1 - row
    group = PAIR * core + wanted
    at = pl.multiple_of(group * columns, columns)
    at_b = pl.multiple_of(inner + core * 128, 128)
    copies = [
        pltpu.make_async_copy(own_hbm.at[:, pl.ds(at_b, 128)], own_b, sems.at[0]),
        pltpu.make_async_copy(own_hbm.at[:, pl.ds(at, columns)], own, sems.at[1]),
    ]
    for copy in copies:
        copy.start()
    is_first = core == 0
    chip_first = (index - core) * tok
    lens = [lengths[i] for i in range(lengths.shape[0])]
    lens = _Lengths(lens)
    doc, same = same_docs(lens, chip_first, 2 * tok, taps.shape[0] - 1)
    prior = doc_of(lens, chip_first - 1)
    end_a = doc_of(lens, chip_first + tok - 1)
    end_b = doc_of(lens, chip_first + 2 * tok - 1)
    tail_a = pick(is_first, tail_own[...], tail_other[...])
    tail_b = pick(is_first, tail_other[...], tail_own[...])
    scales, ends = [], []
    for part, (tail, end) in enumerate(((tail_a, end_a), (tail_b, end_b))):
        here = doc[RIM + part * tok : RIM + (part + 1) * tok, :heads] == end
        if part == 0:
            here = here & (lax.broadcasted_iota(jnp.int32, here.shape, 0) >= RIM)
        scales.append(jnp.where(here, tail[:tok], 0.0))
        ends.append(tail[tok : tok + 1])
    pass_a = jnp.where(end_a == prior, ends[0], 0.0)
    pass_b = jnp.where(end_b == end_a, ends[1], 0.0)
    rest = jnp.concatenate([pass_b, pass_a * pass_b, jnp.zeros((6, heads), F32)], axis=0)
    scale = widen(jnp.concatenate(scales + [rest], axis=0), selector(heads, columns, width, group * (heads // GROUPS)))
    for copy in copies:
        copy.wait()

    def padded(o, lanes, lanes_at):
        a, b = o[:, lanes].astype(F32), other[:, lanes_at].astype(F32)
        return jnp.concatenate([jnp.zeros((RIM, a.shape[1]), F32), pick(is_first, a, b), pick(is_first, b, a)], axis=0)

    b_pair = convolve(padded(own_b, slice(0, 128), pl.ds(at_b, 128)), taps[:, pl.ds(at_b, 128)], bias[pl.ds(at_b, 128)].reshape(1, 128), same)
    b_pair = b_pair.astype(F32)
    half = b_pair.shape[1] // 2
    b_rows = pick(wanted == 0, b_pair[:, :half], b_pair[:, half:]).astype(BF16)
    for j in range(columns // 128):
        lanes = slice(j * 128, (j + 1) * 128)
        lanes_at = pl.ds(pl.multiple_of(at + j * 128, 128), 128)
        x = convolve(padded(own, lanes, lanes_at), taps[:, lanes_at], bias[lanes_at].reshape(1, 128), same)
        weighted[:, lanes] = (x.astype(F32) * scale[: 2 * tok, lanes]).astype(BF16)
    state_a = dot(b_rows[:tok], weighted[:tok], ((0,), (0,)))
    state_b = dot(b_rows[tok:], weighted[tok:], ((0,), (0,)))
    passes = scale[2 * tok + 1 : 2 * tok + 2]
    total = scale[2 * tok : 2 * tok + 1] * state_a + state_b
    out[:state] = total.astype(out.dtype)
    if keep:
        out[state:] = jnp.broadcast_to(passes, (8, columns))
    else:
        out[state:] = two_rows(passes, (8, columns))


def rim_kernel(dims, lengths, own_hbm, other, rim_own, rim_other, tail_own, tail_other, taps, bias,
               out_sent, out_kept, own, own_b, sems):
    heads, width, inner, tok = dims
    index = lax.axis_index("seq")
    core, row = index % 2, (index // 2) % 2
    columns = inner // GROUPS
    at = pl.multiple_of(PAIR * core * columns, PAIR * columns)
    at_b = pl.multiple_of(inner + core * 128, 128)
    copies = [
        pltpu.make_async_copy(own_hbm.at[:RIM, pl.ds(at_b, 128)], own_b, sems.at[0]),
        pltpu.make_async_copy(own_hbm.at[:RIM, pl.ds(at, PAIR * columns)], own, sems.at[1]),
    ]
    for copy in copies:
        copy.start()
    is_first = core == 0
    chip_first = (index - core) * tok
    lens = _Lengths([lengths[i] for i in range(lengths.shape[0])])
    doc, same = same_docs(lens, chip_first, RIM, taps.shape[0] - 1)
    end_a = doc_of(lens, chip_first + tok - 1)
    end_b = doc_of(lens, chip_first + 2 * tok - 1)
    here = (doc[RIM:, :heads] == end_a) & (end_b == end_a)
    head_rows = pick(is_first, tail_own[:RIM], tail_other[:RIM])
    end_decay = pick(is_first, tail_other[tok : tok + 1], tail_own[tok : tok + 1])
    scale = jnp.where(here, head_rows * end_decay, 0.0)
    scale = widen(scale, selector(heads, PAIR * columns, width, core * (heads // PAIR)))
    for copy in copies:
        copy.wait()

    def mixed(o, lanes, first):
        lanes_at = pl.ds(pl.multiple_of(first + lanes.start, 128), 128)
        rim = pick(is_first, rim_own[:, lanes_at].astype(F32), rim_other[:, lanes_at].astype(F32))
        rows = jnp.concatenate([rim, pick(is_first, o[:, lanes].astype(F32), other[:RIM, lanes_at].astype(F32))], axis=0)
        return convolve(rows, taps[:, lanes_at], bias[lanes_at].reshape(1, 128), same).astype(F32)

    b_pair = mixed(own_b, slice(0, 128), at_b)
    half = b_pair.shape[1] // 2
    upper = row == 1
    for out, flip in ((out_sent, False), (out_kept, True)):
        which = upper if flip else row == 0
        b_rows = pick(which, b_pair[:, half:], b_pair[:, :half])
        out[RIM:] = jnp.zeros((RIM, columns), BF16)
        out[RIM:, :half] = b_rows.astype(BF16)
    for j in range(columns // 128):
        lanes = slice(j * 128, (j + 1) * 128)
        behind = slice(columns + j * 128, columns + (j + 1) * 128)
        low = mixed(own, lanes, at) * scale[:, lanes]
        high = mixed(own, behind, at) * scale[:, behind]
        out_sent[:RIM, lanes] = pick(upper, low, high).astype(BF16)
        out_kept[:RIM, lanes] = pick(upper, high, low).astype(BF16)


def late(rows):
    half = 64
    return dot(rows[RIM:, :half], rows[:RIM], ((0,), (0,)))


class _Lengths:
    def __init__(self, values):
        self.values, self.shape = values, (len(values),)

    def __getitem__(self, i):
        return self.values[i]


def two_rows(passes, shape):
    top = passes.astype(BF16).astype(F32)
    which = lax.broadcasted_iota(jnp.int32, shape, 0)
    both = jnp.where(which == 0, top, jnp.where(which == 1, passes - top, 0.0))
    return both.astype(BF16)


def one_row(payload):
    wide = payload[-8:].astype(F32)
    return wide[0:1] + wide[1:2]


def plane_kernel(state, own, own_rim, got, got_rim, out, far, base):
    upper = (lax.axis_index("seq") // 2) % 2 == 1
    mine = own[:state] + late(own_rim[...])
    theirs = got[:state].astype(F32) + late(got_rim[...])
    my_pass, their_pass = own[state : state + 1], one_row(got[...])
    first, second = pick(upper, theirs, mine), pick(upper, mine, theirs)
    first_pass, later_pass = pick(upper, their_pass, my_pass), pick(upper, my_pass, their_pass)
    total = (later_pass * first + second).astype(BF16)
    out[:state] = total
    far[...] = total
    out[state:] = two_rows(my_pass * their_pass, (8, own.shape[1]))
    base[:state] = first
    base[state:] = jnp.broadcast_to(first_pass, (8, own.shape[1]))


def arrive_kernel(reach, rows, base, *rest):
    parts, (out_own, out_sent) = rest[:-2], rest[-2:]
    index = lax.axis_index("seq")
    plane = index // GROUPS
    upper = (index // 2) % 2 == 1
    state = None
    for back in range(reach, 0, -1):
        even, odd = parts[2 * (back - 1) : 2 * back]
        source = plane - back
        is_even = (source + 2 * back) // back % 2 == 0
        there = source >= 0
        arrived = jnp.where(there, pick(is_even, even[...].astype(F32), odd[...].astype(F32)), 0.0)
        if state is None:
            state = arrived[:rows]
        else:
            state = arrived[:rows] + one_row(arrived) * state
    later = base[rows : rows + 1] * state + base[:rows]
    out_own[...] = pick(upper, later, state).astype(BF16)
    out_sent[...] = pick(upper, state, later).astype(BF16)


def local_kernel(dims, lengths, x_ref, bc_ref, before, before_bc, rim, rim_bc, gate, tail, decays, taps, bias,
                 taps_bc, bias_bc, skip, a_out, b_out, c_out, s_out, b_all, compact):
    heads, width, state, tok = dims
    g = pl.program_id(0)
    index = lax.axis_index("seq")
    core = index % 2
    is_first = core == 0
    first = index * tok
    lens = _Lengths([lengths[i] for i in range(lengths.shape[0])])
    doc, same = same_docs(lens, first, tok, taps.shape[0] - 1)
    prior = doc_of(lens, first - 1)
    final = doc_of(lens, first + tok - 1)

    def padded(ref, rim_ref, before_ref, lanes):
        top = pick(is_first, rim_ref[:, lanes].astype(F32), before_ref[:, lanes].astype(F32))
        return jnp.concatenate([top, ref[:, lanes].astype(F32)], axis=0)

    @pl.when(g == 0)
    def _():
        for j in range(bc_ref.shape[1] // 128):
            lanes = slice(j * 128, (j + 1) * 128)
            mixed = convolve(padded(bc_ref, rim_bc, before_bc, lanes), taps_bc[:, lanes], bias_bc[:, lanes], same)
            for k in range(128 // state):
                which = j * (128 // state) + k
                value = mixed.astype(F32)[:, k * state : (k + 1) * state].astype(BF16)
                if which < GROUPS:
                    b_all[which] = value
                else:
                    c_out[which - GROUPS] = value
        ending_decay = tail[tok : tok + 1]
        rest = jnp.concatenate(
            [ending_decay, jnp.where(final == prior, ending_decay, 0.0), skip[...], jnp.zeros((5, heads), F32)], axis=0)
        whole = jnp.concatenate([decays[...], rest], axis=0)
        compact[...] = jnp.concatenate([p.astype(F32) for p in split(whole, 3)], axis=1).astype(BF16)

    columns = x_ref.shape[1]
    wide = dot(compact[...], selector(heads, columns, width, g * (heads // GROUPS)))
    inward, outward = wide[:tok], wide[tok : 2 * tok]
    end_decay, passes, gains = (wide[2 * tok + k : 2 * tok + k + 1] for k in range(3))
    b_rows, c_rows = b_all[g], c_out[g]
    scores = dot(c_rows, b_rows, ((1,), (1,)))
    down, across = (lax.broadcasted_iota(jnp.int32, (tok, tok), k) for k in range(2))
    causal = (down >= across) & (doc[RIM:, :tok] == doc_of(lens, across + first))
    mask = jnp.where(causal, scores, 0.0)
    m_top, m_rest = split(mask, 2)
    here = doc[RIM:, :state] == final
    ending = jnp.where(here, b_rows.astype(F32), 0.0).astype(BF16)
    lhs = jnp.concatenate([m_top.astype(F32), m_rest.astype(F32)], axis=1).astype(BF16)
    entered = doc[RIM:] == prior
    for j in range(columns // 128):
        lanes = slice(j * 128, (j + 1) * 128)
        x = convolve(padded(x_ref, rim, before, lanes), taps[:, lanes], bias[:, lanes], same).astype(F32)
        scaled = x * outward[:, lanes]
        s_top, s_rest = split(scaled, 2)
        within = dot(lhs, jnp.concatenate([s_top, s_top], axis=0)) + dot(m_top, s_rest)
        local = dot(ending, s_top, ((0,), (0,))) + dot(ending, s_rest, ((0,), (0,)))
        opened = silu(gate[:, lanes].astype(F32))
        a_out[:, lanes] = (inward[:, lanes] * within + gains[:, lanes] * x) * opened
        b_out[:, lanes] = jnp.where(entered, inward[:, lanes] * opened, 0.0)
        s_out[:state, lanes] = (end_decay[:, lanes] * local).astype(BF16)
    s_out[state:] = two_rows(passes, (8, columns))


def finish_kernel(width, places, a_ref, b_ref, c_ref, prior, gain, *rest):
    arrivals, (out, ready, sems) = rest[: len(places)], rest[-3:]
    index = lax.axis_index("seq")
    core, row = index % 2, (index // 2) % 2
    second = core == 1
    state_rows, columns = arrivals[0].shape
    block = 256
    shape = (2 * block, block)
    r, c = lax.broadcasted_iota(jnp.int32, shape, 0) % block // width, lax.broadcasted_iota(jnp.int32, shape, 1) // width
    means = jnp.where(r == c, 1.0 / width, 0.0).astype(BF16)
    copies = []
    for k, (arrived, (far_core, far_row)) in enumerate(zip(arrivals, places)):
        group = PAIR * (1 - core if far_core else core) + (1 - row if far_row else row)
        c_rows = c_ref[group]
        first = pl.multiple_of(group * columns, columns)
        for j in range(columns // block):
            lanes = slice(j * block, (j + 1) * block)
            at = pl.ds(pl.multiple_of(first + j * block, block), block)
            state = arrived[:, lanes].astype(F32)
            before = prior[:, at].astype(F32)
            stepped = (before[state_rows : state_rows + 1] + before[state_rows + 1 : state_rows + 2]) * state + before[:state_rows]
            state = pick(second, stepped, state).astype(BF16)
            gated = a_ref[:, at] + b_ref[:, at] * dot(c_rows, state)
            top, rest_ = split(gated * gated, 2)
            mean = dot(jnp.concatenate([top, rest_], axis=1), means)
            ready[k, :, lanes] = (gated * lax.rsqrt(mean + EPSILON) * gain[:, at]).astype(BF16)
        copies.append(pltpu.make_async_copy(ready.at[k], out.at[:, pl.ds(first, columns)], sems.at[k]))
        copies[-1].start()
    for copy in copies:
        copy.wait()


def swap(block, pairs):
    return lax.ppermute(block, "seq", [*pairs, *((b, a) for a, b in pairs)])


def on_device(mixer_in, gate_in, step_raw, step_bias, rate_log, conv_weight, conv_bias, skip_gain, norm_gain, doc_lengths):
    tok, channels = mixer_in.shape
    heads, inner = rate_log.shape[0], gate_in.shape[1]
    width = inner // heads
    state = (channels - inner) // (2 * GROUPS)
    devices = lax.axis_size("seq")
    planes = devices // GROUPS
    columns = inner // GROUPS
    taps_n = conv_weight.shape[0]
    longest = devices * tok // 2
    reach = -(-(longest - 1) // (GROUPS * tok))
    row = lambda a: a.reshape(1, -1)
    step_bias, rate_log, skip_gain, norm_gain = map(row, (step_bias, rate_log, skip_gain, norm_gain))
    wide_bias = row(conv_bias)
    cores = [(i, i + 1) for i in range(0, devices, 2)]
    rows = [(i, i + 2) for i in range(0, devices, 4) for i in (i, i + 1)]
    chips = [(i, i + 1) for i in range(1, devices - 1, 2)]

    placed = pltpu.with_memory_space_constraint(mixer_in, pltpu.HBM)
    other = swap(mixer_in, cores)
    rim, tail, decays = pl.pallas_call(
        prepare_kernel,
        out_shape=(jax.ShapeDtypeStruct((RIM, channels), BF16), jax.ShapeDtypeStruct((tok + 8, heads), F32),
                   jax.ShapeDtypeStruct((2 * tok, heads), F32)),
        in_specs=[HBM] + [VMEM] * 3,
        out_specs=(VMEM,) * 3,
        scratch_shapes=[pltpu.SemaphoreType.DMA],
        compiler_params=pltpu.CompilerParams(vmem_limit_bytes=4 << 20),
        name="prepare",
    )(placed, step_raw, step_bias, rate_log)
    other_tail = swap(tail, cores)
    rim = swap(rim, chips)
    other_rim = swap(rim, cores)

    def params(mib):
        return pltpu.CompilerParams(vmem_limit_bytes=mib << 20)

    packed = jax.ShapeDtypeStruct((state + 8, columns), BF16)
    packed_wide = jax.ShapeDtypeStruct((state + 8, columns), F32)
    piece = jax.ShapeDtypeStruct((state, columns), BF16)
    dims = (heads, width, inner, tok)

    def states(keep):
        return pl.pallas_call(
            functools.partial(states_kernel, keep, dims, state),
            out_shape=packed_wide if keep else packed,
            in_specs=[SMEM, HBM] + [VMEM] * 5,
            out_specs=VMEM,
            scratch_shapes=[pltpu.VMEM((tok, columns), BF16), pltpu.VMEM((tok, 128), BF16),
                            pltpu.VMEM((2 * tok, columns), BF16), pltpu.SemaphoreType.DMA((2,))],
            compiler_params=params(8),
            name="states_kept" if keep else "states_sent",
        )(doc_lengths, placed, other, tail, other_tail, conv_weight, conv_bias)

    sent = states(False)
    got = swap(sent, rows)
    kept = states(True)
    corner = jax.ShapeDtypeStruct((2 * RIM, columns), BF16)
    rim_sent, rim_kept = pl.pallas_call(
        functools.partial(rim_kernel, dims),
        out_shape=(corner, corner),
        in_specs=[SMEM, HBM] + [VMEM] * 7,
        out_specs=(VMEM, VMEM),
        scratch_shapes=[pltpu.VMEM((RIM, PAIR * columns), BF16), pltpu.VMEM((RIM, 128), BF16), pltpu.SemaphoreType.DMA((2,))],
        compiler_params=params(4),
        name="rim_terms",
    )(doc_lengths, placed, other, rim, other_rim, tail, other_tail, conv_weight, conv_bias)
    rim_got = swap(rim_sent, rows)
    plane, far, base = pl.pallas_call(
        functools.partial(plane_kernel, state), out_shape=(packed, piece, packed_wide), in_specs=[VMEM] * 4, out_specs=(VMEM,) * 3,
        compiler_params=params(4), name="plane_total",
    )(kept, rim_kept, got, rim_got)
    parts = []
    for back in range(1, reach + 1):
        for parity in range(2):
            pairs = [
                (GROUPS * p + q, GROUPS * (p + back) + q)
                for p in range(planes - back) if p // back % 2 == parity
                for q in range(GROUPS)
            ]
            payload = far if back == reach else plane
            parts.append(swap(payload, pairs) if pairs else parts[-1])

    def whole(height, length):
        return pl.BlockSpec((height, length), lambda g: (0, 0))

    def by_group(height):
        return pl.BlockSpec((height, columns), lambda g: (0, g))

    rest = channels - inner
    bc = pl.BlockSpec((tok, rest), lambda g: (0, inner // rest))
    last = pl.BlockSpec((RIM, columns), lambda g: (tok // RIM - 1, g))
    last_bc = pl.BlockSpec((RIM, rest), lambda g: (tok // RIM - 1, inner // rest))
    a, b, c, own_state = pl.pallas_call(
        functools.partial(local_kernel, (heads, width, state, tok)),
        grid=(GROUPS,),
        out_shape=(
            jax.ShapeDtypeStruct((tok, inner), F32),
            jax.ShapeDtypeStruct((tok, inner), F32),
            jax.ShapeDtypeStruct((GROUPS, tok, state), BF16),
            jax.ShapeDtypeStruct((state + 8, inner), BF16),
        ),
        in_specs=[
            SMEM, by_group(tok), bc, last, last_bc, by_group(RIM), pl.BlockSpec((RIM, rest), lambda g: (0, inner // rest)),
            by_group(tok), whole(tok + 8, heads), whole(2 * tok, heads), by_group(taps_n), by_group(1),
            pl.BlockSpec((taps_n, rest), lambda g: (0, inner // rest)), pl.BlockSpec((1, rest), lambda g: (0, inner // rest)),
            whole(1, heads),
        ],
        out_specs=(by_group(tok), by_group(tok), pl.BlockSpec((GROUPS, tok, state), lambda g: (0, 0, 0)), by_group(state + 8)),
        scratch_shapes=[pltpu.VMEM((GROUPS, tok, state), BF16), pltpu.VMEM((2 * tok + 8, 3 * heads), BF16)],
        compiler_params=params(16),
        name="local_block",
        cost_estimate=pl.CostEstimate(flops=2 * 10**9, bytes_accessed=8 << 20, transcendentals=10**6),
    )(doc_lengths, mixer_in, mixer_in, other, other, rim, rim, gate_in, tail, decays, conv_weight, wide_bias,
      conv_weight, wide_bias, skip_gain)
    prior = swap(own_state, cores)

    x0, mine = pl.pallas_call(
        functools.partial(arrive_kernel, reach, state), out_shape=(piece, piece), in_specs=[VMEM] * (1 + 2 * reach),
        out_specs=(VMEM, VMEM), compiler_params=params(4), name="arrive",
    )(base, *parts)
    x1 = swap(mine, rows)
    x2 = swap(x0, cores)
    x3 = swap(x1, cores)

    def finish(out, places, *arrivals):
        count = len(places)
        return pl.pallas_call(
            functools.partial(finish_kernel, width, places),
            out_shape=jax.ShapeDtypeStruct((tok, inner), BF16),
            in_specs=[VMEM] * (5 + count) + [HBM] * (out is not None),
            out_specs=HBM,
            scratch_shapes=[pltpu.VMEM((count, tok, columns), BF16), pltpu.SemaphoreType.DMA((count,))],
            input_output_aliases={} if out is None else {5 + count: 0},
            compiler_params=params(8),
        )(a, b, c, prior, norm_gain, *arrivals, *([] if out is None else [out]))

    out = finish(None, ((False, False), (True, False)), x0, x2)
    out = finish(out, ((False, True),), x1)
    return finish(out, ((True, True),), x3)


def solution(mesh):
    split_rows = P(("groups", "seq"), None)
    return jax.shard_map(
        on_device,
        mesh=mesh,
        in_specs=(split_rows, split_rows, split_rows, P(), P(), P(), P(), P(), P(), P("groups")),
        out_specs=split_rows,
        check_vma=False,
    )
```

time: 62.1 us -> 55.5 us (0.89)
  starting transfers between devices: 25.9 us -> 16.7 us
  waiting for transfers between devices: 14.2 us -> 17.4 us
  local copies, waits for them, and re-layouts: 6.72 us -> 4.62 us
  Pallas kernels: 14.8 us -> 16.1 us
    ppermute x17 -> x13, starting transfers between devices: 25.9 us -> 16.7 us  [swap(): return lax.ppermute(block, 'seq', [*pairs, *((b, a) for a, b in pairs)])]
    ppermute x17 -> x13, waiting for transfers between devices: 14.2 us -> 17.4 us  [swap(): return lax.ppermute(block, 'seq', [*pairs, *((b, a) for a, b in pairs)])]
    pallas_call x5 -> x9, Pallas kernels: 10.5 us -> 11.9 us  [the longest x2 4.81 us: states(): pl.pallas_call(functools.partial(states_kernel, keep, dims, state), out_s...]
    unnamed x40 -> x20, local copies, waits for them, and re-layouts: 5.82 us -> 4.61 us
    slice x1 -> x0, local copies, waits for them, and re-layouts: 0.89 us -> none  [on_device(): rim = swap(mixer_in[tok - RIM:], chips)]
  transfers between devices with their start and end apart: 17 -> 13, of which waited for: 5 -> 5; matrix products, arithmetic and copies ran while one was open for 1% -> 0% of each run, Pallas kernels for 17% -> 19%
where the time goes in v2:
time: 55.5 us; the launch traced here: 55 us
  waiting for transfers between devices  17.4 us (31%)
  starting transfers between devices  16.7 us (30%)
  Pallas kernels  16.1 us (29%)
  local copies, waits for them, and re-layouts  4.62 us (8%)
    ppermute x13, waiting for transfers between devices, swap(): return lax.ppermute(block, 'seq', [*pairs, *((b, a) for a, b in pairs)])  17.4 us
    ppermute x13, starting transfers between devices, swap(): return lax.ppermute(block, 'seq', [*pairs, *((b, a) for a, b in pairs)])  16.7 us
    pallas_call x2, Pallas kernels, states(): pl.pallas_call(functools.partial(states_kernel, keep, dims, state), out_s...  4.81 us
    unnamed x20, local copies, waits for them, and re-layouts  4.61 us
    pallas_call x1, Pallas kernels, on_device(): pl.pallas_call(functools.partial(local_kernel, (heads, width, state, tok)...  4.23 us
    pallas_call x3, Pallas kernels, finish(): pl.pallas_call(functools.partial(finish_kernel, width, places), out_shape...  4.19 us
    pallas_call x1, Pallas kernels, on_device(): pl.pallas_call(functools.partial(rim_kernel, dims), out_shape=(corner, co...  1.52 us
  transfers between devices with their start and end apart: 13, of which 5 were waited for; matrix products, arithmetic and copies ran while one was open for 0% of the time, Pallas kernels for 19%

profile of v2, /device:TPU:0, one launch (start us, length us, event | category | flops | bytes accessed | tf_op | source)
XLA Modules:
  0.0 55.0 jit_solution(7169015799335377143)
XLA Ops:
  0.5 0.7 %copy-done.4 = bf16[64,64]{1,0:T(8,128)(2,1)S(1)} copy-done((bf16[64,64]{1,0:T(8,128)(2,1)S(1)}, bf16[64,64]{1,0:T(8,128)(2,1)}, u32[]{:S(2)}) %copy-start.4) | copy-done | bytes 8216
  1.2 0.7 %copy-done.6 = f32[64]{0:T(128)S(1)} copy-done((f32[64]{0:T(128)S(1)}, f32[64]{0:T(128)}, u32[]{:S(2)}) %copy-start.6) | copy-done | bytes 280
  2.5 0.9 %prepare.1 = (bf16[8,4608]{1,0:T(8,128)(2,1)S(1)}, f32[72,64]{1,0:T(8,128)S(1)}, f32[128,64]{1,0:T(8,128)S(1)}) custom-call(bf16[64,4608]{1,0:T(8,128)(2,1)} %own_hbm.5, bf16[64,64]{1,0:T(8,128)(2,1)S(1)} %copy-done.4, f32[1,64]{1,0:T(1,128)S(1)} %bitcast.7, f32[1,64]{1,0:T(1,128)S(1)} %bitcast.8), custom_call_target="tpu_custom_call" | custom-call | tf_op jit(solution)/shard_map/prepare/pallas_call | solution.py:398
  3.4 0.7 %collective-permute-start.1 = (bf16[8,4608]{1,0:T(8,128)(2,1)S(1)}, bf16[8,4608]{1,0:T(8,128)(2,1)S(1)}, u32[]{:S(2)}, u32[]{:S(2)}) collective-permute-start(bf16[8,4608]{1,0:T(8,128)(2,1)S(1)} %get-tuple-element.19), channel_id=1, source_target_pairs={{1,2},{3,4},{5,6},{7,8},{9,10},{11,12},{13,14},{2,1},{4,3},{6,5},{... | collective-permute-start | bytes 221192 | tf_op jit(solution)/shard_map/ppermute | solution.py:375
  4.8 0.9 %copy-done.1 = f32[4,4608]{1,0:T(4,128)S(1)} copy-done((f32[4,4608]{1,0:T(4,128)S(1)}, f32[4,4608]{1,0:T(4,128)}, u32[]{:S(2)}) %copy-start.1) | copy-done | bytes 73752
  5.7 1.0 %copy-done.8 = bf16[64,4096]{1,0:T(8,128)(2,1)S(1)} copy-done((bf16[64,4096]{1,0:T(8,128)(2,1)S(1)}, bf16[64,4096]{1,0:T(8,128)(2,1)}, u32[]{:S(2)}) %copy-start.8) | copy-done | bytes 524312
  6.8 4.2 %local_block.1 = (f32[64,4096]{1,0:T(8,128)S(1)}, f32[64,4096]{1,0:T(8,128)S(1)}, bf16[4,64,64]{2,1,0:T(8,128)(2,1)S(1)}, bf16[72,4096]{1,0:T(8,128)(2,1)S(1)}) custom-call(s32[6]{0:T(128)S(1)} %copy-done.5, bf16[64,4608]{1,0:T(8,128)(2,1)S(1)} %copy-done, bf16[64,4608]{1,0:T(8,128)(2,1)S(1)} %copy-done, ...), custom_call_target="tpu_custom_call" | custom-call | flops 2000000000 | bytes 8388608 | tf_op jit(solution)/shard_map/local_block/pallas_call | solution.py:471
  11.0 6.0 %collective-permute-start.2 = (bf16[72,4096]{1,0:T(8,128)(2,1)S(1)}, bf16[72,4096]{1,0:T(8,128)(2,1)S(1)}, u32[]{:S(2)}, u32[]{:S(2)}) collective-permute-start(bf16[72,4096]{1,0:T(8,128)(2,1)S(1)} %get-tuple-element.25), channel_id=1, source_target_pairs={{0,1},{2,3},{4,5},{6,7},{8,9},{10,11},{12,13},{14,15},{1,0},{3,2},... | collective-permute-start | bytes 1769480 | tf_op jit(solution)/shard_map/ppermute | solution.py:375
  17.0 1.6 %collective-permute-done.3.tail_other = f32[72,64]{1,0:T(8,128)S(1)} collective-permute-done((f32[72,64]{1,0:T(8,128)S(1)}, f32[72,64]{1,0:T(8,128)S(1)}, u32[]{:S(2)}, u32[]{:S(2)}) %collective-permute-start.3) | collective-permute-done | bytes 18464 | tf_op jit(solution)/shard_map/ppermute | solution.py:375
  18.6 2.4 %states_sent.1 = bf16[72,1024]{1,0:T(8,128)(2,1)S(1)} custom-call(s32[6]{0:T(128)S(1)} %copy-done.5, bf16[64,4608]{1,0:T(8,128)(2,1)} %own_hbm.5, bf16[64,4608]{1,0:T(8,128)(2,1)S(1)} %collective-permute-done.before.before_bc.other, f32[72,64]{1,0:T(8,128)S(1)} %get-tuple-element.20.tail.tail_own, f32[72,64]{1,0:T(8,128)S(1)} %collective-permute-done.3.tail_other, ...), custom_call_target="tpu_custom_call" | custom-call | tf_op jit(solution)/shard_map/states_sent/pallas_call | solution.py:421
  21.1 3.0 %collective-permute-start.5 = (bf16[72,1024]{1,0:T(8,128)(2,1)S(1)}, bf16[72,1024]{1,0:T(8,128)(2,1)S(1)}, u32[]{:S(2)}, u32[]{:S(2)}) collective-permute-start(bf16[72,1024]{1,0:T(8,128)(2,1)S(1)} %states_sent.1), channel_id=1, source_target_pairs={{0,2},{1,3},{4,6},{5,7},{8,10},{9,11},{12,14},{13,15},{2,0},{3,1},... | collective-permute-start | bytes 442376 | tf_op jit(solution)/shard_map/ppermute | solution.py:375
  24.2 1.2 %collective-permute-done.4.rim_other = bf16[8,4608]{1,0:T(8,128)(2,1)S(1)} collective-permute-done((bf16[8,4608]{1,0:T(8,128)(2,1)S(1)}, bf16[8,4608]{1,0:T(8,128)(2,1)S(1)}, u32[]{:S(2)}, u32[]{:S(2)}) %collective-permute-start.4) | collective-permute-done | bytes 73760 | tf_op jit(solution)/shard_map/ppermute | solution.py:375
  25.4 1.5 %rim_terms.1 = (bf16[16,1024]{1,0:T(8,128)(2,1)S(1)}, bf16[16,1024]{1,0:T(8,128)(2,1)S(1)}) custom-call(s32[6]{0:T(128)S(1)} %copy-done.5, bf16[64,4608]{1,0:T(8,128)(2,1)} %own_hbm.5, bf16[64,4608]{1,0:T(8,128)(2,1)S(1)} %collective-permute-done.before.before_bc.other, bf16[8,4608]{1,0:T(8,128)(2,1)S(1)} %collective-permute-done.1.rim.rim_bc.rim_own, ...), custom_call_target="tpu_custom_call" | custom-call | tf_op jit(solution)/shard_map/rim_terms/pallas_call | solution.py:436
  27.1 2.4 %states_kept.1.own = f32[72,1024]{1,0:T(8,128)S(1)} custom-call(s32[6]{0:T(128)S(1)} %copy-done.5, bf16[64,4608]{1,0:T(8,128)(2,1)} %own_hbm.5, bf16[64,4608]{1,0:T(8,128)(2,1)S(1)} %collective-permute-done.before.before_bc.other, f32[72,64]{1,0:T(8,128)S(1)} %get-tuple-element.20.tail.tail_own, f32[72,64]{1,0:T(8,128)S(1)} %collective-permute-done.3.tail_other, ...), custom_call_target="tpu_custom_call" | custom-call | tf_op jit(solution)/shard_map/states_kept/pallas_call | solution.py:421
  29.5 1.4 %collective-permute-done.6.got_rim = bf16[16,1024]{1,0:T(8,128)(2,1)S(1)} collective-permute-done((bf16[16,1024]{1,0:T(8,128)(2,1)S(1)}, bf16[16,1024]{1,0:T(8,128)(2,1)S(1)}, u32[]{:S(2)}, u32[]{:S(2)}) %collective-permute-start.6) | collective-permute-done | bytes 32800 | tf_op jit(solution)/shard_map/ppermute | solution.py:375
  31.2 1.6 %collective-permute-start.7 = (bf16[72,1024]{1,0:T(8,128)(2,1)S(1)}, bf16[72,1024]{1,0:T(8,128)(2,1)S(1)}, u32[]{:S(2)}, u32[]{:S(2)}) collective-permute-start(bf16[72,1024]{1,0:T(8,128)(2,1)S(1)} %get-tuple-element.29), channel_id=1, source_target_pairs={{0,4},{1,5},{2,6},{3,7},{8,12},{9,13},{10,14},{11,15},{4,0},{5,1},... | collective-permute-start | bytes 442376 | tf_op jit(solution)/shard_map/ppermute | solution.py:375
  32.8 0.7 %collective-permute-start.8 = (bf16[72,1024]{1,0:T(8,128)(2,1)S(1)}, bf16[72,1024]{1,0:T(8,128)(2,1)S(1)}, u32[]{:S(2)}, u32[]{:S(2)}) collective-permute-start(bf16[72,1024]{1,0:T(8,128)(2,1)S(1)} %get-tuple-element.29), channel_id=1, source_target_pairs={{4,8},{5,9},{6,10},{7,11},{8,4},{9,5},{10,6},{11,7},{20,24},{21,25... | collective-permute-start | bytes 442376 | tf_op jit(solution)/shard_map/ppermute | solution.py:375
  33.5 3.2 %collective-permute-start.9 = (bf16[64,1024]{1,0:T(8,128)(2,1)S(1)}, bf16[64,1024]{1,0:T(8,128)(2,1)S(1)}, u32[]{:S(2)}, u32[]{:S(2)}) collective-permute-start(bf16[64,1024]{1,0:T(8,128)(2,1)S(1)} %get-tuple-element.30), channel_id=1, source_target_pairs={{0,8},{1,9},{2,10},{3,11},{4,12},{5,13},{6,14},{7,15},{8,0},{9,1},... | collective-permute-start | bytes 393224 | tf_op jit(solution)/shard_map/ppermute | solution.py:375
  36.7 8.9 %collective-permute-done.9.rest_2_.rest_3_ = bf16[64,1024]{1,0:T(8,128)(2,1)S(1)} collective-permute-done((bf16[64,1024]{1,0:T(8,128)(2,1)S(1)}, bf16[64,1024]{1,0:T(8,128)(2,1)S(1)}, u32[]{:S(2)}, u32[]{:S(2)}) %collective-permute-start.9) | collective-permute-done | bytes 131104 | tf_op jit(solution)/shard_map/ppermute | solution.py:375
  45.7 0.7 %collective-permute-start.10 = (bf16[64,1024]{1,0:T(8,128)(2,1)S(1)}, bf16[64,1024]{1,0:T(8,128)(2,1)S(1)}, u32[]{:S(2)}, u32[]{:S(2)}) collective-permute-start(bf16[64,1024]{1,0:T(8,128)(2,1)S(1)} %get-tuple-element.31), channel_id=1, source_target_pairs={{0,2},{1,3},{4,6},{5,7},{8,10},{9,11},{12,14},{13,15},{2,0},{3,1},... | collective-permute-start | bytes 393224 | tf_op jit(solution)/shard_map/ppermute | solution.py:375
  46.4 4.4 %collective-permute-done.10.rest_0_ = bf16[64,1024]{1,0:T(8,128)(2,1)S(1)} collective-permute-done((bf16[64,1024]{1,0:T(8,128)(2,1)S(1)}, bf16[64,1024]{1,0:T(8,128)(2,1)S(1)}, u32[]{:S(2)}, u32[]{:S(2)}) %collective-permute-start.10) | collective-permute-done | bytes 131104 | tf_op jit(solution)/shard_map/ppermute | solution.py:375
  50.8 1.7 %shard_map.100.rest_1_ = bf16[64,4096]{1,0:T(8,128)(2,1)} custom-call(f32[64,4096]{1,0:T(8,128)S(1)} %get-tuple-element.22.a_ref, f32[64,4096]{1,0:T(8,128)S(1)} %get-tuple-element.23.b_ref, bf16[4,64,64]{2,1,0:T(8,128)(2,1)S(1)} %get-tuple-element.24.c_ref, bf16[72,4096]{1,0:T(8,128)(2,1)S(1)} %collective-permute-done.2.prior, f32[1,4096]{1,0:T(1,128)S(1)} %bitcast.4, ...), custom_call_target="tpu_custom_call" | custom-call | tf_op jit(solution)/shard_map/pallas_call | solution.py:505
  52.5 1.3 %shard_map.101.rest_1_ = bf16[64,4096]{1,0:T(8,128)(2,1)} custom-call(f32[64,4096]{1,0:T(8,128)S(1)} %get-tuple-element.22.a_ref, f32[64,4096]{1,0:T(8,128)S(1)} %get-tuple-element.23.b_ref, bf16[4,64,64]{2,1,0:T(8,128)(2,1)S(1)} %get-tuple-element.24.c_ref, bf16[72,4096]{1,0:T(8,128)(2,1)S(1)} %collective-permute-done.2.prior, ...), custom_call_target="tpu_custom_call", output_to_operand_aliasing={{}: (6, {})} | custom-call | tf_op jit(solution)/shard_map/pallas_call | solution.py:505
  53.8 1.3 %shard_map.102 = bf16[64,4096]{1,0:T(8,128)(2,1)} custom-call(f32[64,4096]{1,0:T(8,128)S(1)} %get-tuple-element.22.a_ref, f32[64,4096]{1,0:T(8,128)S(1)} %get-tuple-element.23.b_ref, bf16[4,64,64]{2,1,0:T(8,128)(2,1)S(1)} %get-tuple-element.24.c_ref, bf16[72,4096]{1,0:T(8,128)(2,1)S(1)} %collective-permute-done.2.prior, ...), custom_call_target="tpu_custom_call", output_to_operand_aliasing={{}: (6, {})} | custom-call | tf_op jit(solution)/shard_map/pallas_call | solution.py:505
  (33 shorter events, 2.6 us)
Async XLA Ops:
  0.0 4.2 %copy-start = (bf16[64,4608]{1,0:T(8,128)(2,1)S(1)}, bf16[64,4608]{1,0:T(8,128)(2,1)}, u32[]{:S(2)}) copy-start(bf16[64,4608]{1,0:T(8,128)(2,1)} %own_hbm.5) | copy-start | bytes 1769476
  0.0 4.2 %collective-permute-start = (bf16[64,4608]{1,0:T(8,128)(2,1)}, bf16[64,4608]{1,0:T(8,128)(2,1)S(1)}, u32[]{:S(2)}, u32[]{:S(2)}) collective-permute-start(bf16[64,4608]{1,0:T(8,128)(2,1)} %own_hbm.5), channel_id=1, source_target_pairs={{0,1},{2,3},{4,5},{6,7},{8,9},{10,11},{12,13},{14,15},{1,0},{3,2},... | collective-permute-start | bytes 1769480 | tf_op jit(solution)/shard_map/ppermute | solution.py:375
  0.5 0.7 %copy-start.4 = (bf16[64,64]{1,0:T(8,128)(2,1)S(1)}, bf16[64,64]{1,0:T(8,128)(2,1)}, u32[]{:S(2)}) copy-start(bf16[64,64]{1,0:T(8,128)(2,1)} %raw.1) | copy-start | bytes 24580
  1.2 0.7 %copy-start.6 = (f32[64]{0:T(128)S(1)}, f32[64]{0:T(128)}, u32[]{:S(2)}) copy-start(f32[64]{0:T(128)} %param.13) | copy-start | bytes 772
  1.9 0.7 %copy-start.7 = (f32[64]{0:T(128)S(1)}, f32[64]{0:T(128)}, u32[]{:S(2)}) copy-start(f32[64]{0:T(128)} %param.14) | copy-start | bytes 772
  2.5 1.6 %copy-start.2 = (f32[4608]{0:T(1024)S(1)}, f32[4608]{0:T(1024)}, u32[]{:S(2)}) copy-start(f32[4608]{0:T(1024)} %bias.5) | copy-start | bytes 55300
  3.4 0.7 %collective-permute-start.1 = (bf16[8,4608]{1,0:T(8,128)(2,1)S(1)}, bf16[8,4608]{1,0:T(8,128)(2,1)S(1)}, u32[]{:S(2)}, u32[]{:S(2)}) collective-permute-start(bf16[8,4608]{1,0:T(8,128)(2,1)S(1)} %get-tuple-element.19), channel_id=1, source_target_pairs={{1,2},{3,4},{5,6},{7,8},{9,10},{11,12},{13,14},{2,1},{4,3},{6,5},{... | collective-permute-start | bytes 221192 | tf_op jit(solution)/shard_map/ppermute | solution.py:375
  4.2 0.7 %copy-start.5 = (s32[6]{0:T(128)S(1)}, s32[6]{0:T(128)}, u32[]{:S(2)}) copy-start(s32[6]{0:T(128)} %lengths.7) | copy-start | bytes 76
  4.2 0.7 %copy-start.9 = (f32[64]{0:T(128)S(1)}, f32[64]{0:T(128)}, u32[]{:S(2)}) copy-start(f32[64]{0:T(128)} %param.17) | copy-start | bytes 772
  4.8 0.9 %copy-start.1 = (f32[4,4608]{1,0:T(4,128)S(1)}, f32[4,4608]{1,0:T(4,128)}, u32[]{:S(2)}) copy-start(f32[4,4608]{1,0:T(4,128)} %taps.7) | copy-start | bytes 221188
  5.7 1.0 %copy-start.8 = (bf16[64,4096]{1,0:T(8,128)(2,1)S(1)}, bf16[64,4096]{1,0:T(8,128)(2,1)}, u32[]{:S(2)}) copy-start(bf16[64,4096]{1,0:T(8,128)(2,1)} %gate.1) | copy-start | bytes 1572868
  11.0 39.8 %collective-permute-start.2 = (bf16[72,4096]{1,0:T(8,128)(2,1)S(1)}, bf16[72,4096]{1,0:T(8,128)(2,1)S(1)}, u32[]{:S(2)}, u32[]{:S(2)}) collective-permute-start(bf16[72,4096]{1,0:T(8,128)(2,1)S(1)} %get-tuple-element.25), channel_id=1, source_target_pairs={{0,1},{2,3},{4,5},{6,7},{8,9},{10,11},{12,13},{14,15},{1,0},{3,2},... | collective-permute-start | bytes 1769480 | tf_op jit(solution)/shard_map/ppermute | solution.py:375
  17.0 1.7 %collective-permute-start.3 = (f32[72,64]{1,0:T(8,128)S(1)}, f32[72,64]{1,0:T(8,128)S(1)}, u32[]{:S(2)}, u32[]{:S(2)}) collective-permute-start(f32[72,64]{1,0:T(8,128)S(1)} %get-tuple-element.20.tail.tail_own), channel_id=1, source_target_pairs={{0,1},{2,3},{4,5},{6,7},{8,9},{10,11},{12,13},{14,15},{1,0},{3,2},... | collective-permute-start | bytes 55304 | tf_op jit(solution)/shard_map/ppermute | solution.py:375
  21.1 9.8 %collective-permute-start.5 = (bf16[72,1024]{1,0:T(8,128)(2,1)S(1)}, bf16[72,1024]{1,0:T(8,128)(2,1)S(1)}, u32[]{:S(2)}, u32[]{:S(2)}) collective-permute-start(bf16[72,1024]{1,0:T(8,128)(2,1)S(1)} %states_sent.1), channel_id=1, source_target_pairs={{0,2},{1,3},{4,6},{5,7},{8,10},{9,11},{12,14},{13,15},{2,0},{3,1},... | collective-permute-start | bytes 442376 | tf_op jit(solution)/shard_map/ppermute | solution.py:375
  24.1 1.3 %collective-permute-start.4 = (bf16[8,4608]{1,0:T(8,128)(2,1)S(1)}, bf16[8,4608]{1,0:T(8,128)(2,1)S(1)}, u32[]{:S(2)}, u32[]{:S(2)}) collective-permute-start(bf16[8,4608]{1,0:T(8,128)(2,1)S(1)} %collective-permute-done.1.rim.rim_bc.rim_own), channel_id=1, source_target_pairs={{0,1},{2,3},{4,5},{6,7},{8,9},{10,11},{12,13},{14,15},{1,0},{3,2},... | collective-permute-start | bytes 221192 | tf_op jit(solution)/shard_map/ppermute | solution.py:375
  26.9 4.0 %collective-permute-start.6 = (bf16[16,1024]{1,0:T(8,128)(2,1)S(1)}, bf16[16,1024]{1,0:T(8,128)(2,1)S(1)}, u32[]{:S(2)}, u32[]{:S(2)}) collective-permute-start(bf16[16,1024]{1,0:T(8,128)(2,1)S(1)} %get-tuple-element.27), channel_id=1, source_target_pairs={{0,2},{1,3},{4,6},{5,7},{8,10},{9,11},{12,14},{13,15},{2,0},{3,1},... | collective-permute-start | bytes 98312 | tf_op jit(solution)/shard_map/ppermute | solution.py:375
  31.2 14.4 %collective-permute-start.7 = (bf16[72,1024]{1,0:T(8,128)(2,1)S(1)}, bf16[72,1024]{1,0:T(8,128)(2,1)S(1)}, u32[]{:S(2)}, u32[]{:S(2)}) collective-permute-start(bf16[72,1024]{1,0:T(8,128)(2,1)S(1)} %get-tuple-element.29), channel_id=1, source_target_pairs={{0,4},{1,5},{2,6},{3,7},{8,12},{9,13},{10,14},{11,15},{4,0},{5,1},... | collective-permute-start | bytes 442376 | tf_op jit(solution)/shard_map/ppermute | solution.py:375
  32.8 12.8 %collective-permute-start.8 = (bf16[72,1024]{1,0:T(8,128)(2,1)S(1)}, bf16[72,1024]{1,0:T(8,128)(2,1)S(1)}, u32[]{:S(2)}, u32[]{:S(2)}) collective-permute-start(bf16[72,1024]{1,0:T(8,128)(2,1)S(1)} %get-tuple-element.29), channel_id=1, source_target_pairs={{4,8},{5,9},{6,10},{7,11},{8,4},{9,5},{10,6},{11,7},{20,24},{21,25... | collective-permute-start | bytes 442376 | tf_op jit(solution)/shard_map/ppermute | solution.py:375
  33.5 12.1 %collective-permute-start.9 = (bf16[64,1024]{1,0:T(8,128)(2,1)S(1)}, bf16[64,1024]{1,0:T(8,128)(2,1)S(1)}, u32[]{:S(2)}, u32[]{:S(2)}) collective-permute-start(bf16[64,1024]{1,0:T(8,128)(2,1)S(1)} %get-tuple-element.30), channel_id=1, source_target_pairs={{0,8},{1,9},{2,10},{3,11},{4,12},{5,13},{6,14},{7,15},{8,0},{9,1},... | collective-permute-start | bytes 393224 | tf_op jit(solution)/shard_map/ppermute | solution.py:375
  45.6 5.2 %copy-start.3 = (f32[4096]{0:T(1024)S(1)}, f32[4096]{0:T(1024)}, u32[]{:S(2)}) copy-start(f32[4096]{0:T(1024)} %param.18) | copy-start | bytes 49156
  45.7 5.0 %collective-permute-start.10 = (bf16[64,1024]{1,0:T(8,128)(2,1)S(1)}, bf16[64,1024]{1,0:T(8,128)(2,1)S(1)}, u32[]{:S(2)}, u32[]{:S(2)}) collective-permute-start(bf16[64,1024]{1,0:T(8,128)(2,1)S(1)} %get-tuple-element.31), channel_id=1, source_target_pairs={{0,2},{1,3},{4,6},{5,7},{8,10},{9,11},{12,14},{13,15},{2,0},{3,1},... | collective-permute-start | bytes 393224 | tf_op jit(solution)/shard_map/ppermute | solution.py:375
  46.4 4.4 %collective-permute-start.12 = (bf16[64,1024]{1,0:T(8,128)(2,1)S(1)}, bf16[64,1024]{1,0:T(8,128)(2,1)S(1)}, u32[]{:S(2)}, u32[]{:S(2)}) collective-permute-start(bf16[64,1024]{1,0:T(8,128)(2,1)S(1)} %get-tuple-element.32.rest_0_), channel_id=1, source_target_pairs={{0,1},{2,3},{4,5},{6,7},{8,9},{10,11},{12,13},{14,15},{1,0},{3,2},... | collective-permute-start | bytes 393224 | tf_op jit(solution)/shard_map/ppermute | solution.py:375
  50.8 3.0 %collective-permute-start.11 = (bf16[64,1024]{1,0:T(8,128)(2,1)S(1)}, bf16[64,1024]{1,0:T(8,128)(2,1)S(1)}, u32[]{:S(2)}, u32[]{:S(2)}) collective-permute-start(bf16[64,1024]{1,0:T(8,128)(2,1)S(1)} %collective-permute-done.10.rest_0_), channel_id=1, source_target_pairs={{0,1},{2,3},{4,5},{6,7},{8,9},{10,11},{12,13},{14,15},{1,0},{3,2},... | collective-permute-start | bytes 393224 | tf_op jit(solution)/shard_map/ppermute | solution.py:375

commit v3 on v2

v3 whole, which is shorter than its diff:
```python
import functools

import jax
import jax.numpy as jnp
from jax import lax
from jax.experimental import pallas as pl
from jax.experimental.pallas import tpu as pltpu
from jax.sharding import PartitionSpec as P

GROUPS = 4
PAIR = 2
RIM = 8
EPSILON = 1e-05
F32 = jnp.float32
BF16 = jnp.bfloat16
VMEM = pl.BlockSpec(memory_space=pltpu.VMEM)
HBM = pl.BlockSpec(memory_space=pltpu.HBM)


def dot(a, b, dims=((1,), (0,))):
    return lax.dot_general(a, b, (dims, ((), ())), preferred_element_type=F32)


def silu(v):
    half = 0.5 * v
    return half + half * jnp.tanh(half)


def split(a, parts):
    out = []
    for _ in range(parts):
        top = a.astype(BF16)
        out.append(top)
        a = a - top.astype(F32)
    return out


def doc_of(ends, position):
    found = jnp.zeros(position.shape, jnp.int32)
    for i in range(ends.shape[0]):
        found = found + jnp.where(position >= ends[i : i + 1, : position.shape[1]], 1, 0)
    return jnp.where(position >= 0, found, -1)


def doc_at(ends, place):
    return doc_of(ends, jnp.broadcast_to(place, (1, ends.shape[1])))


def log_sums(raw, bias, rate_log):
    v = raw.astype(F32) + bias
    step = jnp.maximum(v, 0.0) + jnp.log(1.0 + jnp.exp(-jnp.abs(v)))
    change = -jnp.exp(rate_log) * step
    down, across = (lax.broadcasted_iota(jnp.int32, (raw.shape[0],) * 2, k) for k in range(2))
    lower = jnp.where(across <= down, 1.0, 0.0).astype(BF16)
    sums = sum(dot(lower, part) for part in split(change, 3))
    return step, sums


def selector(heads, columns, width, first):
    start = (lax.broadcasted_iota(jnp.int32, (heads, 128), 0) - first) * width
    lane = lax.broadcasted_iota(jnp.int32, (heads, 128), 1)
    tiles = []
    for j in range(columns // 128):
        column = lane + j * 128
        tiles.append(jnp.where((column >= start) & (column < start + width), 1.0, 0.0))
    once = jnp.concatenate(tiles, axis=1).astype(BF16)
    return jnp.concatenate([once] * 3, axis=0)


def widen(compact, chosen):
    return dot(jnp.concatenate([p.astype(F32) for p in split(compact, 3)], axis=1).astype(BF16), chosen)


def convolve(padded, taps, bias, same):
    width = len(same)
    total = bias + taps[width : width + 1] * padded
    for back in range(1, width + 1):
        moved = pltpu.roll(padded, back, 0)
        total = total + taps[width - back : width - back + 1] * jnp.where(same[back - 1], moved, 0.0)
    return silu(total[RIM:]).astype(BF16)


def same_docs(ends, first, rows, width):
    position = lax.broadcasted_iota(jnp.int32, (rows + RIM, 128), 0) + (first - RIM)
    doc = doc_of(ends, position)
    return doc, [pltpu.roll(doc, back, 0) == doc for back in range(1, width + 1)]


def pick(first, a, b):
    return jnp.where(first, a, b)


def load_kernel(lengths, rows, raw, step_bias, rate_log, taps, bias, out_rows, rim, out_raw, out_bias, out_rate, out_taps,
                out_conv, ends, lens, sems):
    tok = rows.shape[0]
    moves = [
        (lengths, lens), (rows.at[tok - RIM :], rim), (raw, out_raw), (step_bias, out_bias), (rate_log, out_rate),
        (taps, out_taps), (bias, out_conv), (rows, out_rows),
    ]
    copies = [pltpu.make_async_copy(a, b, sems.at[k]) for k, (a, b) in enumerate(moves)]
    for copy in copies:
        copy.start()
    copies[0].wait()
    end = jnp.int32(0)
    for i in range(lengths.shape[0]):
        end = end + lens[i]
        ends[i : i + 1] = jnp.broadcast_to(end, (1, 128))
    for copy in copies[1:]:
        copy.wait()


def states_kernel(keep, dims, state, ends_ref, own, other, *rest):
    heads, width, inner, tok = dims
    if keep:
        compact, taps, bias, out, weighted = rest
    else:
        raw_own, raw_other, step_bias, rate_log, taps, bias, out, compact, weighted = rest
    index = lax.axis_index("seq")
    core, row = index % 2, (index // 2) % 2
    columns = inner // GROUPS
    wanted = row if keep else 1 - row
    group = PAIR * core + wanted
    at = pl.multiple_of(group * columns, columns)
    at_b = pl.multiple_of(inner + core * 128, 128)
    is_first = core == 0
    chip_first = (index - core) * tok
    ends = ends_ref[...]
    doc, same = same_docs(ends, chip_first, 2 * tok, taps.shape[0] - 1)
    if not keep:
        prior, end_a, end_b = (
            doc_at(ends, chip_first + place)[:, :heads] for place in (-1, tok - 1, 2 * tok - 1)
        )
        one, two = (log_sums(raw[...], step_bias[...], rate_log[...]) for raw in (raw_own, raw_other))
        scales, lasts = [], []
        for part, end in enumerate((end_a, end_b)):
            step, sums = (pick(is_first == (part == 0), a, b) for a, b in zip(one, two))
            last = sums[tok - 1 :]
            here = doc[RIM + part * tok : RIM + (part + 1) * tok, :heads] == end
            scales.append(jnp.where(here, jnp.exp(last - sums) * step, 0.0))
            lasts.append(jnp.exp(last))
        pass_a = jnp.where(end_a == prior, lasts[0], 0.0)
        pass_b = jnp.where(end_b == end_a, lasts[1], 0.0)
        compact[:RIM] = jnp.zeros((RIM, heads), F32)
        compact[RIM:tok] = scales[0][RIM:]
        compact[tok : 2 * tok] = scales[1]
        which = lax.broadcasted_iota(jnp.int32, (8, heads), 0)
        compact[2 * tok : 2 * tok + 8] = jnp.where(which == 0, pass_b, jnp.where(which == 1, pass_a * pass_b, 0.0))
        compact[2 * tok + 8 :] = scales[0][:RIM] * pass_b
    scale = widen(compact[: 2 * tok + 8], selector(heads, columns, width, group * (heads // GROUPS)))

    def padded(lanes_at):
        a, b = own[:, lanes_at].astype(F32), other[:, lanes_at].astype(F32)
        return jnp.concatenate([jnp.zeros((RIM, a.shape[1]), F32), pick(is_first, a, b), pick(is_first, b, a)], axis=0)

    here_b = pl.ds(at_b, 128)
    b_pair = convolve(padded(here_b), taps[:, here_b], bias[here_b].reshape(1, 128), same).astype(F32)
    half = b_pair.shape[1] // 2
    b_rows = pick(wanted == 0, b_pair[:, :half], b_pair[:, half:]).astype(BF16)
    for j in range(columns // 128):
        lanes = slice(j * 128, (j + 1) * 128)
        lanes_at = pl.ds(pl.multiple_of(at + j * 128, 128), 128)
        x = convolve(padded(lanes_at), taps[:, lanes_at], bias[lanes_at].reshape(1, 128), same)
        weighted[:, lanes] = (x.astype(F32) * scale[: 2 * tok, lanes]).astype(BF16)
    state_a = dot(b_rows[:tok], weighted[:tok], ((0,), (0,)))
    state_b = dot(b_rows[tok:], weighted[tok:], ((0,), (0,)))
    passes = scale[2 * tok + 1 : 2 * tok + 2]
    total = scale[2 * tok : 2 * tok + 1] * state_a + state_b
    out[:state] = total.astype(out.dtype)
    if keep:
        out[state:] = jnp.broadcast_to(passes, (8, columns))
    else:
        out[state:] = two_rows(passes, (8, columns))


def rim_kernel(dims, ends, own, other, rim_own, rim_other, compact, taps, bias, out_sent, out_kept):
    heads, width, inner, tok = dims
    index = lax.axis_index("seq")
    core, row = index % 2, (index // 2) % 2
    columns = inner // GROUPS
    at = pl.multiple_of(PAIR * core * columns, PAIR * columns)
    at_b = pl.multiple_of(inner + core * 128, 128)
    is_first = core == 0
    chip_first = (index - core) * tok
    _, same = same_docs(ends[...], chip_first, RIM, taps.shape[0] - 1)
    scale = widen(compact[2 * tok + 8 :], selector(heads, PAIR * columns, width, core * (heads // PAIR)))

    def mixed(lanes_at):
        rim = pick(is_first, rim_own[:, lanes_at].astype(F32), rim_other[:, lanes_at].astype(F32))
        top = pick(is_first, own[:RIM, lanes_at].astype(F32), other[:RIM, lanes_at].astype(F32))
        rows = jnp.concatenate([rim, top], axis=0)
        return convolve(rows, taps[:, lanes_at], bias[lanes_at].reshape(1, 128), same).astype(F32)

    b_pair = mixed(pl.ds(at_b, 128))
    half = b_pair.shape[1] // 2
    upper = row == 1
    for out, which in ((out_sent, row == 0), (out_kept, upper)):
        b_rows = pick(which, b_pair[:, half:], b_pair[:, :half])
        out[RIM:] = jnp.zeros((RIM, columns), BF16)
        out[RIM:, :half] = b_rows.astype(BF16)
    for j in range(columns // 128):
        lanes = slice(j * 128, (j + 1) * 128)
        behind = slice(columns + j * 128, columns + (j + 1) * 128)
        low = mixed(pl.ds(pl.multiple_of(at + j * 128, 128), 128)) * scale[:, lanes]
        high = mixed(pl.ds(pl.multiple_of(at + columns + j * 128, 128), 128)) * scale[:, behind]
        out_sent[:RIM, lanes] = pick(upper, low, high).astype(BF16)
        out_kept[:RIM, lanes] = pick(upper, high, low).astype(BF16)


def late(rows, state):
    return dot(rows[RIM:, :state], rows[:RIM], ((0,), (0,)))


def two_rows(passes, shape):
    top = passes.astype(BF16).astype(F32)
    which = lax.broadcasted_iota(jnp.int32, shape, 0)
    both = jnp.where(which == 0, top, jnp.where(which == 1, passes - top, 0.0))
    return both.astype(BF16)


def one_row(payload):
    wide = payload[-8:].astype(F32)
    return wide[0:1] + wide[1:2]


def plane_kernel(state, own, own_rim, got, got_rim, out, far, base):
    upper = (lax.axis_index("seq") // 2) % 2 == 1
    mine = own[:state] + late(own_rim[...], state)
    theirs = got[:state].astype(F32) + late(got_rim[...], state)
    my_pass, their_pass = own[state : state + 1], one_row(got[...])
    first, second = pick(upper, theirs, mine), pick(upper, mine, theirs)
    first_pass, later_pass = pick(upper, their_pass, my_pass), pick(upper, my_pass, their_pass)
    total = (later_pass * first + second).astype(BF16)
    out[:state] = total
    far[...] = total
    out[state:] = two_rows(my_pass * their_pass, (8, own.shape[1]))
    base[:state] = first
    base[state:] = jnp.broadcast_to(first_pass, (8, own.shape[1]))


def arrive_kernel(reach, rows, base, *rest):
    parts, (out_own, out_sent) = rest[:-2], rest[-2:]
    index = lax.axis_index("seq")
    plane = index // GROUPS
    upper = (index // 2) % 2 == 1
    state = None
    for back in range(reach, 0, -1):
        even, odd = parts[2 * (back - 1) : 2 * back]
        source = plane - back
        is_even = (source + 2 * back) // back % 2 == 0
        there = source >= 0
        arrived = jnp.where(there, pick(is_even, even[...].astype(F32), odd[...].astype(F32)), 0.0)
        if state is None:
            state = arrived[:rows]
        else:
            state = arrived[:rows] + one_row(arrived) * state
    later = base[rows : rows + 1] * state + base[:rows]
    out_own[...] = pick(upper, later, state).astype(BF16)
    out_sent[...] = pick(upper, state, later).astype(BF16)


def local_kernel(dims, ends_ref, x_ref, bc_ref, before, before_bc, rim, rim_bc, gate, raw, step_bias, rate_log, taps, bias,
                 taps_bc, bias_bc, skip, a_out, b_out, c_out, s_out, b_all, compact):
    heads, width, state, tok = dims
    g = pl.program_id(0)
    index = lax.axis_index("seq")
    core = index % 2
    is_first = core == 0
    first = index * tok
    ends = ends_ref[...]
    doc, same = same_docs(ends, first, tok, taps.shape[0] - 1)
    prior = doc_at(ends, first - 1)
    final = doc_at(ends, first + tok - 1)

    def padded(ref, rim_ref, before_ref, lanes):
        top = pick(is_first, rim_ref[:, lanes].astype(F32), before_ref[:, lanes].astype(F32))
        return jnp.concatenate([top, ref[:, lanes].astype(F32)], axis=0)

    @pl.when(g == 0)
    def _():
        for j in range(bc_ref.shape[1] // 128):
            lanes = slice(j * 128, (j + 1) * 128)
            mixed = convolve(padded(bc_ref, rim_bc, before_bc, lanes), taps_bc[:, lanes], bias_bc[:, lanes], same)
            for k in range(128 // state):
                which = j * (128 // state) + k
                value = mixed.astype(F32)[:, k * state : (k + 1) * state].astype(BF16)
                if which < GROUPS:
                    b_all[which] = value
                else:
                    c_out[which - GROUPS] = value
        step, sums = log_sums(raw[...], step_bias[...], rate_log[...])
        ending_decay = jnp.exp(sums[tok - 1 :])
        passed = jnp.where((final == prior)[:, :heads], ending_decay, 0.0)
        rest = jnp.concatenate([ending_decay, passed, skip[...], jnp.zeros((5, heads), F32)], axis=0)
        whole = jnp.concatenate([jnp.exp(sums), jnp.exp(-sums) * step, rest], axis=0)
        compact[...] = jnp.concatenate([p.astype(F32) for p in split(whole, 3)], axis=1).astype(BF16)

    columns = x_ref.shape[1]
    wide = dot(compact[...], selector(heads, columns, width, g * (heads // GROUPS)))
    inward, outward = wide[:tok], wide[tok : 2 * tok]
    end_decay, passes, gains = (wide[2 * tok + k : 2 * tok + k + 1] for k in range(3))
    b_rows, c_rows = b_all[g], c_out[g]
    scores = dot(c_rows, b_rows, ((1,), (1,)))
    down, across = (lax.broadcasted_iota(jnp.int32, (tok, tok), k) for k in range(2))
    causal = (down >= across) & (doc[RIM:, :tok] == doc_of(ends, across + first))
    mask = jnp.where(causal, scores, 0.0)
    m_top, m_rest = split(mask, 2)
    here = doc[RIM:, :state] == final[:, :state]
    ending = jnp.where(here, b_rows.astype(F32), 0.0).astype(BF16)
    lhs = jnp.concatenate([m_top.astype(F32), m_rest.astype(F32)], axis=1).astype(BF16)
    entered = doc[RIM:] == prior
    for j in range(columns // 128):
        lanes = slice(j * 128, (j + 1) * 128)
        x = convolve(padded(x_ref, rim, before, lanes), taps[:, lanes], bias[:, lanes], same).astype(F32)
        scaled = x * outward[:, lanes]
        s_top, s_rest = split(scaled, 2)
        within = dot(lhs, jnp.concatenate([s_top, s_top], axis=0)) + dot(m_top, s_rest)
        local = dot(ending, s_top, ((0,), (0,))) + dot(ending, s_rest, ((0,), (0,)))
        opened = silu(gate[:, lanes].astype(F32))
        a_out[:, lanes] = (inward[:, lanes] * within + gains[:, lanes] * x) * opened
        b_out[:, lanes] = jnp.where(entered, inward[:, lanes] * opened, 0.0)
        s_out[:state, lanes] = (end_decay[:, lanes] * local).astype(BF16)
    s_out[state:] = two_rows(passes, (8, columns))


def place_of(far_core, far_row):
    index = lax.axis_index("seq")
    core, row = index % 2, (index // 2) % 2
    return PAIR * (1 - core if far_core else core) + (1 - row if far_row else row)


def finish_piece(width, group, arrived, a_ref, b_ref, c_ref, prior, gain, put):
    second = lax.axis_index("seq") % 2 == 1
    state_rows, columns = arrived.shape
    block = 256
    down, across = (lax.broadcasted_iota(jnp.int32, (block, block), k) for k in range(2))
    low = across - lax.rem(across, width)
    means = jnp.where((down >= low) & (down < low + width), 1.0 / width, 0.0).astype(BF16)
    c_rows = c_ref[group]
    for j in range(columns // block):
        lanes = slice(j * block, (j + 1) * block)
        at = pl.ds(pl.multiple_of(group * columns + j * block, block), block)
        state = arrived[:, lanes].astype(F32)
        before = prior[:, at].astype(F32)
        stepped = (before[state_rows : state_rows + 1] + before[state_rows + 1 : state_rows + 2]) * state + before[:state_rows]
        state = pick(second, stepped, state).astype(BF16)
        gated = a_ref[:, at] + b_ref[:, at] * dot(c_rows, state)
        top, rest = split(gated * gated, 2)
        mean = dot(top, means) + dot(rest, means)
        put(lanes, (gated * lax.rsqrt(mean + EPSILON) * gain[:, at]).astype(BF16))


def finish_near_kernel(width, a, b, c, prior, gain, x0, x2, out, ready, sems):
    columns, copies = x0.shape[1], []
    for k, arrived in enumerate((x0, x2)):
        group = place_of(k == 1, False)

        def put(lanes, value, k=k):
            ready[k, :, lanes] = value

        finish_piece(width, group, arrived, a, b, c, prior, gain, put)
        target = out.at[:, pl.ds(pl.multiple_of(group * columns, columns), columns)]
        copies.append(pltpu.make_async_copy(ready.at[k], target, sems.at[k]))
        copies[-1].start()
    for copy in copies:
        copy.wait()


def finish_back_kernel(width, a, b, c, prior, gain, x1, out):
    def put(lanes, value):
        out[:, lanes] = value

    finish_piece(width, place_of(False, True), x1, a, b, c, prior, gain, put)


def finish_far_kernel(width, a, b, c, prior, gain, x3, piece, begun, out, ready, sems):
    columns = x3.shape[1]

    def target(group):
        return out.at[:, pl.ds(pl.multiple_of(group * columns, columns), columns)]

    early = pltpu.make_async_copy(piece, target(place_of(False, True)), sems.at[0])
    early.start()

    def put(lanes, value):
        ready[:, lanes] = value

    group = place_of(True, True)
    finish_piece(width, group, x3, a, b, c, prior, gain, put)
    copy = pltpu.make_async_copy(ready, target(group), sems.at[1])
    copy.start()
    early.wait()
    copy.wait()


def swap(block, pairs):
    return lax.ppermute(block, "seq", [*pairs, *((b, a) for a, b in pairs)])


def on_device(mixer_in, gate_in, step_raw, step_bias, rate_log, conv_weight, conv_bias, skip_gain, norm_gain, doc_lengths):
    tok, channels = mixer_in.shape
    heads, inner = rate_log.shape[0], gate_in.shape[1]
    width = inner // heads
    state = (channels - inner) // (2 * GROUPS)
    devices = lax.axis_size("seq")
    planes = devices // GROUPS
    columns = inner // GROUPS
    taps_n = conv_weight.shape[0]
    longest = devices * tok // 2
    reach = -(-(longest - 1) // (GROUPS * tok))
    row = lambda a: a.reshape(1, -1)
    step_bias, rate_log, skip_gain, norm_gain, wide_bias = map(row, (step_bias, rate_log, skip_gain, norm_gain, conv_bias))
    cores = [(i, i + 1) for i in range(0, devices, 2)]
    rows = [(i, i + 2) for i in range(0, devices, 4) for i in (i, i + 1)]
    chips = [(i, i + 1) for i in range(1, devices - 1, 2)]

    def hbm(block):
        return pltpu.with_memory_space_constraint(block, pltpu.HBM)

    other = swap(mixer_in, cores)
    other_raw = swap(step_raw, cores)
    own, rim, raw, step_bias, rate_log, taps, bias, ends = pl.pallas_call(
        load_kernel,
        out_shape=(
            jax.ShapeDtypeStruct((tok, channels), BF16), jax.ShapeDtypeStruct((RIM, channels), BF16),
            jax.ShapeDtypeStruct((tok, heads), BF16), jax.ShapeDtypeStruct((1, heads), F32),
            jax.ShapeDtypeStruct((1, heads), F32), jax.ShapeDtypeStruct((taps_n, channels), F32),
            jax.ShapeDtypeStruct((channels,), F32), jax.ShapeDtypeStruct((doc_lengths.shape[0], 128), jnp.int32),
        ),
        in_specs=[HBM] * 7,
        out_specs=(VMEM,) * 8,
        scratch_shapes=[pltpu.SMEM(doc_lengths.shape, jnp.int32), pltpu.SemaphoreType.DMA((8,))],
        compiler_params=pltpu.CompilerParams(vmem_limit_bytes=4 << 20),
        name="load",
    )(*map(hbm, (doc_lengths, mixer_in, step_raw, step_bias, rate_log, conv_weight, conv_bias)))
    rim = swap(rim, chips)
    other_rim = swap(rim, cores)

    def params(mib):
        return pltpu.CompilerParams(vmem_limit_bytes=mib << 20)

    packed = jax.ShapeDtypeStruct((state + 8, columns), BF16)
    packed_wide = jax.ShapeDtypeStruct((state + 8, columns), F32)
    piece = jax.ShapeDtypeStruct((state, columns), BF16)
    dims = (heads, width, inner, tok)

    def states(keep, *operands):
        compact = () if keep else (jax.ShapeDtypeStruct((2 * tok + 16, heads), F32),)
        return pl.pallas_call(
            functools.partial(states_kernel, keep, dims, state),
            out_shape=(packed_wide if keep else packed, *compact),
            in_specs=[VMEM] * (3 + len(operands) + 2),
            out_specs=(VMEM,) * (1 + len(compact)),
            scratch_shapes=[pltpu.VMEM((2 * tok, columns), BF16)],
            compiler_params=params(8),
            name="states_kept" if keep else "states_sent",
        )(ends, own, other, *operands, taps, bias)

    sent, compact = states(False, raw, other_raw, step_bias, rate_log)
    got = swap(sent, rows)
    kept, = states(True, compact)
    corner = jax.ShapeDtypeStruct((2 * RIM, columns), BF16)
    rim_sent, rim_kept = pl.pallas_call(
        functools.partial(rim_kernel, dims),
        out_shape=(corner, corner),
        in_specs=[VMEM] * 8,
        out_specs=(VMEM, VMEM),
        compiler_params=params(4),
        name="rim_terms",
    )(ends, own, other, rim, other_rim, compact, taps, bias)
    rim_got = swap(rim_sent, rows)
    plane, far, base = pl.pallas_call(
        functools.partial(plane_kernel, state), out_shape=(packed, piece, packed_wide), in_specs=[VMEM] * 4, out_specs=(VMEM,) * 3,
        compiler_params=params(4), name="plane_total",
    )(kept, rim_kept, got, rim_got)
    parts = []
    for back in range(1, reach + 1):
        for parity in range(2):
            pairs = [
                (GROUPS * p + q, GROUPS * (p + back) + q)
                for p in range(planes - back) if p // back % 2 == parity
                for q in range(GROUPS)
            ]
            payload = far if back == reach else plane
            parts.append(swap(payload, pairs) if pairs else parts[-1])

    def whole(height, length):
        return pl.BlockSpec((height, length), lambda g: (0, 0))

    def by_group(height):
        return pl.BlockSpec((height, columns), lambda g: (0, g))

    rest = channels - inner
    bc = pl.BlockSpec((tok, rest), lambda g: (0, inner // rest))
    last = pl.BlockSpec((RIM, columns), lambda g: (tok // RIM - 1, g))
    last_bc = pl.BlockSpec((RIM, rest), lambda g: (tok // RIM - 1, inner // rest))
    a, b, c, own_state = pl.pallas_call(
        functools.partial(local_kernel, (heads, width, state, tok)),
        grid=(GROUPS,),
        out_shape=(
            jax.ShapeDtypeStruct((tok, inner), F32),
            jax.ShapeDtypeStruct((tok, inner), F32),
            jax.ShapeDtypeStruct((GROUPS, tok, state), BF16),
            jax.ShapeDtypeStruct((state + 8, inner), BF16),
        ),
        in_specs=[
            whole(*ends.shape), by_group(tok), bc, last, last_bc, by_group(RIM), pl.BlockSpec((RIM, rest), lambda g: (0, inner // rest)),
            by_group(tok), whole(tok, heads), whole(1, heads), whole(1, heads), by_group(taps_n), by_group(1),
            pl.BlockSpec((taps_n, rest), lambda g: (0, inner // rest)), pl.BlockSpec((1, rest), lambda g: (0, inner // rest)),
            whole(1, heads),
        ],
        out_specs=(by_group(tok), by_group(tok), pl.BlockSpec((GROUPS, tok, state), lambda g: (0, 0, 0)), by_group(state + 8)),
        scratch_shapes=[pltpu.VMEM((GROUPS, tok, state), BF16), pltpu.VMEM((2 * tok + 8, 3 * heads), BF16)],
        compiler_params=params(16),
        name="local_block",
        cost_estimate=pl.CostEstimate(flops=2 * 10**9, bytes_accessed=8 << 20, transcendentals=10**6),
    )(ends, own, own, other, other, rim, rim, gate_in, raw, step_bias, rate_log, taps, wide_bias,
      taps, wide_bias, skip_gain)
    prior = swap(own_state, cores)

    x0, mine = pl.pallas_call(
        functools.partial(arrive_kernel, reach, state), out_shape=(piece, piece), in_specs=[VMEM] * (1 + 2 * reach),
        out_specs=(VMEM, VMEM), compiler_params=params(4), name="arrive",
    )(base, *parts)
    x1 = swap(mine, rows)
    x2 = swap(x0, cores)
    x3 = swap(x1, cores)

    common = (a, b, c, prior, norm_gain)
    whole_out = jax.ShapeDtypeStruct((tok, inner), BF16)
    ready = [pltpu.VMEM((2, tok, columns), BF16), pltpu.SemaphoreType.DMA((2,))]
    out = pl.pallas_call(
        functools.partial(finish_near_kernel, width), out_shape=whole_out, in_specs=[VMEM] * 7, out_specs=HBM,
        scratch_shapes=ready, compiler_params=params(8), name="finish_near",
    )(*common, x0, x2)
    back_piece = pl.pallas_call(
        functools.partial(finish_back_kernel, width), out_shape=jax.ShapeDtypeStruct((tok, columns), BF16),
        in_specs=[VMEM] * 6, out_specs=VMEM, compiler_params=params(8), name="finish_back",
    )(*common, x1)
    return pl.pallas_call(
        functools.partial(finish_far_kernel, width), out_shape=whole_out, in_specs=[VMEM] * 7 + [HBM], out_specs=HBM,
        scratch_shapes=[pltpu.VMEM((tok, columns), BF16), pltpu.SemaphoreType.DMA((2,))],
        input_output_aliases={7: 0}, compiler_params=params(8), name="finish_far",
    )(*common, x3, back_piece, out)


def solution(mesh):
    split_rows = P(("groups", "seq"), None)
    return jax.shard_map(
        on_device,
        mesh=mesh,
        in_specs=(split_rows, split_rows, split_rows, P(), P(), P(), P(), P(), P(), P("groups")),
        out_specs=split_rows,
        check_vma=False,
    )
```

time: 55.5 us -> 48.2 us (0.87)
  Pallas kernels: 16.1 us -> 11.6 us
  local copies, waits for them, and re-layouts: 4.62 us -> 0.67 us
  waiting for transfers between devices: 17.4 us -> 18.4 us
    unnamed x20 -> x10, local copies, waits for them, and re-layouts: 4.61 us -> 0.66 us
    pallas_call x2, Pallas kernels: 4.81 us -> 2.18 us  [states(): pl.pallas_call(functools.partial(states_kernel, keep, dims, state), out_s...]
    pallas_call x1, Pallas kernels: 1.52 us -> 0.32 us  [on_device(): pl.pallas_call(functools.partial(rim_kernel, dims), out_shape=(corner, co...]
    ppermute x13, waiting for transfers between devices: 17.4 us -> 18.4 us  [swap(): return lax.ppermute(block, 'seq', [*pairs, *((b, a) for a, b in pairs)])]
  transfers between devices with their start and end apart: 13 -> 13, of which waited for: 5 -> 5; matrix products, arithmetic and copies ran while one was open for 0% -> 0% of each run, Pallas kernels for 19% -> 14%
where the time goes in v3:
time: 48.2 us; the launch traced here: 48.1 us
  waiting for transfers between devices  18.4 us (38%)
  starting transfers between devices  17.2 us (36%)
  Pallas kernels  11.6 us (24%)
  local copies, waits for them, and re-layouts  0.67 us (1%)
    ppermute x13, waiting for transfers between devices, swap(): return lax.ppermute(block, 'seq', [*pairs, *((b, a) for a, b in pairs)])  18.4 us
    ppermute x13, starting transfers between devices, swap(): return lax.ppermute(block, 'seq', [*pairs, *((b, a) for a, b in pairs)])  17.2 us
    pallas_call x1, Pallas kernels, on_device(): pl.pallas_call(functools.partial(local_kernel, (heads, width, state, tok)...  3.86 us
    pallas_call x2, Pallas kernels, states(): pl.pallas_call(functools.partial(states_kernel, keep, dims, state), out_s...  2.18 us
    pallas_call x1, Pallas kernels, on_device(): pl.pallas_call(functools.partial(finish_near_kernel, width), out_shape=wh...  1.69 us
    pallas_call x1, Pallas kernels, on_device(): pl.pallas_call(load_kernel, out_shape=(jax.ShapeDtypeStruct((tok, channel...  1.29 us
    pallas_call x1, Pallas kernels, on_device(): pl.pallas_call(functools.partial(finish_far_kernel, width), out_shape=who...  1.27 us
  transfers between devices with their start and end apart: 13, of which 5 were waited for; matrix products, arithmetic and copies ran while one was open for 0% of the time, Pallas kernels for 14%

profile of v3, /device:TPU:0, one launch (start us, length us, event | category | flops | bytes accessed | tf_op | source)
XLA Modules:
  0.0 48.1 jit_solution(5694534707155292924)
XLA Ops:
  0.0 0.5 %collective-permute-start = (bf16[64,4608]{1,0:T(8,128)(2,1)}, bf16[64,4608]{1,0:T(8,128)(2,1)S(1)}, u32[]{:S(2)}, u32[]{:S(2)}) collective-permute-start(bf16[64,4608]{1,0:T(8,128)(2,1)} %rows.1), channel_id=1, source_target_pairs={{0,1},{2,3},{4,5},{6,7},{8,9},{10,11},{12,13},{14,15},{1,0},{3,2},... | collective-permute-start | bytes 1769480 | tf_op jit(solution)/shard_map/ppermute | solution.py:396
  0.5 1.3 %load.1 = (bf16[64,4608]{1,0:T(8,128)(2,1)S(1)}, bf16[8,4608]{1,0:T(8,128)(2,1)S(1)}, bf16[64,64]{1,0:T(8,128)(2,1)S(1)}, f32[1,64]{1,0:T(1,128)S(1)}, f32[1,64]...) custom-call(s32[6]{0:T(128)} %lengths.1, bf16[64,4608]{1,0:T(8,128)(2,1)} %rows.1, ...), custom_call_target="tpu_custom_call" | custom-call | tf_op jit(solution)/shard_map/load/pallas_call | solution.py:421
  1.8 0.7 %collective-permute-start.1 = (bf16[8,4608]{1,0:T(8,128)(2,1)S(1)}, bf16[8,4608]{1,0:T(8,128)(2,1)S(1)}, u32[]{:S(2)}, u32[]{:S(2)}) collective-permute-start(bf16[8,4608]{1,0:T(8,128)(2,1)S(1)} %get-tuple-element.28), channel_id=1, source_target_pairs={{1,2},{3,4},{5,6},{7,8},{9,10},{11,12},{13,14},{2,1},{4,3},{6,5},{... | collective-permute-start | bytes 221192 | tf_op jit(solution)/shard_map/ppermute | solution.py:396
  2.5 0.6 %copy-done.2 = f32[64]{0:T(128)S(1)} copy-done((f32[64]{0:T(128)S(1)}, f32[64]{0:T(128)}, u32[]{:S(2)}) %copy-start.2) | copy-done | bytes 280
  3.2 3.9 %local_block.1 = (f32[64,4096]{1,0:T(8,128)S(1)}, f32[64,4096]{1,0:T(8,128)S(1)}, bf16[4,64,64]{2,1,0:T(8,128)(2,1)S(1)}, bf16[72,4096]{1,0:T(8,128)(2,1)S(1)}) custom-call(s32[6,128]{1,0:T(8,128)S(1)} %get-tuple-element.26.ends_ref.ends, bf16[64,4608]{1,0:T(8,128)(2,1)S(1)} %get-tuple-element.27.x_ref.bc_ref.own, ...), custom_call_target="tpu_custom_call" | custom-call | flops 2000000000 | bytes 8388608 | tf_op jit(solution)/shard_map/local_block/pallas_call | solution.py:496
  7.0 6.0 %collective-permute-start.2 = (bf16[72,4096]{1,0:T(8,128)(2,1)S(1)}, bf16[72,4096]{1,0:T(8,128)(2,1)S(1)}, u32[]{:S(2)}, u32[]{:S(2)}) collective-permute-start(bf16[72,4096]{1,0:T(8,128)(2,1)S(1)} %get-tuple-element.36), channel_id=1, source_target_pairs={{0,1},{2,3},{4,5},{6,7},{8,9},{10,11},{12,13},{14,15},{1,0},{3,2},... | collective-permute-start | bytes 1769480 | tf_op jit(solution)/shard_map/ppermute | solution.py:396
  13.1 1.6 %collective-permute-done.3.rest_1_ = bf16[64,64]{1,0:T(8,128)(2,1)S(1)} collective-permute-done((bf16[64,64]{1,0:T(8,128)(2,1)S(1)}, bf16[64,64]{1,0:T(8,128)(2,1)S(1)}, u32[]{:S(2)}, u32[]{:S(2)}) %collective-permute-start.3) | collective-permute-done | bytes 8224 | tf_op jit(solution)/shard_map/ppermute | solution.py:396
  14.7 1.2 %states_sent.1 = (bf16[72,1024]{1,0:T(8,128)(2,1)S(1)}, f32[144,64]{1,0:T(8,128)S(1)}) custom-call(s32[6,128]{1,0:T(8,128)S(1)} %get-tuple-element.26.ends_ref.ends, bf16[64,4608]{1,0:T(8,128)(2,1)S(1)} %get-tuple-element.27.x_ref.bc_ref.own, bf16[64,4608]{1,0:T(8,128)(2,1)S(1)} %collective-permute-done.before.before_bc.other, ...), custom_call_target="tpu_custom_call" | custom-call | tf_op jit(solution)/shard_map/states_sent/pallas_call | solution.py:448
  15.8 3.0 %collective-permute-start.5 = (bf16[72,1024]{1,0:T(8,128)(2,1)S(1)}, bf16[72,1024]{1,0:T(8,128)(2,1)S(1)}, u32[]{:S(2)}, u32[]{:S(2)}) collective-permute-start(bf16[72,1024]{1,0:T(8,128)(2,1)S(1)} %get-tuple-element.40), channel_id=1, source_target_pairs={{0,2},{1,3},{4,6},{5,7},{8,10},{9,11},{12,14},{13,15},{2,0},{3,1},... | collective-permute-start | bytes 442376 | tf_op jit(solution)/shard_map/ppermute | solution.py:396
  19.0 1.2 %collective-permute-done.4.rim_other = bf16[8,4608]{1,0:T(8,128)(2,1)S(1)} collective-permute-done((bf16[8,4608]{1,0:T(8,128)(2,1)S(1)}, bf16[8,4608]{1,0:T(8,128)(2,1)S(1)}, u32[]{:S(2)}, u32[]{:S(2)}) %collective-permute-start.4) | collective-permute-done | bytes 73760 | tf_op jit(solution)/shard_map/ppermute | solution.py:396
  20.1 0.3 rim_terms.1
  20.6 1.0 %states_kept.1.own = f32[72,1024]{1,0:T(8,128)S(1)} custom-call(s32[6,128]{1,0:T(8,128)S(1)} %get-tuple-element.26.ends_ref.ends, bf16[64,4608]{1,0:T(8,128)(2,1)S(1)} %get-tuple-element.27.x_ref.bc_ref.own, bf16[64,4608]{1,0:T(8,128)(2,1)S(1)} %collective-permute-done.before.before_bc.other, f32[144,64]{1,0:T(8,128)S(1)} %get-tuple-element.38.rest_0_.compact, ...), custom_call_target="tpu_custom_call" | custom-call | tf_op jit(solution)/shard_map/states_kept/pallas_call | solution.py:448
  21.6 2.8 %collective-permute-done.6.got_rim = bf16[16,1024]{1,0:T(8,128)(2,1)S(1)} collective-permute-done((bf16[16,1024]{1,0:T(8,128)(2,1)S(1)}, bf16[16,1024]{1,0:T(8,128)(2,1)S(1)}, u32[]{:S(2)}, u32[]{:S(2)}) %collective-permute-start.6) | collective-permute-done | bytes 32800 | tf_op jit(solution)/shard_map/ppermute | solution.py:396
  24.4 0.3 plane_total.1
  24.7 1.6 %collective-permute-start.7 = (bf16[72,1024]{1,0:T(8,128)(2,1)S(1)}, bf16[72,1024]{1,0:T(8,128)(2,1)S(1)}, u32[]{:S(2)}, u32[]{:S(2)}) collective-permute-start(bf16[72,1024]{1,0:T(8,128)(2,1)S(1)} %get-tuple-element.43), channel_id=1, source_target_pairs={{0,4},{1,5},{2,6},{3,7},{8,12},{9,13},{10,14},{11,15},{4,0},{5,1},... | collective-permute-start | bytes 442376 | tf_op jit(solution)/shard_map/ppermute | solution.py:396
  26.4 0.7 %collective-permute-start.8 = (bf16[72,1024]{1,0:T(8,128)(2,1)S(1)}, bf16[72,1024]{1,0:T(8,128)(2,1)S(1)}, u32[]{:S(2)}, u32[]{:S(2)}) collective-permute-start(bf16[72,1024]{1,0:T(8,128)(2,1)S(1)} %get-tuple-element.43), channel_id=1, source_target_pairs={{4,8},{5,9},{6,10},{7,11},{8,4},{9,5},{10,6},{11,7},{20,24},{21,25... | collective-permute-start | bytes 442376 | tf_op jit(solution)/shard_map/ppermute | solution.py:396
  27.0 3.6 %collective-permute-start.9 = (bf16[64,1024]{1,0:T(8,128)(2,1)S(1)}, bf16[64,1024]{1,0:T(8,128)(2,1)S(1)}, u32[]{:S(2)}, u32[]{:S(2)}) collective-permute-start(bf16[64,1024]{1,0:T(8,128)(2,1)S(1)} %get-tuple-element.44), channel_id=1, source_target_pairs={{0,8},{1,9},{2,10},{3,11},{4,12},{5,13},{6,14},{7,15},{8,0},{9,1},... | collective-permute-start | bytes 393224 | tf_op jit(solution)/shard_map/ppermute | solution.py:396
  30.6 8.7 %collective-permute-done.9.rest_2_.rest_3_ = bf16[64,1024]{1,0:T(8,128)(2,1)S(1)} collective-permute-done((bf16[64,1024]{1,0:T(8,128)(2,1)S(1)}, bf16[64,1024]{1,0:T(8,128)(2,1)S(1)}, u32[]{:S(2)}, u32[]{:S(2)}) %collective-permute-start.9) | collective-permute-done | bytes 131104 | tf_op jit(solution)/shard_map/ppermute | solution.py:396
  39.2 0.2 arrive.1
  39.4 0.8 %collective-permute-start.10 = (bf16[64,1024]{1,0:T(8,128)(2,1)S(1)}, bf16[64,1024]{1,0:T(8,128)(2,1)S(1)}, u32[]{:S(2)}, u32[]{:S(2)}) collective-permute-start(bf16[64,1024]{1,0:T(8,128)(2,1)S(1)} %get-tuple-element.45), channel_id=1, source_target_pairs={{0,2},{1,3},{4,6},{5,7},{8,10},{9,11},{12,14},{13,15},{2,0},{3,1},... | collective-permute-start | bytes 393224 | tf_op jit(solution)/shard_map/ppermute | solution.py:396
  40.3 4.2 %collective-permute-done.10.x1 = bf16[64,1024]{1,0:T(8,128)(2,1)S(1)} collective-permute-done((bf16[64,1024]{1,0:T(8,128)(2,1)S(1)}, bf16[64,1024]{1,0:T(8,128)(2,1)S(1)}, u32[]{:S(2)}, u32[]{:S(2)}) %collective-permute-start.10) | collective-permute-done | bytes 131104 | tf_op jit(solution)/shard_map/ppermute | solution.py:396
  44.5 0.6 %finish_back.1.piece = bf16[64,1024]{1,0:T(8,128)(2,1)S(1)} custom-call(f32[64,4096]{1,0:T(8,128)S(1)} %get-tuple-element.33.a, f32[64,4096]{1,0:T(8,128)S(1)} %get-tuple-element.34.b, bf16[4,64,64]{2,1,0:T(8,128)(2,1)S(1)} %get-tuple-element.35.c, bf16[72,4096]{1,0:T(8,128)(2,1)S(1)} %collective-permute-done.2.prior, f32[1,4096]{1,0:T(1,128)S(1)} %bitcast.4, ...), custom_call_target="tpu_custom_call" | custom-call | tf_op jit(solution)/shard_map/finish_back/pallas_call | solution.py:535
  45.1 1.7 %finish_near.1.begun = bf16[64,4096]{1,0:T(8,128)(2,1)} custom-call(f32[64,4096]{1,0:T(8,128)S(1)} %get-tuple-element.33.a, f32[64,4096]{1,0:T(8,128)S(1)} %get-tuple-element.34.b, bf16[4,64,64]{2,1,0:T(8,128)(2,1)S(1)} %get-tuple-element.35.c, bf16[72,4096]{1,0:T(8,128)(2,1)S(1)} %collective-permute-done.2.prior, f32[1,4096]{1,0:T(1,128)S(1)} %bitcast.5, ...), custom_call_target="tpu_custom_call" | custom-call | tf_op jit(solution)/shard_map/finish_near/pallas_call | solution.py:531
  46.8 1.3 %finish_far.1 = bf16[64,4096]{1,0:T(8,128)(2,1)} custom-call(f32[64,4096]{1,0:T(8,128)S(1)} %get-tuple-element.33.a, f32[64,4096]{1,0:T(8,128)S(1)} %get-tuple-element.34.b, bf16[4,64,64]{2,1,0:T(8,128)(2,1)S(1)} %get-tuple-element.35.c, bf16[72,4096]{1,0:T(8,128)(2,1)S(1)} %collective-permute-done.2.prior, ...), custom_call_target="tpu_custom_call", output_to_operand_aliasing={{}: (7, {})} | custom-call | tf_op jit(solution)/shard_map/finish_far/pallas_call | solution.py:539
  (23 shorter events, 0.4 us)
Async XLA Ops:
  0.0 2.5 %copy-start.1 = (bf16[64,4096]{1,0:T(8,128)(2,1)S(1)}, bf16[64,4096]{1,0:T(8,128)(2,1)}, u32[]{:S(2)}) copy-start(bf16[64,4096]{1,0:T(8,128)(2,1)} %gate.1) | copy-start | bytes 1572868
  0.0 2.5 %collective-permute-start = (bf16[64,4608]{1,0:T(8,128)(2,1)}, bf16[64,4608]{1,0:T(8,128)(2,1)S(1)}, u32[]{:S(2)}, u32[]{:S(2)}) collective-permute-start(bf16[64,4608]{1,0:T(8,128)(2,1)} %rows.1), channel_id=1, source_target_pairs={{0,1},{2,3},{4,5},{6,7},{8,9},{10,11},{12,13},{14,15},{1,0},{3,2},... | collective-permute-start | bytes 1769480 | tf_op jit(solution)/shard_map/ppermute | solution.py:396
  0.5 2.0 %copy-start.3 = (f32[4608]{0:T(1024)S(1)}, f32[4608]{0:T(1024)}, u32[]{:S(2)}) copy-start(f32[4608]{0:T(1024)} %bias.1) | copy-start | bytes 55300
  1.8 0.7 %collective-permute-start.1 = (bf16[8,4608]{1,0:T(8,128)(2,1)S(1)}, bf16[8,4608]{1,0:T(8,128)(2,1)S(1)}, u32[]{:S(2)}, u32[]{:S(2)}) collective-permute-start(bf16[8,4608]{1,0:T(8,128)(2,1)S(1)} %get-tuple-element.28), channel_id=1, source_target_pairs={{1,2},{3,4},{5,6},{7,8},{9,10},{11,12},{13,14},{2,1},{4,3},{6,5},{... | collective-permute-start | bytes 221192 | tf_op jit(solution)/shard_map/ppermute | solution.py:396
  2.5 0.7 %copy-start.2 = (f32[64]{0:T(128)S(1)}, f32[64]{0:T(128)}, u32[]{:S(2)}) copy-start(f32[64]{0:T(128)} %param.17) | copy-start | bytes 772
  3.2 9.8 %copy-start.4 = (bf16[64,64]{1,0:T(8,128)(2,1)S(1)}, bf16[64,64]{1,0:T(8,128)(2,1)}, u32[]{:S(2)}) copy-start(bf16[64,64]{1,0:T(8,128)(2,1)} %raw.1) | copy-start | bytes 24580
  7.0 37.4 %collective-permute-start.2 = (bf16[72,4096]{1,0:T(8,128)(2,1)S(1)}, bf16[72,4096]{1,0:T(8,128)(2,1)S(1)}, u32[]{:S(2)}, u32[]{:S(2)}) collective-permute-start(bf16[72,4096]{1,0:T(8,128)(2,1)S(1)} %get-tuple-element.36), channel_id=1, source_target_pairs={{0,1},{2,3},{4,5},{6,7},{8,9},{10,11},{12,13},{14,15},{1,0},{3,2},... | collective-permute-start | bytes 1769480 | tf_op jit(solution)/shard_map/ppermute | solution.py:396
  13.0 1.7 %collective-permute-start.3 = (bf16[64,64]{1,0:T(8,128)(2,1)S(1)}, bf16[64,64]{1,0:T(8,128)(2,1)S(1)}, u32[]{:S(2)}, u32[]{:S(2)}) collective-permute-start(bf16[64,64]{1,0:T(8,128)(2,1)S(1)} %copy-done.4), channel_id=1, source_target_pairs={{0,1},{2,3},{4,5},{6,7},{8,9},{10,11},{12,13},{14,15},{1,0},{3,2},... | collective-permute-start | bytes 24584 | tf_op jit(solution)/shard_map/ppermute | solution.py:396
  15.8 8.6 %collective-permute-start.5 = (bf16[72,1024]{1,0:T(8,128)(2,1)S(1)}, bf16[72,1024]{1,0:T(8,128)(2,1)S(1)}, u32[]{:S(2)}, u32[]{:S(2)}) collective-permute-start(bf16[72,1024]{1,0:T(8,128)(2,1)S(1)} %get-tuple-element.40), channel_id=1, source_target_pairs={{0,2},{1,3},{4,6},{5,7},{8,10},{9,11},{12,14},{13,15},{2,0},{3,1},... | collective-permute-start | bytes 442376 | tf_op jit(solution)/shard_map/ppermute | solution.py:396
  18.9 1.3 %collective-permute-start.4 = (bf16[8,4608]{1,0:T(8,128)(2,1)S(1)}, bf16[8,4608]{1,0:T(8,128)(2,1)S(1)}, u32[]{:S(2)}, u32[]{:S(2)}) collective-permute-start(bf16[8,4608]{1,0:T(8,128)(2,1)S(1)} %collective-permute-done.1.rim.rim_bc.rim_own), channel_id=1, source_target_pairs={{0,1},{2,3},{4,5},{6,7},{8,9},{10,11},{12,13},{14,15},{1,0},{3,2},... | collective-permute-start | bytes 221192 | tf_op jit(solution)/shard_map/ppermute | solution.py:396
  20.5 4.0 %collective-permute-start.6 = (bf16[16,1024]{1,0:T(8,128)(2,1)S(1)}, bf16[16,1024]{1,0:T(8,128)(2,1)S(1)}, u32[]{:S(2)}, u32[]{:S(2)}) collective-permute-start(bf16[16,1024]{1,0:T(8,128)(2,1)S(1)} %get-tuple-element.41), channel_id=1, source_target_pairs={{0,2},{1,3},{4,6},{5,7},{8,10},{9,11},{12,14},{13,15},{2,0},{3,1},... | collective-permute-start | bytes 98312 | tf_op jit(solution)/shard_map/ppermute | solution.py:396
  24.7 14.5 %collective-permute-start.7 = (bf16[72,1024]{1,0:T(8,128)(2,1)S(1)}, bf16[72,1024]{1,0:T(8,128)(2,1)S(1)}, u32[]{:S(2)}, u32[]{:S(2)}) collective-permute-start(bf16[72,1024]{1,0:T(8,128)(2,1)S(1)} %get-tuple-element.43), channel_id=1, source_target_pairs={{0,4},{1,5},{2,6},{3,7},{8,12},{9,13},{10,14},{11,15},{4,0},{5,1},... | collective-permute-start | bytes 442376 | tf_op jit(solution)/shard_map/ppermute | solution.py:396
  26.4 12.9 %collective-permute-start.8 = (bf16[72,1024]{1,0:T(8,128)(2,1)S(1)}, bf16[72,1024]{1,0:T(8,128)(2,1)S(1)}, u32[]{:S(2)}, u32[]{:S(2)}) collective-permute-start(bf16[72,1024]{1,0:T(8,128)(2,1)S(1)} %get-tuple-element.43), channel_id=1, source_target_pairs={{4,8},{5,9},{6,10},{7,11},{8,4},{9,5},{10,6},{11,7},{20,24},{21,25... | collective-permute-start | bytes 442376 | tf_op jit(solution)/shard_map/ppermute | solution.py:396
  27.0 12.2 %collective-permute-start.9 = (bf16[64,1024]{1,0:T(8,128)(2,1)S(1)}, bf16[64,1024]{1,0:T(8,128)(2,1)S(1)}, u32[]{:S(2)}, u32[]{:S(2)}) collective-permute-start(bf16[64,1024]{1,0:T(8,128)(2,1)S(1)} %get-tuple-element.44), channel_id=1, source_target_pairs={{0,8},{1,9},{2,10},{3,11},{4,12},{5,13},{6,14},{7,15},{8,0},{9,1},... | collective-permute-start | bytes 393224 | tf_op jit(solution)/shard_map/ppermute | solution.py:396
  39.2 5.2 %copy-start = (f32[4096]{0:T(1024)S(1)}, f32[4096]{0:T(1024)}, u32[]{:S(2)}) copy-start(f32[4096]{0:T(1024)} %param.18) | copy-start | bytes 49156
  39.4 5.0 %collective-permute-start.10 = (bf16[64,1024]{1,0:T(8,128)(2,1)S(1)}, bf16[64,1024]{1,0:T(8,128)(2,1)S(1)}, u32[]{:S(2)}, u32[]{:S(2)}) collective-permute-start(bf16[64,1024]{1,0:T(8,128)(2,1)S(1)} %get-tuple-element.45), channel_id=1, source_target_pairs={{0,2},{1,3},{4,6},{5,7},{8,10},{9,11},{12,14},{13,15},{2,0},{3,1},... | collective-permute-start | bytes 393224 | tf_op jit(solution)/shard_map/ppermute | solution.py:396
  40.3 4.8 %collective-permute-start.12 = (bf16[64,1024]{1,0:T(8,128)(2,1)S(1)}, bf16[64,1024]{1,0:T(8,128)(2,1)S(1)}, u32[]{:S(2)}, u32[]{:S(2)}) collective-permute-start(bf16[64,1024]{1,0:T(8,128)(2,1)S(1)} %get-tuple-element.46.x0), channel_id=1, source_target_pairs={{0,1},{2,3},{4,5},{6,7},{8,9},{10,11},{12,13},{14,15},{1,0},{3,2},... | collective-permute-start | bytes 393224 | tf_op jit(solution)/shard_map/ppermute | solution.py:396
  44.5 2.3 %collective-permute-start.11 = (bf16[64,1024]{1,0:T(8,128)(2,1)S(1)}, bf16[64,1024]{1,0:T(8,128)(2,1)S(1)}, u32[]{:S(2)}, u32[]{:S(2)}) collective-permute-start(bf16[64,1024]{1,0:T(8,128)(2,1)S(1)} %collective-permute-done.10.x1), channel_id=1, source_target_pairs={{0,1},{2,3},{4,5},{6,7},{8,9},{10,11},{12,13},{14,15},{1,0},{3,2},... | collective-permute-start | bytes 393224 | tf_op jit(solution)/shard_map/ppermute | solution.py:396

commit v4 on v3

--- a/solution.py
+++ b/solution.py
@@ -10,6 +10,7 @@
 GROUPS = 4
 PAIR = 2
 RIM = 8
+BLOCK = 256
 EPSILON = 1e-05
 F32 = jnp.float32
 BF16 = jnp.bfloat16
@@ -35,15 +36,16 @@
     return out
 
 
-def doc_of(ends, position):
-    found = jnp.zeros(position.shape, jnp.int32)
+def start_of(ends, position):
+    start = jnp.zeros(position.shape, jnp.int32)
     for i in range(ends.shape[0]):
-        found = found + jnp.where(position >= ends[i : i + 1, : position.shape[1]], 1, 0)
-    return jnp.where(position >= 0, found, -1)
-
-
-def doc_at(ends, place):
-    return doc_of(ends, jnp.broadcast_to(place, (1, ends.shape[1])))
+        end = ends[i : i + 1, : position.shape[1]]
+        start = jnp.where(position >= end, end, start)
+    return start
+
+
+def start_at(ends, place):
+    return start_of(ends, jnp.broadcast_to(place, (1, ends.shape[1])))
 
 
 def log_sums(raw, bias, rate_log):
@@ -71,19 +73,30 @@
     return dot(jnp.concatenate([p.astype(F32) for p in split(compact, 3)], axis=1).astype(BF16), chosen)
 
 
-def convolve(padded, taps, bias, same):
-    width = len(same)
-    total = bias + taps[width : width + 1] * padded
-    for back in range(1, width + 1):
-        moved = pltpu.roll(padded, back, 0)
-        total = total + taps[width - back : width - back + 1] * jnp.where(same[back - 1], moved, 0.0)
-    return silu(total[RIM:]).astype(BF16)
-
-
-def same_docs(ends, first, rows, width):
-    position = lax.broadcasted_iota(jnp.int32, (rows + RIM, 128), 0) + (first - RIM)
-    doc = doc_of(ends, position)
-    return doc, [pltpu.roll(doc, back, 0) == doc for back in range(1, width + 1)]
+def shifts(starts, first, places, count):
+    down = lax.broadcasted_iota(jnp.int32, places.shape, 0)
+    inside = jnp.where(places + first >= starts[:, : places.shape[1]], 1.0, 0.0)
+    back = down - places
+    return jnp.concatenate([jnp.where(back == k, inside, 0.0) for k in range(count)], axis=0).astype(BF16)
+
+
+def convolve(moves, rows, taps, bias):
+    count = taps.shape[0]
+    length = moves.shape[0] // count
+    moved = dot(moves, rows)
+    half = 0.5 * bias
+    for back in range(count):
+        half = half + (0.5 * taps[count - 1 - back : count - back]) * moved[back * length : (back + 1) * length]
+    return (half + half * jnp.tanh(half)).astype(BF16)
+
+
+def convolve_few(rows, reached, taps, bias):
+    count = taps.shape[0]
+    half = 0.5 * bias + (0.5 * taps[count - 1 :]) * rows[RIM:]
+    for back in range(1, count):
+        moved = pltpu.roll(rows, back, 0)[RIM:]
+        half = half + (0.5 * taps[count - 1 - back : count - back]) * jnp.where(reached[back - 1], moved, 0.0)
+    return (half + half * jnp.tanh(half)).astype(BF16)
 
 
 def pick(first, a, b):
@@ -125,21 +138,24 @@
     is_first = core == 0
     chip_first = (index - core) * tok
     ends = ends_ref[...]
-    doc, same = same_docs(ends, chip_first, 2 * tok, taps.shape[0] - 1)
+    first_at = pick(is_first, 0, tok)
+    column = lax.broadcasted_iota(jnp.int32, (2 * tok, 2 * tok), 1)
+    places = jnp.where(column < tok, column + first_at, column - first_at)
+    position = lax.broadcasted_iota(jnp.int32, (2 * tok, 128), 0) + chip_first
+    moves = shifts(start_of(ends, position), chip_first, places, taps.shape[0])
     if not keep:
-        prior, end_a, end_b = (
-            doc_at(ends, chip_first + place)[:, :heads] for place in (-1, tok - 1, 2 * tok - 1)
-        )
+        prior = chip_first - 1
+        start_a, start_b = (start_at(ends, chip_first + place)[:, :heads] for place in (tok - 1, 2 * tok - 1))
         one, two = (log_sums(raw[...], step_bias[...], rate_log[...]) for raw in (raw_own, raw_other))
         scales, lasts = [], []
-        for part, end in enumerate((end_a, end_b)):
+        for part, start in enumerate((start_a, start_b)):
             step, sums = (pick(is_first == (part == 0), a, b) for a, b in zip(one, two))
             last = sums[tok - 1 :]
-            here = doc[RIM + part * tok : RIM + (part + 1) * tok, :heads] == end
+            here = position[part * tok : (part + 1) * tok, :heads] >= start
             scales.append(jnp.where(here, jnp.exp(last - sums) * step, 0.0))
             lasts.append(jnp.exp(last))
-        pass_a = jnp.where(end_a == prior, lasts[0], 0.0)
-        pass_b = jnp.where(end_b == end_a, lasts[1], 0.0)
+        pass_a = jnp.where(start_a <= prior, lasts[0], 0.0)
+        pass_b = jnp.where(start_b <= prior + tok, lasts[1], 0.0)
         compact[:RIM] = jnp.zeros((RIM, heads), F32)
         compact[RIM:tok] = scales[0][RIM:]
         compact[tok : 2 * tok] = scales[1]
@@ -148,19 +164,18 @@
         compact[2 * tok + 8 :] = scales[0][:RIM] * pass_b
     scale = widen(compact[: 2 * tok + 8], selector(heads, columns, width, group * (heads // GROUPS)))
 
-    def padded(lanes_at):
-        a, b = own[:, lanes_at].astype(F32), other[:, lanes_at].astype(F32)
-        return jnp.concatenate([jnp.zeros((RIM, a.shape[1]), F32), pick(is_first, a, b), pick(is_first, b, a)], axis=0)
-
-    here_b = pl.ds(at_b, 128)
-    b_pair = convolve(padded(here_b), taps[:, here_b], bias[here_b].reshape(1, 128), same).astype(F32)
+
+    def mixed(lanes_at, size):
+        rows = jnp.concatenate([own[:, lanes_at], other[:, lanes_at]], axis=0)
+        return convolve(moves, rows, taps[:, lanes_at], bias[lanes_at].reshape(1, size)).astype(F32)
+
+    b_pair = mixed(pl.ds(at_b, 128), 128)
     half = b_pair.shape[1] // 2
     b_rows = pick(wanted == 0, b_pair[:, :half], b_pair[:, half:]).astype(BF16)
-    for j in range(columns // 128):
-        lanes = slice(j * 128, (j + 1) * 128)
-        lanes_at = pl.ds(pl.multiple_of(at + j * 128, 128), 128)
-        x = convolve(padded(lanes_at), taps[:, lanes_at], bias[lanes_at].reshape(1, 128), same)
-        weighted[:, lanes] = (x.astype(F32) * scale[: 2 * tok, lanes]).astype(BF16)
+    for j in range(columns // BLOCK):
+        lanes = slice(j * BLOCK, (j + 1) * BLOCK)
+        x = mixed(pl.ds(pl.multiple_of(at + j * BLOCK, BLOCK), BLOCK), BLOCK)
+        weighted[:, lanes] = (x * scale[: 2 * tok, lanes]).astype(BF16)
     state_a = dot(b_rows[:tok], weighted[:tok], ((0,), (0,)))
     state_b = dot(b_rows[tok:], weighted[tok:], ((0,), (0,)))
     passes = scale[2 * tok + 1 : 2 * tok + 2]
@@ -181,14 +196,16 @@
     at_b = pl.multiple_of(inner + core * 128, 128)
     is_first = core == 0
     chip_first = (index - core) * tok
-    _, same = same_docs(ends[...], chip_first, RIM, taps.shape[0] - 1)
+    position = lax.broadcasted_iota(jnp.int32, (RIM, 128), 0) + chip_first
+    starts = start_of(ends[...], position)
+    reached = [position - back >= starts for back in range(1, taps.shape[0])]
     scale = widen(compact[2 * tok + 8 :], selector(heads, PAIR * columns, width, core * (heads // PAIR)))
 
     def mixed(lanes_at):
         rim = pick(is_first, rim_own[:, lanes_at].astype(F32), rim_other[:, lanes_at].astype(F32))
         top = pick(is_first, own[:RIM, lanes_at].astype(F32), other[:RIM, lanes_at].astype(F32))
         rows = jnp.concatenate([rim, top], axis=0)
-        return convolve(rows, taps[:, lanes_at], bias[lanes_at].reshape(1, 128), same).astype(F32)
+        return convolve_few(rows, reached, taps[:, lanes_at], bias[lanes_at].reshape(1, 128)).astype(F32)
 
     b_pair = mixed(pl.ds(at_b, 128))
     half = b_pair.shape[1] // 2
@@ -258,68 +275,68 @@
     out_sent[...] = pick(upper, state, later).astype(BF16)
 
 
-def local_kernel(dims, ends_ref, x_ref, bc_ref, before, before_bc, rim, rim_bc, gate, raw, step_bias, rate_log, taps, bias,
-                 taps_bc, bias_bc, skip, a_out, b_out, c_out, s_out, b_all, compact):
+def local_kernel(dims, ends_ref, own, other, rim, gate_hbm, raw, step_bias, rate_log, taps, bias, skip,
+                 a_out, b_out, c_out, s_out, gate, sem):
     heads, width, state, tok = dims
-    g = pl.program_id(0)
+    copy = pltpu.make_async_copy(gate_hbm, gate, sem)
+    copy.start()
     index = lax.axis_index("seq")
-    core = index % 2
-    is_first = core == 0
+    is_first = index % 2 == 0
     first = index * tok
+    inner, per = gate.shape[1], heads // GROUPS
+    columns = inner // GROUPS
     ends = ends_ref[...]
-    doc, same = same_docs(ends, first, tok, taps.shape[0] - 1)
-    prior = doc_at(ends, first - 1)
-    final = doc_at(ends, first + tok - 1)
-
-    def padded(ref, rim_ref, before_ref, lanes):
-        top = pick(is_first, rim_ref[:, lanes].astype(F32), before_ref[:, lanes].astype(F32))
-        return jnp.concatenate([top, ref[:, lanes].astype(F32)], axis=0)
-
-    @pl.when(g == 0)
-    def _():
-        for j in range(bc_ref.shape[1] // 128):
-            lanes = slice(j * 128, (j + 1) * 128)
-            mixed = convolve(padded(bc_ref, rim_bc, before_bc, lanes), taps_bc[:, lanes], bias_bc[:, lanes], same)
-            for k in range(128 // state):
-                which = j * (128 // state) + k
-                value = mixed.astype(F32)[:, k * state : (k + 1) * state].astype(BF16)
-                if which < GROUPS:
-                    b_all[which] = value
-                else:
-                    c_out[which - GROUPS] = value
-        step, sums = log_sums(raw[...], step_bias[...], rate_log[...])
-        ending_decay = jnp.exp(sums[tok - 1 :])
-        passed = jnp.where((final == prior)[:, :heads], ending_decay, 0.0)
-        rest = jnp.concatenate([ending_decay, passed, skip[...], jnp.zeros((5, heads), F32)], axis=0)
-        whole = jnp.concatenate([jnp.exp(sums), jnp.exp(-sums) * step, rest], axis=0)
-        compact[...] = jnp.concatenate([p.astype(F32) for p in split(whole, 3)], axis=1).astype(BF16)
-
-    columns = x_ref.shape[1]
-    wide = dot(compact[...], selector(heads, columns, width, g * (heads // GROUPS)))
-    inward, outward = wide[:tok], wide[tok : 2 * tok]
-    end_decay, passes, gains = (wide[2 * tok + k : 2 * tok + k + 1] for k in range(3))
-    b_rows, c_rows = b_all[g], c_out[g]
-    scores = dot(c_rows, b_rows, ((1,), (1,)))
+    position = lax.broadcasted_iota(jnp.int32, (tok, 128), 0) + first
+    starts = start_of(ends, position)
+    final = start_at(ends, first + tok - 1)
+    column = lax.broadcasted_iota(jnp.int32, (tok, tok + 2 * RIM), 1)
+    places = jnp.where(column < tok, column, jnp.where(column < tok + RIM, column - tok - RIM, tok))
+    moves = shifts(starts, first, places, taps.shape[0])
+
+    def mixed(lanes):
+        top = pick(is_first, rim[:, lanes].astype(F32), other[tok - RIM :, lanes].astype(F32))
+        extra = jnp.concatenate([top, jnp.zeros_like(top)], axis=0).astype(BF16)
+        rows = jnp.concatenate([own[:, lanes], extra], axis=0)
+        return convolve(moves, rows, taps[:, lanes], bias[lanes].reshape(1, lanes.stop - lanes.start)).astype(F32)
+
+    b_all, c_all = [], []
+    for j in range(2 * GROUPS * state // BLOCK):
+        pieces = mixed(slice(inner + j * BLOCK, inner + (j + 1) * BLOCK))
+        for k in range(BLOCK // state):
+            (b_all if len(b_all) < GROUPS else c_all).append(pieces[:, k * state : (k + 1) * state].astype(BF16))
+    step, sums = log_sums(raw[...], step_bias[...], rate_log[...])
+    ending_decay = jnp.exp(sums[tok - 1 :])
+    passed = jnp.where(final[:, :heads] < first, ending_decay, 0.0)
+    rest = jnp.concatenate([ending_decay, passed, skip[...], jnp.zeros((5, heads), F32)], axis=0)
+    whole = jnp.concatenate([jnp.exp(sums), jnp.exp(-sums) * step, rest], axis=0)
+    chosen = selector(per, columns, width, 0)
     down, across = (lax.broadcasted_iota(jnp.int32, (tok, tok), k) for k in range(2))
-    causal = (down >= across) & (doc[RIM:, :tok] == doc_of(ends, across + first))
-    mask = jnp.where(causal, scores, 0.0)
-    m_top, m_rest = split(mask, 2)
-    here = doc[RIM:, :state] == final[:, :state]
-    ending = jnp.where(here, b_rows.astype(F32), 0.0).astype(BF16)
-    lhs = jnp.concatenate([m_top.astype(F32), m_rest.astype(F32)], axis=1).astype(BF16)
-    entered = doc[RIM:] == prior
-    for j in range(columns // 128):
-        lanes = slice(j * 128, (j + 1) * 128)
-        x = convolve(padded(x_ref, rim, before, lanes), taps[:, lanes], bias[:, lanes], same).astype(F32)
-        scaled = x * outward[:, lanes]
-        s_top, s_rest = split(scaled, 2)
-        within = dot(lhs, jnp.concatenate([s_top, s_top], axis=0)) + dot(m_top, s_rest)
-        local = dot(ending, s_top, ((0,), (0,))) + dot(ending, s_rest, ((0,), (0,)))
-        opened = silu(gate[:, lanes].astype(F32))
-        a_out[:, lanes] = (inward[:, lanes] * within + gains[:, lanes] * x) * opened
-        b_out[:, lanes] = jnp.where(entered, inward[:, lanes] * opened, 0.0)
-        s_out[:state, lanes] = (end_decay[:, lanes] * local).astype(BF16)
-    s_out[state:] = two_rows(passes, (8, columns))
+    causal = (down >= across) & (across + first >= starts[:, :tok])
+    here = position[:, :state] >= final[:, :state]
+    entered = jnp.concatenate([starts] * (BLOCK // 128), axis=1) < first
+    copy.wait()
+    for g in range(GROUPS):
+        wide = widen(whole[:, g * per : (g + 1) * per], chosen)
+        b_rows, c_rows = b_all[g], c_all[g]
+        c_out[g] = c_rows
+        mask = jnp.where(causal, dot(c_rows, b_rows, ((1,), (1,))), 0.0)
+        m_top, m_rest = split(mask, 2)
+        lhs = jnp.concatenate([m_top.astype(F32), m_rest.astype(F32)], axis=1).astype(BF16)
+        ending = jnp.where(here, b_rows.astype(F32), 0.0).astype(BF16)
+        for j in range(columns // BLOCK):
+            part = slice(j * BLOCK, (j + 1) * BLOCK)
+            lanes = slice(g * columns + j * BLOCK, g * columns + (j + 1) * BLOCK)
+            inward, outward = wide[:tok, part], wide[tok : 2 * tok, part]
+            end_decay, gain = wide[2 * tok : 2 * tok + 1, part], wide[2 * tok + 2 : 2 * tok + 3, part]
+            x = mixed(lanes)
+            s_top, s_rest = split(x * outward, 2)
+            within = dot(lhs, jnp.concatenate([s_top, s_top], axis=0)) + dot(m_top, s_rest)
+            local = dot(ending, s_top, ((0,), (0,))) + dot(ending, s_rest, ((0,), (0,)))
+            opened = silu(gate[:, lanes].astype(F32))
+            a_out[:, lanes] = (inward * within + gain * x) * opened
+            b_out[:, lanes] = jnp.where(entered, inward * opened, 0.0)
+            s_out[:state, lanes] = (end_decay * local).astype(BF16)
+        s_out[state:, g * columns : (g + 1) * columns] = two_rows(wide[2 * tok + 1 : 2 * tok + 2], (8, columns))
 
 
 def place_of(far_core, far_row):
@@ -331,7 +348,7 @@
 def finish_piece(width, group, arrived, a_ref, b_ref, c_ref, prior, gain, put):
     second = lax.axis_index("seq") % 2 == 1
     state_rows, columns = arrived.shape
-    block = 256
+    block = BLOCK
     down, across = (lax.broadcasted_iota(jnp.int32, (block, block), k) for k in range(2))
     low = across - lax.rem(across, width)
     means = jnp.where((down >= low) & (down < low + width), 1.0 / width, 0.0).astype(BF16)
@@ -344,8 +361,7 @@
         stepped = (before[state_rows : state_rows + 1] + before[state_rows + 1 : state_rows + 2]) * state + before[:state_rows]
         state = pick(second, stepped, state).astype(BF16)
         gated = a_ref[:, at] + b_ref[:, at] * dot(c_rows, state)
-        top, rest = split(gated * gated, 2)
-        mean = dot(top, means) + dot(rest, means)
+        mean = dot((gated * gated).astype(BF16), means)
         put(lanes, (gated * lax.rsqrt(mean + EPSILON) * gain[:, at]).astype(BF16))
 
 
@@ -408,7 +424,7 @@
     longest = devices * tok // 2
     reach = -(-(longest - 1) // (GROUPS * tok))
     row = lambda a: a.reshape(1, -1)
-    step_bias, rate_log, skip_gain, norm_gain, wide_bias = map(row, (step_bias, rate_log, skip_gain, norm_gain, conv_bias))
+    step_bias, rate_log, skip_gain, norm_gain = map(row, (step_bias, rate_log, skip_gain, norm_gain))
     cores = [(i, i + 1) for i in range(0, devices, 2)]
     rows = [(i, i + 2) for i in range(0, devices, 4) for i in (i, i + 1)]
     chips = [(i, i + 1) for i in range(1, devices - 1, 2)]
@@ -483,38 +499,20 @@
             payload = far if back == reach else plane
             parts.append(swap(payload, pairs) if pairs else parts[-1])
 
-    def whole(height, length):
-        return pl.BlockSpec((height, length), lambda g: (0, 0))
-
-    def by_group(height):
-        return pl.BlockSpec((height, columns), lambda g: (0, g))
-
-    rest = channels - inner
-    bc = pl.BlockSpec((tok, rest), lambda g: (0, inner // rest))
-    last = pl.BlockSpec((RIM, columns), lambda g: (tok // RIM - 1, g))
-    last_bc = pl.BlockSpec((RIM, rest), lambda g: (tok // RIM - 1, inner // rest))
     a, b, c, own_state = pl.pallas_call(
         functools.partial(local_kernel, (heads, width, state, tok)),
-        grid=(GROUPS,),
         out_shape=(
             jax.ShapeDtypeStruct((tok, inner), F32),
             jax.ShapeDtypeStruct((tok, inner), F32),
             jax.ShapeDtypeStruct((GROUPS, tok, state), BF16),
             jax.ShapeDtypeStruct((state + 8, inner), BF16),
         ),
-        in_specs=[
-            whole(*ends.shape), by_group(tok), bc, last, last_bc, by_group(RIM), pl.BlockSpec((RIM, rest), lambda g: (0, inner // rest)),
-            by_group(tok), whole(tok, heads), whole(1, heads), whole(1, heads), by_group(taps_n), by_group(1),
-            pl.BlockSpec((taps_n, rest), lambda g: (0, inner // rest)), pl.BlockSpec((1, rest), lambda g: (0, inner // rest)),
-            whole(1, heads),
-        ],
-        out_specs=(by_group(tok), by_group(tok), pl.BlockSpec((GROUPS, tok, state), lambda g: (0, 0, 0)), by_group(state + 8)),
-        scratch_shapes=[pltpu.VMEM((GROUPS, tok, state), BF16), pltpu.VMEM((2 * tok + 8, 3 * heads), BF16)],
+        in_specs=[VMEM] * 4 + [HBM] + [VMEM] * 6,
+        out_specs=(VMEM,) * 4,
+        scratch_shapes=[pltpu.VMEM((tok, inner), BF16), pltpu.SemaphoreType.DMA],
         compiler_params=params(16),
         name="local_block",
-        cost_estimate=pl.CostEstimate(flops=2 * 10**9, bytes_accessed=8 << 20, transcendentals=10**6),
-    )(ends, own, own, other, other, rim, rim, gate_in, raw, step_bias, rate_log, taps, wide_bias,
-      taps, wide_bias, skip_gain)
+    )(ends, own, other, rim, hbm(gate_in), raw, step_bias, rate_log, taps, bias, skip_gain)
     prior = swap(own_state, cores)
 
     x0, mine = pl.pallas_call(

time: 48.2 us -> 47.4 us (0.983)
  Pallas kernels: 11.6 us -> 10.5 us
  transfers between devices with their start and end apart: 13 -> 13, of which waited for: 5 -> 5; matrix products, arithmetic and copies ran while one was open for 0% -> 0% of each run, Pallas kernels for 14% -> 12%
where the time goes in v4:
time: 47.4 us; the launch traced here: 47.2 us
  waiting for transfers between devices  18.6 us (39%)
  starting transfers between devices  17.2 us (36%)
  Pallas kernels  10.5 us (22%)
  local copies, waits for them, and re-layouts  0.66 us (1%)
    ppermute x13, waiting for transfers between devices, swap(): return lax.ppermute(block, 'seq', [*pairs, *((b, a) for a, b in pairs)])  18.6 us
    ppermute x13, starting transfers between devices, swap(): return lax.ppermute(block, 'seq', [*pairs, *((b, a) for a, b in pairs)])  17.2 us
    pallas_call x1, Pallas kernels, on_device(): pl.pallas_call(functools.partial(local_kernel, (heads, width, state, tok)...  3.52 us
    pallas_call x2, Pallas kernels, states(): pl.pallas_call(functools.partial(states_kernel, keep, dims, state), out_s...  1.86 us
    pallas_call x1, Pallas kernels, on_device(): pl.pallas_call(functools.partial(finish_near_kernel, width), out_shape=wh...  1.48 us
    pallas_call x1, Pallas kernels, on_device(): pl.pallas_call(load_kernel, out_shape=(jax.ShapeDtypeStruct((tok, channel...  1.28 us
    pallas_call x1, Pallas kernels, on_device(): pl.pallas_call(functools.partial(finish_far_kernel, width), out_shape=who...  1.17 us
  transfers between devices with their start and end apart: 13, of which 5 were waited for; matrix products, arithmetic and copies ran while one was open for 0% of the time, Pallas kernels for 12%

profile of v4, /device:TPU:0, one launch (start us, length us, event | category | flops | bytes accessed | tf_op | source)
XLA Modules:
  0.0 47.2 jit_solution(17740710098209040974)
XLA Ops:
  0.0 0.5 %collective-permute-start = (bf16[64,4608]{1,0:T(8,128)(2,1)}, bf16[64,4608]{1,0:T(8,128)(2,1)S(1)}, u32[]{:S(2)}, u32[]{:S(2)}) collective-permute-start(bf16[64,4608]{1,0:T(8,128)(2,1)} %rows.1), channel_id=1, source_target_pairs={{0,1},{2,3},{4,5},{6,7},{8,9},{10,11},{12,13},{14,15},{1,0},{3,2},... | collective-permute-start | bytes 1769480 | tf_op jit(solution)/shard_map/ppermute | solution.py:412
  0.5 1.3 %load.1 = (bf16[64,4608]{1,0:T(8,128)(2,1)S(1)}, bf16[8,4608]{1,0:T(8,128)(2,1)S(1)}, bf16[64,64]{1,0:T(8,128)(2,1)S(1)}, f32[1,64]{1,0:T(1,128)S(1)}, f32[1,64]...) custom-call(s32[6]{0:T(128)} %lengths.1, bf16[64,4608]{1,0:T(8,128)(2,1)} %rows.1, ...), custom_call_target="tpu_custom_call" | custom-call | tf_op jit(solution)/shard_map/load/pallas_call | solution.py:437
  1.8 0.7 %collective-permute-start.1 = (bf16[8,4608]{1,0:T(8,128)(2,1)S(1)}, bf16[8,4608]{1,0:T(8,128)(2,1)S(1)}, u32[]{:S(2)}, u32[]{:S(2)}) collective-permute-start(bf16[8,4608]{1,0:T(8,128)(2,1)S(1)} %get-tuple-element.28), channel_id=1, source_target_pairs={{1,2},{3,4},{5,6},{7,8},{9,10},{11,12},{13,14},{2,1},{4,3},{6,5},{... | collective-permute-start | bytes 221192 | tf_op jit(solution)/shard_map/ppermute | solution.py:412
  2.5 0.6 %copy-done.1 = f32[64]{0:T(128)S(1)} copy-done((f32[64]{0:T(128)S(1)}, f32[64]{0:T(128)}, u32[]{:S(2)}) %copy-start.1) | copy-done | bytes 280
  3.1 3.5 %local_block.1 = (f32[64,4096]{1,0:T(8,128)S(1)}, f32[64,4096]{1,0:T(8,128)S(1)}, bf16[4,64,64]{2,1,0:T(8,128)(2,1)S(1)}, bf16[72,4096]{1,0:T(8,128)(2,1)S(1)}) custom-call(s32[6,128]{1,0:T(8,128)S(1)} %get-tuple-element.26.ends_ref.ends, bf16[64,4608]{1,0:T(8,128)(2,1)S(1)} %get-tuple-element.27.own, bf16[64,4608]{1,0:T(8,128)(2,1)S(1)} %collective-permute-done.other, ...), custom_call_target="tpu_custom_call" | custom-call | tf_op jit(solution)/shard_map/local_block/pallas_call | solution.py:502
  6.7 5.9 %collective-permute-start.2 = (bf16[72,4096]{1,0:T(8,128)(2,1)S(1)}, bf16[72,4096]{1,0:T(8,128)(2,1)S(1)}, u32[]{:S(2)}, u32[]{:S(2)}) collective-permute-start(bf16[72,4096]{1,0:T(8,128)(2,1)S(1)} %get-tuple-element.37), channel_id=1, source_target_pairs={{0,1},{2,3},{4,5},{6,7},{8,9},{10,11},{12,13},{14,15},{1,0},{3,2},... | collective-permute-start | bytes 1769480 | tf_op jit(solution)/shard_map/ppermute | solution.py:412
  12.7 1.6 %collective-permute-done.3.rest_1_ = bf16[64,64]{1,0:T(8,128)(2,1)S(1)} collective-permute-done((bf16[64,64]{1,0:T(8,128)(2,1)S(1)}, bf16[64,64]{1,0:T(8,128)(2,1)S(1)}, u32[]{:S(2)}, u32[]{:S(2)}) %collective-permute-start.3) | collective-permute-done | bytes 8224 | tf_op jit(solution)/shard_map/ppermute | solution.py:412
  14.3 1.0 %states_sent.1 = (bf16[72,1024]{1,0:T(8,128)(2,1)S(1)}, f32[144,64]{1,0:T(8,128)S(1)}) custom-call(s32[6,128]{1,0:T(8,128)S(1)} %get-tuple-element.26.ends_ref.ends, bf16[64,4608]{1,0:T(8,128)(2,1)S(1)} %get-tuple-element.27.own, bf16[64,4608]{1,0:T(8,128)(2,1)S(1)} %collective-permute-done.other, bf16[64,64]{1,0:T(8,128)(2,1)S(1)} %get-tuple-element.29.raw.rest_0_, ...), custom_call_target="tpu_custom_call" | custom-call | tf_op jit(solution)/shard_map/states_sent/pallas_call | solution.py:464
  15.3 3.1 %collective-permute-start.5 = (bf16[72,1024]{1,0:T(8,128)(2,1)S(1)}, bf16[72,1024]{1,0:T(8,128)(2,1)S(1)}, u32[]{:S(2)}, u32[]{:S(2)}) collective-permute-start(bf16[72,1024]{1,0:T(8,128)(2,1)S(1)} %get-tuple-element.40), channel_id=1, source_target_pairs={{0,2},{1,3},{4,6},{5,7},{8,10},{9,11},{12,14},{13,15},{2,0},{3,1},... | collective-permute-start | bytes 442376 | tf_op jit(solution)/shard_map/ppermute | solution.py:412
  18.5 1.2 %collective-permute-done.4.rim_other = bf16[8,4608]{1,0:T(8,128)(2,1)S(1)} collective-permute-done((bf16[8,4608]{1,0:T(8,128)(2,1)S(1)}, bf16[8,4608]{1,0:T(8,128)(2,1)S(1)}, u32[]{:S(2)}, u32[]{:S(2)}) %collective-permute-start.4) | collective-permute-done | bytes 73760 | tf_op jit(solution)/shard_map/ppermute | solution.py:412
  19.6 0.3 rim_terms.1
  20.1 0.8 %states_kept.1.own = f32[72,1024]{1,0:T(8,128)S(1)} custom-call(s32[6,128]{1,0:T(8,128)S(1)} %get-tuple-element.26.ends_ref.ends, bf16[64,4608]{1,0:T(8,128)(2,1)S(1)} %get-tuple-element.27.own, bf16[64,4608]{1,0:T(8,128)(2,1)S(1)} %collective-permute-done.other, f32[144,64]{1,0:T(8,128)S(1)} %get-tuple-element.38.rest_0_.compact, ...), custom_call_target="tpu_custom_call" | custom-call | tf_op jit(solution)/shard_map/states_kept/pallas_call | solution.py:464
  20.9 3.0 %collective-permute-done.6.got_rim = bf16[16,1024]{1,0:T(8,128)(2,1)S(1)} collective-permute-done((bf16[16,1024]{1,0:T(8,128)(2,1)S(1)}, bf16[16,1024]{1,0:T(8,128)(2,1)S(1)}, u32[]{:S(2)}, u32[]{:S(2)}) %collective-permute-start.6) | collective-permute-done | bytes 32800 | tf_op jit(solution)/shard_map/ppermute | solution.py:412
  23.9 0.3 plane_total.1
  24.2 1.6 %collective-permute-start.7 = (bf16[72,1024]{1,0:T(8,128)(2,1)S(1)}, bf16[72,1024]{1,0:T(8,128)(2,1)S(1)}, u32[]{:S(2)}, u32[]{:S(2)}) collective-permute-start(bf16[72,1024]{1,0:T(8,128)(2,1)S(1)} %get-tuple-element.43), channel_id=1, source_target_pairs={{0,4},{1,5},{2,6},{3,7},{8,12},{9,13},{10,14},{11,15},{4,0},{5,1},... | collective-permute-start | bytes 442376 | tf_op jit(solution)/shard_map/ppermute | solution.py:412
  25.8 0.7 %collective-permute-start.8 = (bf16[72,1024]{1,0:T(8,128)(2,1)S(1)}, bf16[72,1024]{1,0:T(8,128)(2,1)S(1)}, u32[]{:S(2)}, u32[]{:S(2)}) collective-permute-start(bf16[72,1024]{1,0:T(8,128)(2,1)S(1)} %get-tuple-element.43), channel_id=1, source_target_pairs={{4,8},{5,9},{6,10},{7,11},{8,4},{9,5},{10,6},{11,7},{20,24},{21,25... | collective-permute-start | bytes 442376 | tf_op jit(solution)/shard_map/ppermute | solution.py:412
  26.5 3.6 %collective-permute-start.9 = (bf16[64,1024]{1,0:T(8,128)(2,1)S(1)}, bf16[64,1024]{1,0:T(8,128)(2,1)S(1)}, u32[]{:S(2)}, u32[]{:S(2)}) collective-permute-start(bf16[64,1024]{1,0:T(8,128)(2,1)S(1)} %get-tuple-element.44), channel_id=1, source_target_pairs={{0,8},{1,9},{2,10},{3,11},{4,12},{5,13},{6,14},{7,15},{8,0},{9,1},... | collective-permute-start | bytes 393224 | tf_op jit(solution)/shard_map/ppermute | solution.py:412
  30.1 8.7 %collective-permute-done.9.rest_2_.rest_3_ = bf16[64,1024]{1,0:T(8,128)(2,1)S(1)} collective-permute-done((bf16[64,1024]{1,0:T(8,128)(2,1)S(1)}, bf16[64,1024]{1,0:T(8,128)(2,1)S(1)}, u32[]{:S(2)}, u32[]{:S(2)}) %collective-permute-start.9) | collective-permute-done | bytes 131104 | tf_op jit(solution)/shard_map/ppermute | solution.py:412
  38.8 0.2 arrive.1
  39.0 0.8 %collective-permute-start.10 = (bf16[64,1024]{1,0:T(8,128)(2,1)S(1)}, bf16[64,1024]{1,0:T(8,128)(2,1)S(1)}, u32[]{:S(2)}, u32[]{:S(2)}) collective-permute-start(bf16[64,1024]{1,0:T(8,128)(2,1)S(1)} %get-tuple-element.45), channel_id=1, source_target_pairs={{0,2},{1,3},{4,6},{5,7},{8,10},{9,11},{12,14},{13,15},{2,0},{3,1},... | collective-permute-start | bytes 393224 | tf_op jit(solution)/shard_map/ppermute | solution.py:412
  39.8 4.2 %collective-permute-done.10.x1 = bf16[64,1024]{1,0:T(8,128)(2,1)S(1)} collective-permute-done((bf16[64,1024]{1,0:T(8,128)(2,1)S(1)}, bf16[64,1024]{1,0:T(8,128)(2,1)S(1)}, u32[]{:S(2)}, u32[]{:S(2)}) %collective-permute-start.10) | collective-permute-done | bytes 131104 | tf_op jit(solution)/shard_map/ppermute | solution.py:412
  44.0 0.5 %finish_back.1.piece = bf16[64,1024]{1,0:T(8,128)(2,1)S(1)} custom-call(f32[64,4096]{1,0:T(8,128)S(1)} %get-tuple-element.34.a, f32[64,4096]{1,0:T(8,128)S(1)} %get-tuple-element.35.b, bf16[4,64,64]{2,1,0:T(8,128)(2,1)S(1)} %get-tuple-element.36.c, bf16[72,4096]{1,0:T(8,128)(2,1)S(1)} %collective-permute-done.2.prior, f32[1,4096]{1,0:T(1,128)S(1)} %bitcast.4, ...), custom_call_target="tpu_custom_call" | custom-call | tf_op jit(solution)/shard_map/finish_back/pallas_call | solution.py:533
  44.5 1.5 %finish_near.1.begun = bf16[64,4096]{1,0:T(8,128)(2,1)} custom-call(f32[64,4096]{1,0:T(8,128)S(1)} %get-tuple-element.34.a, f32[64,4096]{1,0:T(8,128)S(1)} %get-tuple-element.35.b, bf16[4,64,64]{2,1,0:T(8,128)(2,1)S(1)} %get-tuple-element.36.c, bf16[72,4096]{1,0:T(8,128)(2,1)S(1)} %collective-permute-done.2.prior, f32[1,4096]{1,0:T(1,128)S(1)} %bitcast.5, ...), custom_call_target="tpu_custom_call" | custom-call | tf_op jit(solution)/shard_map/finish_near/pallas_call | solution.py:529
  46.0 1.2 %finish_far.1 = bf16[64,4096]{1,0:T(8,128)(2,1)} custom-call(f32[64,4096]{1,0:T(8,128)S(1)} %get-tuple-element.34.a, f32[64,4096]{1,0:T(8,128)S(1)} %get-tuple-element.35.b, bf16[4,64,64]{2,1,0:T(8,128)(2,1)S(1)} %get-tuple-element.36.c, bf16[72,4096]{1,0:T(8,128)(2,1)S(1)} %collective-permute-done.2.prior, ...), custom_call_target="tpu_custom_call", output_to_operand_aliasing={{}: (7, {})} | custom-call | tf_op jit(solution)/shard_map/finish_far/pallas_call | solution.py:537
  (18 shorter events, 0.4 us)
Async XLA Ops:
  0.0 2.5 %collective-permute-start = (bf16[64,4608]{1,0:T(8,128)(2,1)}, bf16[64,4608]{1,0:T(8,128)(2,1)S(1)}, u32[]{:S(2)}, u32[]{:S(2)}) collective-permute-start(bf16[64,4608]{1,0:T(8,128)(2,1)} %rows.1), channel_id=1, source_target_pairs={{0,1},{2,3},{4,5},{6,7},{8,9},{10,11},{12,13},{14,15},{1,0},{3,2},... | collective-permute-start | bytes 1769480 | tf_op jit(solution)/shard_map/ppermute | solution.py:412
  1.8 0.7 %collective-permute-start.1 = (bf16[8,4608]{1,0:T(8,128)(2,1)S(1)}, bf16[8,4608]{1,0:T(8,128)(2,1)S(1)}, u32[]{:S(2)}, u32[]{:S(2)}) collective-permute-start(bf16[8,4608]{1,0:T(8,128)(2,1)S(1)} %get-tuple-element.28), channel_id=1, source_target_pairs={{1,2},{3,4},{5,6},{7,8},{9,10},{11,12},{13,14},{2,1},{4,3},{6,5},{... | collective-permute-start | bytes 221192 | tf_op jit(solution)/shard_map/ppermute | solution.py:412
  2.5 0.7 %copy-start.1 = (f32[64]{0:T(128)S(1)}, f32[64]{0:T(128)}, u32[]{:S(2)}) copy-start(f32[64]{0:T(128)} %param.17) | copy-start | bytes 772
  3.1 9.5 %copy-start.2 = (bf16[64,64]{1,0:T(8,128)(2,1)S(1)}, bf16[64,64]{1,0:T(8,128)(2,1)}, u32[]{:S(2)}) copy-start(bf16[64,64]{1,0:T(8,128)(2,1)} %raw.1) | copy-start | bytes 24580
  6.7 37.3 %collective-permute-start.2 = (bf16[72,4096]{1,0:T(8,128)(2,1)S(1)}, bf16[72,4096]{1,0:T(8,128)(2,1)S(1)}, u32[]{:S(2)}, u32[]{:S(2)}) collective-permute-start(bf16[72,4096]{1,0:T(8,128)(2,1)S(1)} %get-tuple-element.37), channel_id=1, source_target_pairs={{0,1},{2,3},{4,5},{6,7},{8,9},{10,11},{12,13},{14,15},{1,0},{3,2},... | collective-permute-start | bytes 1769480 | tf_op jit(solution)/shard_map/ppermute | solution.py:412
  12.6 1.7 %collective-permute-start.3 = (bf16[64,64]{1,0:T(8,128)(2,1)S(1)}, bf16[64,64]{1,0:T(8,128)(2,1)S(1)}, u32[]{:S(2)}, u32[]{:S(2)}) collective-permute-start(bf16[64,64]{1,0:T(8,128)(2,1)S(1)} %copy-done.2), channel_id=1, source_target_pairs={{0,1},{2,3},{4,5},{6,7},{8,9},{10,11},{12,13},{14,15},{1,0},{3,2},... | collective-permute-start | bytes 24584 | tf_op jit(solution)/shard_map/ppermute | solution.py:412
  15.3 8.6 %collective-permute-start.5 = (bf16[72,1024]{1,0:T(8,128)(2,1)S(1)}, bf16[72,1024]{1,0:T(8,128)(2,1)S(1)}, u32[]{:S(2)}, u32[]{:S(2)}) collective-permute-start(bf16[72,1024]{1,0:T(8,128)(2,1)S(1)} %get-tuple-element.40), channel_id=1, source_target_pairs={{0,2},{1,3},{4,6},{5,7},{8,10},{9,11},{12,14},{13,15},{2,0},{3,1},... | collective-permute-start | bytes 442376 | tf_op jit(solution)/shard_map/ppermute | solution.py:412
  18.4 1.3 %collective-permute-start.4 = (bf16[8,4608]{1,0:T(8,128)(2,1)S(1)}, bf16[8,4608]{1,0:T(8,128)(2,1)S(1)}, u32[]{:S(2)}, u32[]{:S(2)}) collective-permute-start(bf16[8,4608]{1,0:T(8,128)(2,1)S(1)} %collective-permute-done.1.rim.rim_own), channel_id=1, source_target_pairs={{0,1},{2,3},{4,5},{6,7},{8,9},{10,11},{12,13},{14,15},{1,0},{3,2},... | collective-permute-start | bytes 221192 | tf_op jit(solution)/shard_map/ppermute | solution.py:412
  19.9 4.0 %collective-permute-start.6 = (bf16[16,1024]{1,0:T(8,128)(2,1)S(1)}, bf16[16,1024]{1,0:T(8,128)(2,1)S(1)}, u32[]{:S(2)}, u32[]{:S(2)}) collective-permute-start(bf16[16,1024]{1,0:T(8,128)(2,1)S(1)} %get-tuple-element.41), channel_id=1, source_target_pairs={{0,2},{1,3},{4,6},{5,7},{8,10},{9,11},{12,14},{13,15},{2,0},{3,1},... | collective-permute-start | bytes 98312 | tf_op jit(solution)/shard_map/ppermute | solution.py:412
  24.2 14.6 %collective-permute-start.7 = (bf16[72,1024]{1,0:T(8,128)(2,1)S(1)}, bf16[72,1024]{1,0:T(8,128)(2,1)S(1)}, u32[]{:S(2)}, u32[]{:S(2)}) collective-permute-start(bf16[72,1024]{1,0:T(8,128)(2,1)S(1)} %get-tuple-element.43), channel_id=1, source_target_pairs={{0,4},{1,5},{2,6},{3,7},{8,12},{9,13},{10,14},{11,15},{4,0},{5,1},... | collective-permute-start | bytes 442376 | tf_op jit(solution)/shard_map/ppermute | solution.py:412
  25.8 12.9 %collective-permute-start.8 = (bf16[72,1024]{1,0:T(8,128)(2,1)S(1)}, bf16[72,1024]{1,0:T(8,128)(2,1)S(1)}, u32[]{:S(2)}, u32[]{:S(2)}) collective-permute-start(bf16[72,1024]{1,0:T(8,128)(2,1)S(1)} %get-tuple-element.43), channel_id=1, source_target_pairs={{4,8},{5,9},{6,10},{7,11},{8,4},{9,5},{10,6},{11,7},{20,24},{21,25... | collective-permute-start | bytes 442376 | tf_op jit(solution)/shard_map/ppermute | solution.py:412
  26.5 12.3 %collective-permute-start.9 = (bf16[64,1024]{1,0:T(8,128)(2,1)S(1)}, bf16[64,1024]{1,0:T(8,128)(2,1)S(1)}, u32[]{:S(2)}, u32[]{:S(2)}) collective-permute-start(bf16[64,1024]{1,0:T(8,128)(2,1)S(1)} %get-tuple-element.44), channel_id=1, source_target_pairs={{0,8},{1,9},{2,10},{3,11},{4,12},{5,13},{6,14},{7,15},{8,0},{9,1},... | collective-permute-start | bytes 393224 | tf_op jit(solution)/shard_map/ppermute | solution.py:412
  38.8 5.2 %copy-start = (f32[4096]{0:T(1024)S(1)}, f32[4096]{0:T(1024)}, u32[]{:S(2)}) copy-start(f32[4096]{0:T(1024)} %param.18) | copy-start | bytes 49156
  39.0 5.0 %collective-permute-start.10 = (bf16[64,1024]{1,0:T(8,128)(2,1)S(1)}, bf16[64,1024]{1,0:T(8,128)(2,1)S(1)}, u32[]{:S(2)}, u32[]{:S(2)}) collective-permute-start(bf16[64,1024]{1,0:T(8,128)(2,1)S(1)} %get-tuple-element.45), channel_id=1, source_target_pairs={{0,2},{1,3},{4,6},{5,7},{8,10},{9,11},{12,14},{13,15},{2,0},{3,1},... | collective-permute-start | bytes 393224 | tf_op jit(solution)/shard_map/ppermute | solution.py:412
  39.8 4.7 %collective-permute-start.12 = (bf16[64,1024]{1,0:T(8,128)(2,1)S(1)}, bf16[64,1024]{1,0:T(8,128)(2,1)S(1)}, u32[]{:S(2)}, u32[]{:S(2)}) collective-permute-start(bf16[64,1024]{1,0:T(8,128)(2,1)S(1)} %get-tuple-element.46.x0), channel_id=1, source_target_pairs={{0,1},{2,3},{4,5},{6,7},{8,9},{10,11},{12,13},{14,15},{1,0},{3,2},... | collective-permute-start | bytes 393224 | tf_op jit(solution)/shard_map/ppermute | solution.py:412
  44.0 2.0 %collective-permute-start.11 = (bf16[64,1024]{1,0:T(8,128)(2,1)S(1)}, bf16[64,1024]{1,0:T(8,128)(2,1)S(1)}, u32[]{:S(2)}, u32[]{:S(2)}) collective-permute-start(bf16[64,1024]{1,0:T(8,128)(2,1)S(1)} %collective-permute-done.10.x1), channel_id=1, source_target_pairs={{0,1},{2,3},{4,5},{6,7},{8,9},{10,11},{12,13},{14,15},{1,0},{3,2},... | collective-permute-start | bytes 393224 | tf_op jit(solution)/shard_map/ppermute | solution.py:412

commit v5 on v4

--- a/solution.py
+++ b/solution.py
@@ -103,9 +103,10 @@
     return jnp.where(first, a, b)
 
 
-def load_kernel(lengths, rows, raw, step_bias, rate_log, taps, bias, out_rows, rim, out_raw, out_bias, out_rate, out_taps,
-                out_conv, ends, lens, sems):
+def load_kernel(dims, lengths, rows, raw, step_bias, rate_log, taps, bias, out_rows, packed, out_raw, out_bias, out_rate, out_taps,
+                out_conv, ends, lens, rim, sems):
     tok = rows.shape[0]
+    inner, pair = dims
     moves = [
         (lengths, lens), (rows.at[tok - RIM :], rim), (raw, out_raw), (step_bias, out_bias), (rate_log, out_rate),
         (taps, out_taps), (bias, out_conv), (rows, out_rows),
@@ -118,8 +119,21 @@
     for i in range(lengths.shape[0]):
         end = end + lens[i]
         ends[i : i + 1] = jnp.broadcast_to(end, (1, 128))
-    for copy in copies[1:]:
+    copies[1].wait()
+    segments = []
+    for k in range(PAIR):
+        starts = ((k * inner // PAIR, inner // PAIR), (inner + k * pair, pair), (inner + (PAIR + k) * pair, pair))
+        segments.append(jnp.concatenate([rim[:, a : a + n].astype(F32) for a, n in starts], axis=1))
+    down = lax.broadcasted_iota(jnp.int32, segments[0].shape, 0)
+    mixed = jnp.where(down < 3, pltpu.roll(segments[0], 3, 0), pltpu.roll(segments[1], 6, 0))
+    packed[...] = mixed.astype(BF16)
+    for copy in copies[2:]:
         copy.wait()
+
+
+def unpacked(packed, lanes, second):
+    rows = packed[:, lanes].astype(F32)
+    return pick(second, pltpu.roll(rows, 2, 0), pltpu.roll(rows, 5, 0))
 
 
 def states_kernel(keep, dims, state, ends_ref, own, other, *rest):
@@ -201,30 +215,29 @@
     reached = [position - back >= starts for back in range(1, taps.shape[0])]
     scale = widen(compact[2 * tok + 8 :], selector(heads, PAIR * columns, width, core * (heads // PAIR)))
 
-    def mixed(lanes_at):
-        rim = pick(is_first, rim_own[:, lanes_at].astype(F32), rim_other[:, lanes_at].astype(F32))
+    def mixed(lanes_at, lanes):
+        rim = pick(is_first, unpacked(rim_own, lanes, False), unpacked(rim_other, lanes, True))
         top = pick(is_first, own[:RIM, lanes_at].astype(F32), other[:RIM, lanes_at].astype(F32))
         rows = jnp.concatenate([rim, top], axis=0)
         return convolve_few(rows, reached, taps[:, lanes_at], bias[lanes_at].reshape(1, 128)).astype(F32)
 
-    b_pair = mixed(pl.ds(at_b, 128))
+    b_pair = mixed(pl.ds(at_b, 128), slice(PAIR * columns, PAIR * columns + 128))
     half = b_pair.shape[1] // 2
     upper = row == 1
     for out, which in ((out_sent, row == 0), (out_kept, upper)):
         b_rows = pick(which, b_pair[:, half:], b_pair[:, :half])
-        out[RIM:] = jnp.zeros((RIM, columns), BF16)
-        out[RIM:, :half] = b_rows.astype(BF16)
+        out[:, columns:] = jnp.concatenate([b_rows, jnp.zeros_like(b_rows)], axis=1).astype(BF16)
     for j in range(columns // 128):
         lanes = slice(j * 128, (j + 1) * 128)
         behind = slice(columns + j * 128, columns + (j + 1) * 128)
-        low = mixed(pl.ds(pl.multiple_of(at + j * 128, 128), 128)) * scale[:, lanes]
-        high = mixed(pl.ds(pl.multiple_of(at + columns + j * 128, 128), 128)) * scale[:, behind]
-        out_sent[:RIM, lanes] = pick(upper, low, high).astype(BF16)
-        out_kept[:RIM, lanes] = pick(upper, high, low).astype(BF16)
-
-
-def late(rows, state):
-    return dot(rows[RIM:, :state], rows[:RIM], ((0,), (0,)))
+        low = mixed(pl.ds(pl.multiple_of(at + j * 128, 128), 128), lanes) * scale[:, lanes]
+        high = mixed(pl.ds(pl.multiple_of(at + columns + j * 128, 128), 128), behind) * scale[:, behind]
+        out_sent[:, lanes] = pick(upper, low, high).astype(BF16)
+        out_kept[:, lanes] = pick(upper, high, low).astype(BF16)
+
+
+def late(rows, state, columns):
+    return dot(rows[:, columns : columns + state], rows[:, :columns], ((0,), (0,)))
 
 
 def two_rows(passes, shape):
@@ -241,8 +254,8 @@
 
 def plane_kernel(state, own, own_rim, got, got_rim, out, far, base):
     upper = (lax.axis_index("seq") // 2) % 2 == 1
-    mine = own[:state] + late(own_rim[...], state)
-    theirs = got[:state].astype(F32) + late(got_rim[...], state)
+    mine = own[:state] + late(own_rim[...], state, own.shape[1])
+    theirs = got[:state].astype(F32) + late(got_rim[...], state, own.shape[1])
     my_pass, their_pass = own[state : state + 1], one_row(got[...])
     first, second = pick(upper, theirs, mine), pick(upper, mine, theirs)
     first_pass, later_pass = pick(upper, their_pass, my_pass), pick(upper, my_pass, their_pass)
@@ -293,8 +306,16 @@
     places = jnp.where(column < tok, column, jnp.where(column < tok + RIM, column - tok - RIM, tok))
     moves = shifts(starts, first, places, taps.shape[0])
 
+    def rim_rows(lanes):
+        if lanes.start < inner:
+            second, at = divmod(lanes.start, inner // PAIR)
+            return unpacked(rim, slice(at, at + BLOCK), second == 1)
+        at = inner // PAIR + (lanes.start - inner) // PAIR
+        halves = [unpacked(rim, slice(at, at + BLOCK // PAIR), k == 1) for k in range(PAIR)]
+        return jnp.concatenate(halves, axis=1)
+
     def mixed(lanes):
-        top = pick(is_first, rim[:, lanes].astype(F32), other[tok - RIM :, lanes].astype(F32))
+        top = pick(is_first, rim_rows(lanes), other[tok - RIM :, lanes].astype(F32))
         extra = jnp.concatenate([top, jnp.zeros_like(top)], axis=0).astype(BF16)
         rows = jnp.concatenate([own[:, lanes], extra], axis=0)
         return convolve(moves, rows, taps[:, lanes], bias[lanes].reshape(1, lanes.stop - lanes.start)).astype(F32)
@@ -435,16 +456,16 @@
     other = swap(mixer_in, cores)
     other_raw = swap(step_raw, cores)
     own, rim, raw, step_bias, rate_log, taps, bias, ends = pl.pallas_call(
-        load_kernel,
+        functools.partial(load_kernel, (inner, PAIR * state)),
         out_shape=(
-            jax.ShapeDtypeStruct((tok, channels), BF16), jax.ShapeDtypeStruct((RIM, channels), BF16),
+            jax.ShapeDtypeStruct((tok, channels), BF16), jax.ShapeDtypeStruct((RIM, channels // PAIR), BF16),
             jax.ShapeDtypeStruct((tok, heads), BF16), jax.ShapeDtypeStruct((1, heads), F32),
             jax.ShapeDtypeStruct((1, heads), F32), jax.ShapeDtypeStruct((taps_n, channels), F32),
             jax.ShapeDtypeStruct((channels,), F32), jax.ShapeDtypeStruct((doc_lengths.shape[0], 128), jnp.int32),
         ),
         in_specs=[HBM] * 7,
         out_specs=(VMEM,) * 8,
-        scratch_shapes=[pltpu.SMEM(doc_lengths.shape, jnp.int32), pltpu.SemaphoreType.DMA((8,))],
+        scratch_shapes=[pltpu.SMEM(doc_lengths.shape, jnp.int32), pltpu.VMEM((RIM, channels), BF16), pltpu.SemaphoreType.DMA((8,))],
         compiler_params=pltpu.CompilerParams(vmem_limit_bytes=4 << 20),
         name="load",
     )(*map(hbm, (doc_lengths, mixer_in, step_raw, step_bias, rate_log, conv_weight, conv_bias)))
@@ -474,7 +495,7 @@
     sent, compact = states(False, raw, other_raw, step_bias, rate_log)
     got = swap(sent, rows)
     kept, = states(True, compact)
-    corner = jax.ShapeDtypeStruct((2 * RIM, columns), BF16)
+    corner = jax.ShapeDtypeStruct((RIM, columns + 128), BF16)
     rim_sent, rim_kept = pl.pallas_call(
         functools.partial(rim_kernel, dims),
         out_shape=(corner, corner),

time: 47.4 us -> 46.3 us (0.977)
  waiting for transfers between devices: 18.6 us -> 17.9 us
    ppermute x13, waiting for transfers between devices: 18.6 us -> 17.9 us  [swap(): return lax.ppermute(block, 'seq', [*pairs, *((b, a) for a, b in pairs)])]
  transfers between devices with their start and end apart: 13 -> 13, of which waited for: 5 -> 5; matrix products, arithmetic and copies ran while one was open for 0% -> 0% of each run, Pallas kernels for 12% -> 13%
where the time goes in v5:
time: 46.3 us; the launch traced here: 46.2 us
  waiting for transfers between devices  17.9 us (39%)
  starting transfers between devices  16.9 us (37%)
  Pallas kernels  10.5 us (23%)
  local copies, waits for them, and re-layouts  0.66 us (1%)
    ppermute x13, waiting for transfers between devices, swap(): return lax.ppermute(block, 'seq', [*pairs, *((b, a) for a, b in pairs)])  17.9 us
    ppermute x13, starting transfers between devices, swap(): return lax.ppermute(block, 'seq', [*pairs, *((b, a) for a, b in pairs)])  16.9 us
    pallas_call x1, Pallas kernels, on_device(): pl.pallas_call(functools.partial(local_kernel, (heads, width, state, tok)...  3.53 us
    pallas_call x2, Pallas kernels, states(): pl.pallas_call(functools.partial(states_kernel, keep, dims, state), out_s...  1.86 us
    pallas_call x1, Pallas kernels, on_device(): pl.pallas_call(functools.partial(finish_near_kernel, width), out_shape=wh...  1.47 us
    pallas_call x1, Pallas kernels, on_device(): pl.pallas_call(functools.partial(load_kernel, (inner, PAIR * state)), out...  1.28 us
    pallas_call x1, Pallas kernels, on_device(): pl.pallas_call(functools.partial(finish_far_kernel, width), out_shape=who...  1.17 us
  transfers between devices with their start and end apart: 13, of which 5 were waited for; matrix products, arithmetic and copies ran while one was open for 0% of the time, Pallas kernels for 13%

profile of v5, /device:TPU:0, one launch (start us, length us, event | category | flops | bytes accessed | tf_op | source)
XLA Modules:
  0.0 46.2 jit_solution(6352821473693246773)
XLA Ops:
  0.0 0.5 %collective-permute-start = (bf16[64,4608]{1,0:T(8,128)(2,1)}, bf16[64,4608]{1,0:T(8,128)(2,1)S(1)}, u32[]{:S(2)}, u32[]{:S(2)}) collective-permute-start(bf16[64,4608]{1,0:T(8,128)(2,1)} %rows.1), channel_id=1, source_target_pairs={{0,1},{2,3},{4,5},{6,7},{8,9},{10,11},{12,13},{14,15},{1,0},{3,2},... | collective-permute-start | bytes 1769480 | tf_op jit(solution)/shard_map/ppermute | solution.py:433
  0.5 1.3 %load.1 = (bf16[64,4608]{1,0:T(8,128)(2,1)S(1)}, bf16[8,2304]{1,0:T(8,128)(2,1)S(1)}, bf16[64,64]{1,0:T(8,128)(2,1)S(1)}, f32[1,64]{1,0:T(1,128)S(1)}, f32[1,64]...) custom-call(s32[6]{0:T(128)} %lengths.1, bf16[64,4608]{1,0:T(8,128)(2,1)} %rows.1, ...), custom_call_target="tpu_custom_call" | custom-call | tf_op jit(solution)/shard_map/load/pallas_call | solution.py:458
  1.8 0.7 %collective-permute-start.1 = (bf16[8,2304]{1,0:T(8,128)(2,1)S(1)}, bf16[8,2304]{1,0:T(8,128)(2,1)S(1)}, u32[]{:S(2)}, u32[]{:S(2)}) collective-permute-start(bf16[8,2304]{1,0:T(8,128)(2,1)S(1)} %get-tuple-element.28), channel_id=1, source_target_pairs={{1,2},{3,4},{5,6},{7,8},{9,10},{11,12},{13,14},{2,1},{4,3},{6,5},{... | collective-permute-start | bytes 110600 | tf_op jit(solution)/shard_map/ppermute | solution.py:433
  2.5 0.6 %copy-done.1 = f32[64]{0:T(128)S(1)} copy-done((f32[64]{0:T(128)S(1)}, f32[64]{0:T(128)}, u32[]{:S(2)}) %copy-start.1) | copy-done | bytes 280
  3.1 3.5 %local_block.1 = (f32[64,4096]{1,0:T(8,128)S(1)}, f32[64,4096]{1,0:T(8,128)S(1)}, bf16[4,64,64]{2,1,0:T(8,128)(2,1)S(1)}, bf16[72,4096]{1,0:T(8,128)(2,1)S(1)}) custom-call(s32[6,128]{1,0:T(8,128)S(1)} %get-tuple-element.26.ends_ref.ends, bf16[64,4608]{1,0:T(8,128)(2,1)S(1)} %get-tuple-element.27.own, bf16[64,4608]{1,0:T(8,128)(2,1)S(1)} %collective-permute-done.other, ...), custom_call_target="tpu_custom_call" | custom-call | tf_op jit(solution)/shard_map/local_block/pallas_call | solution.py:523
  6.7 5.5 %collective-permute-start.2 = (bf16[72,4096]{1,0:T(8,128)(2,1)S(1)}, bf16[72,4096]{1,0:T(8,128)(2,1)S(1)}, u32[]{:S(2)}, u32[]{:S(2)}) collective-permute-start(bf16[72,4096]{1,0:T(8,128)(2,1)S(1)} %get-tuple-element.37), channel_id=1, source_target_pairs={{0,1},{2,3},{4,5},{6,7},{8,9},{10,11},{12,13},{14,15},{1,0},{3,2},... | collective-permute-start | bytes 1769480 | tf_op jit(solution)/shard_map/ppermute | solution.py:433
  12.3 1.6 %collective-permute-done.3.rest_1_ = bf16[64,64]{1,0:T(8,128)(2,1)S(1)} collective-permute-done((bf16[64,64]{1,0:T(8,128)(2,1)S(1)}, bf16[64,64]{1,0:T(8,128)(2,1)S(1)}, u32[]{:S(2)}, u32[]{:S(2)}) %collective-permute-start.3) | collective-permute-done | bytes 8224 | tf_op jit(solution)/shard_map/ppermute | solution.py:433
  13.9 1.0 %states_sent.1 = (bf16[72,1024]{1,0:T(8,128)(2,1)S(1)}, f32[144,64]{1,0:T(8,128)S(1)}) custom-call(s32[6,128]{1,0:T(8,128)S(1)} %get-tuple-element.26.ends_ref.ends, bf16[64,4608]{1,0:T(8,128)(2,1)S(1)} %get-tuple-element.27.own, bf16[64,4608]{1,0:T(8,128)(2,1)S(1)} %collective-permute-done.other, bf16[64,64]{1,0:T(8,128)(2,1)S(1)} %get-tuple-element.29.raw.rest_0_, ...), custom_call_target="tpu_custom_call" | custom-call | tf_op jit(solution)/shard_map/states_sent/pallas_call | solution.py:485
  14.9 3.1 %collective-permute-start.5 = (bf16[72,1024]{1,0:T(8,128)(2,1)S(1)}, bf16[72,1024]{1,0:T(8,128)(2,1)S(1)}, u32[]{:S(2)}, u32[]{:S(2)}) collective-permute-start(bf16[72,1024]{1,0:T(8,128)(2,1)S(1)} %get-tuple-element.40), channel_id=1, source_target_pairs={{0,2},{1,3},{4,6},{5,7},{8,10},{9,11},{12,14},{13,15},{2,0},{3,1},... | collective-permute-start | bytes 442376 | tf_op jit(solution)/shard_map/ppermute | solution.py:433
  18.1 1.1 %collective-permute-done.4.rim_other = bf16[8,2304]{1,0:T(8,128)(2,1)S(1)} collective-permute-done((bf16[8,2304]{1,0:T(8,128)(2,1)S(1)}, bf16[8,2304]{1,0:T(8,128)(2,1)S(1)}, u32[]{:S(2)}, u32[]{:S(2)}) %collective-permute-start.4) | collective-permute-done | bytes 36896 | tf_op jit(solution)/shard_map/ppermute | solution.py:433
  19.2 0.3 rim_terms.1
  19.7 0.8 %states_kept.1.own = f32[72,1024]{1,0:T(8,128)S(1)} custom-call(s32[6,128]{1,0:T(8,128)S(1)} %get-tuple-element.26.ends_ref.ends, bf16[64,4608]{1,0:T(8,128)(2,1)S(1)} %get-tuple-element.27.own, bf16[64,4608]{1,0:T(8,128)(2,1)S(1)} %collective-permute-done.other, f32[144,64]{1,0:T(8,128)S(1)} %get-tuple-element.38.rest_0_.compact, ...), custom_call_target="tpu_custom_call" | custom-call | tf_op jit(solution)/shard_map/states_kept/pallas_call | solution.py:485
  20.5 2.8 %collective-permute-done.6.got_rim = bf16[8,1152]{1,0:T(8,128)(2,1)S(1)} collective-permute-done((bf16[8,1152]{1,0:T(8,128)(2,1)S(1)}, bf16[8,1152]{1,0:T(8,128)(2,1)S(1)}, u32[]{:S(2)}, u32[]{:S(2)}) %collective-permute-start.6) | collective-permute-done | bytes 18464 | tf_op jit(solution)/shard_map/ppermute | solution.py:433
  23.3 0.3 plane_total.1
  23.6 1.6 %collective-permute-start.7 = (bf16[72,1024]{1,0:T(8,128)(2,1)S(1)}, bf16[72,1024]{1,0:T(8,128)(2,1)S(1)}, u32[]{:S(2)}, u32[]{:S(2)}) collective-permute-start(bf16[72,1024]{1,0:T(8,128)(2,1)S(1)} %get-tuple-element.43), channel_id=1, source_target_pairs={{0,4},{1,5},{2,6},{3,7},{8,12},{9,13},{10,14},{11,15},{4,0},{5,1},... | collective-permute-start | bytes 442376 | tf_op jit(solution)/shard_map/ppermute | solution.py:433
  25.2 0.7 %collective-permute-start.8 = (bf16[72,1024]{1,0:T(8,128)(2,1)S(1)}, bf16[72,1024]{1,0:T(8,128)(2,1)S(1)}, u32[]{:S(2)}, u32[]{:S(2)}) collective-permute-start(bf16[72,1024]{1,0:T(8,128)(2,1)S(1)} %get-tuple-element.43), channel_id=1, source_target_pairs={{4,8},{5,9},{6,10},{7,11},{8,4},{9,5},{10,6},{11,7},{20,24},{21,25... | collective-permute-start | bytes 442376 | tf_op jit(solution)/shard_map/ppermute | solution.py:433
  25.9 3.3 %collective-permute-start.9 = (bf16[64,1024]{1,0:T(8,128)(2,1)S(1)}, bf16[64,1024]{1,0:T(8,128)(2,1)S(1)}, u32[]{:S(2)}, u32[]{:S(2)}) collective-permute-start(bf16[64,1024]{1,0:T(8,128)(2,1)S(1)} %get-tuple-element.44), channel_id=1, source_target_pairs={{0,8},{1,9},{2,10},{3,11},{4,12},{5,13},{6,14},{7,15},{8,0},{9,1},... | collective-permute-start | bytes 393224 | tf_op jit(solution)/shard_map/ppermute | solution.py:433
  29.2 8.5 %collective-permute-done.9.rest_2_.rest_3_ = bf16[64,1024]{1,0:T(8,128)(2,1)S(1)} collective-permute-done((bf16[64,1024]{1,0:T(8,128)(2,1)S(1)}, bf16[64,1024]{1,0:T(8,128)(2,1)S(1)}, u32[]{:S(2)}, u32[]{:S(2)}) %collective-permute-start.9) | collective-permute-done | bytes 131104 | tf_op jit(solution)/shard_map/ppermute | solution.py:433
  37.8 0.2 arrive.1
  37.9 1.1 %collective-permute-start.10 = (bf16[64,1024]{1,0:T(8,128)(2,1)S(1)}, bf16[64,1024]{1,0:T(8,128)(2,1)S(1)}, u32[]{:S(2)}, u32[]{:S(2)}) collective-permute-start(bf16[64,1024]{1,0:T(8,128)(2,1)S(1)} %get-tuple-element.45), channel_id=1, source_target_pairs={{0,2},{1,3},{4,6},{5,7},{8,10},{9,11},{12,14},{13,15},{2,0},{3,1},... | collective-permute-start | bytes 393224 | tf_op jit(solution)/shard_map/ppermute | solution.py:433
  39.1 3.9 %collective-permute-done.10.x1 = bf16[64,1024]{1,0:T(8,128)(2,1)S(1)} collective-permute-done((bf16[64,1024]{1,0:T(8,128)(2,1)S(1)}, bf16[64,1024]{1,0:T(8,128)(2,1)S(1)}, u32[]{:S(2)}, u32[]{:S(2)}) %collective-permute-start.10) | collective-permute-done | bytes 131104 | tf_op jit(solution)/shard_map/ppermute | solution.py:433
  43.0 0.5 %finish_back.1.piece = bf16[64,1024]{1,0:T(8,128)(2,1)S(1)} custom-call(f32[64,4096]{1,0:T(8,128)S(1)} %get-tuple-element.34.a, f32[64,4096]{1,0:T(8,128)S(1)} %get-tuple-element.35.b, bf16[4,64,64]{2,1,0:T(8,128)(2,1)S(1)} %get-tuple-element.36.c, bf16[72,4096]{1,0:T(8,128)(2,1)S(1)} %collective-permute-done.2.prior, f32[1,4096]{1,0:T(1,128)S(1)} %bitcast.4, ...), custom_call_target="tpu_custom_call" | custom-call | tf_op jit(solution)/shard_map/finish_back/pallas_call | solution.py:554
  43.5 1.5 %finish_near.1.begun = bf16[64,4096]{1,0:T(8,128)(2,1)} custom-call(f32[64,4096]{1,0:T(8,128)S(1)} %get-tuple-element.34.a, f32[64,4096]{1,0:T(8,128)S(1)} %get-tuple-element.35.b, bf16[4,64,64]{2,1,0:T(8,128)(2,1)S(1)} %get-tuple-element.36.c, bf16[72,4096]{1,0:T(8,128)(2,1)S(1)} %collective-permute-done.2.prior, f32[1,4096]{1,0:T(1,128)S(1)} %bitcast.5, ...), custom_call_target="tpu_custom_call" | custom-call | tf_op jit(solution)/shard_map/finish_near/pallas_call | solution.py:550
  45.0 1.2 %finish_far.1 = bf16[64,4096]{1,0:T(8,128)(2,1)} custom-call(f32[64,4096]{1,0:T(8,128)S(1)} %get-tuple-element.34.a, f32[64,4096]{1,0:T(8,128)S(1)} %get-tuple-element.35.b, bf16[4,64,64]{2,1,0:T(8,128)(2,1)S(1)} %get-tuple-element.36.c, bf16[72,4096]{1,0:T(8,128)(2,1)S(1)} %collective-permute-done.2.prior, ...), custom_call_target="tpu_custom_call", output_to_operand_aliasing={{}: (7, {})} | custom-call | tf_op jit(solution)/shard_map/finish_far/pallas_call | solution.py:558
  (18 shorter events, 0.4 us)
Async XLA Ops:
  0.0 2.5 %collective-permute-start = (bf16[64,4608]{1,0:T(8,128)(2,1)}, bf16[64,4608]{1,0:T(8,128)(2,1)S(1)}, u32[]{:S(2)}, u32[]{:S(2)}) collective-permute-start(bf16[64,4608]{1,0:T(8,128)(2,1)} %rows.1), channel_id=1, source_target_pairs={{0,1},{2,3},{4,5},{6,7},{8,9},{10,11},{12,13},{14,15},{1,0},{3,2},... | collective-permute-start | bytes 1769480 | tf_op jit(solution)/shard_map/ppermute | solution.py:433
  1.8 0.7 %collective-permute-start.1 = (bf16[8,2304]{1,0:T(8,128)(2,1)S(1)}, bf16[8,2304]{1,0:T(8,128)(2,1)S(1)}, u32[]{:S(2)}, u32[]{:S(2)}) collective-permute-start(bf16[8,2304]{1,0:T(8,128)(2,1)S(1)} %get-tuple-element.28), channel_id=1, source_target_pairs={{1,2},{3,4},{5,6},{7,8},{9,10},{11,12},{13,14},{2,1},{4,3},{6,5},{... | collective-permute-start | bytes 110600 | tf_op jit(solution)/shard_map/ppermute | solution.py:433
  2.5 0.7 %copy-start.1 = (f32[64]{0:T(128)S(1)}, f32[64]{0:T(128)}, u32[]{:S(2)}) copy-start(f32[64]{0:T(128)} %param.17) | copy-start | bytes 772
  3.1 9.1 %copy-start.2 = (bf16[64,64]{1,0:T(8,128)(2,1)S(1)}, bf16[64,64]{1,0:T(8,128)(2,1)}, u32[]{:S(2)}) copy-start(bf16[64,64]{1,0:T(8,128)(2,1)} %raw.1) | copy-start | bytes 24580
  6.7 36.3 %collective-permute-start.2 = (bf16[72,4096]{1,0:T(8,128)(2,1)S(1)}, bf16[72,4096]{1,0:T(8,128)(2,1)S(1)}, u32[]{:S(2)}, u32[]{:S(2)}) collective-permute-start(bf16[72,4096]{1,0:T(8,128)(2,1)S(1)} %get-tuple-element.37), channel_id=1, source_target_pairs={{0,1},{2,3},{4,5},{6,7},{8,9},{10,11},{12,13},{14,15},{1,0},{3,2},... | collective-permute-start | bytes 1769480 | tf_op jit(solution)/shard_map/ppermute | solution.py:433
  12.2 1.7 %collective-permute-start.3 = (bf16[64,64]{1,0:T(8,128)(2,1)S(1)}, bf16[64,64]{1,0:T(8,128)(2,1)S(1)}, u32[]{:S(2)}, u32[]{:S(2)}) collective-permute-start(bf16[64,64]{1,0:T(8,128)(2,1)S(1)} %copy-done.2), channel_id=1, source_target_pairs={{0,1},{2,3},{4,5},{6,7},{8,9},{10,11},{12,13},{14,15},{1,0},{3,2},... | collective-permute-start | bytes 24584 | tf_op jit(solution)/shard_map/ppermute | solution.py:433
  14.9 8.4 %collective-permute-start.5 = (bf16[72,1024]{1,0:T(8,128)(2,1)S(1)}, bf16[72,1024]{1,0:T(8,128)(2,1)S(1)}, u32[]{:S(2)}, u32[]{:S(2)}) collective-permute-start(bf16[72,1024]{1,0:T(8,128)(2,1)S(1)} %get-tuple-element.40), channel_id=1, source_target_pairs={{0,2},{1,3},{4,6},{5,7},{8,10},{9,11},{12,14},{13,15},{2,0},{3,1},... | collective-permute-start | bytes 442376 | tf_op jit(solution)/shard_map/ppermute | solution.py:433
  18.0 1.2 %collective-permute-start.4 = (bf16[8,2304]{1,0:T(8,128)(2,1)S(1)}, bf16[8,2304]{1,0:T(8,128)(2,1)S(1)}, u32[]{:S(2)}, u32[]{:S(2)}) collective-permute-start(bf16[8,2304]{1,0:T(8,128)(2,1)S(1)} %collective-permute-done.1.rim.rim_own), channel_id=1, source_target_pairs={{0,1},{2,3},{4,5},{6,7},{8,9},{10,11},{12,13},{14,15},{1,0},{3,2},... | collective-permute-start | bytes 110600 | tf_op jit(solution)/shard_map/ppermute | solution.py:433
  19.5 3.8 %collective-permute-start.6 = (bf16[8,1152]{1,0:T(8,128)(2,1)S(1)}, bf16[8,1152]{1,0:T(8,128)(2,1)S(1)}, u32[]{:S(2)}, u32[]{:S(2)}) collective-permute-start(bf16[8,1152]{1,0:T(8,128)(2,1)S(1)} %get-tuple-element.41), channel_id=1, source_target_pairs={{0,2},{1,3},{4,6},{5,7},{8,10},{9,11},{12,14},{13,15},{2,0},{3,1},... | collective-permute-start | bytes 55304 | tf_op jit(solution)/shard_map/ppermute | solution.py:433
  23.6 14.2 %collective-permute-start.7 = (bf16[72,1024]{1,0:T(8,128)(2,1)S(1)}, bf16[72,1024]{1,0:T(8,128)(2,1)S(1)}, u32[]{:S(2)}, u32[]{:S(2)}) collective-permute-start(bf16[72,1024]{1,0:T(8,128)(2,1)S(1)} %get-tuple-element.43), channel_id=1, source_target_pairs={{0,4},{1,5},{2,6},{3,7},{8,12},{9,13},{10,14},{11,15},{4,0},{5,1},... | collective-permute-start | bytes 442376 | tf_op jit(solution)/shard_map/ppermute | solution.py:433
  25.2 12.5 %collective-permute-start.8 = (bf16[72,1024]{1,0:T(8,128)(2,1)S(1)}, bf16[72,1024]{1,0:T(8,128)(2,1)S(1)}, u32[]{:S(2)}, u32[]{:S(2)}) collective-permute-start(bf16[72,1024]{1,0:T(8,128)(2,1)S(1)} %get-tuple-element.43), channel_id=1, source_target_pairs={{4,8},{5,9},{6,10},{7,11},{8,4},{9,5},{10,6},{11,7},{20,24},{21,25... | collective-permute-start | bytes 442376 | tf_op jit(solution)/shard_map/ppermute | solution.py:433
  25.9 11.8 %collective-permute-start.9 = (bf16[64,1024]{1,0:T(8,128)(2,1)S(1)}, bf16[64,1024]{1,0:T(8,128)(2,1)S(1)}, u32[]{:S(2)}, u32[]{:S(2)}) collective-permute-start(bf16[64,1024]{1,0:T(8,128)(2,1)S(1)} %get-tuple-element.44), channel_id=1, source_target_pairs={{0,8},{1,9},{2,10},{3,11},{4,12},{5,13},{6,14},{7,15},{8,0},{9,1},... | collective-permute-start | bytes 393224 | tf_op jit(solution)/shard_map/ppermute | solution.py:433
  37.8 5.2 %copy-start = (f32[4096]{0:T(1024)S(1)}, f32[4096]{0:T(1024)}, u32[]{:S(2)}) copy-start(f32[4096]{0:T(1024)} %param.18) | copy-start | bytes 49156
  37.9 5.0 %collective-permute-start.10 = (bf16[64,1024]{1,0:T(8,128)(2,1)S(1)}, bf16[64,1024]{1,0:T(8,128)(2,1)S(1)}, u32[]{:S(2)}, u32[]{:S(2)}) collective-permute-start(bf16[64,1024]{1,0:T(8,128)(2,1)S(1)} %get-tuple-element.45), channel_id=1, source_target_pairs={{0,2},{1,3},{4,6},{5,7},{8,10},{9,11},{12,14},{13,15},{2,0},{3,1},... | collective-permute-start | bytes 393224 | tf_op jit(solution)/shard_map/ppermute | solution.py:433
  39.1 4.4 %collective-permute-start.12 = (bf16[64,1024]{1,0:T(8,128)(2,1)S(1)}, bf16[64,1024]{1,0:T(8,128)(2,1)S(1)}, u32[]{:S(2)}, u32[]{:S(2)}) collective-permute-start(bf16[64,1024]{1,0:T(8,128)(2,1)S(1)} %get-tuple-element.46.x0), channel_id=1, source_target_pairs={{0,1},{2,3},{4,5},{6,7},{8,9},{10,11},{12,13},{14,15},{1,0},{3,2},... | collective-permute-start | bytes 393224 | tf_op jit(solution)/shard_map/ppermute | solution.py:433
  43.0 2.0 %collective-permute-start.11 = (bf16[64,1024]{1,0:T(8,128)(2,1)S(1)}, bf16[64,1024]{1,0:T(8,128)(2,1)S(1)}, u32[]{:S(2)}, u32[]{:S(2)}) collective-permute-start(bf16[64,1024]{1,0:T(8,128)(2,1)S(1)} %collective-permute-done.10.x1), channel_id=1, source_target_pairs={{0,1},{2,3},{4,5},{6,7},{8,9},{10,11},{12,13},{14,15},{1,0},{3,2},... | collective-permute-start | bytes 393224 | tf_op jit(solution)/shard_map/ppermute | solution.py:433

commit v6 on v5

--- a/solution.py
+++ b/solution.py
@@ -194,11 +194,11 @@
     state_b = dot(b_rows[tok:], weighted[tok:], ((0,), (0,)))
     passes = scale[2 * tok + 1 : 2 * tok + 2]
     total = scale[2 * tok : 2 * tok + 1] * state_a + state_b
-    out[:state] = total.astype(out.dtype)
     if keep:
+        out[:state] = total
         out[state:] = jnp.broadcast_to(passes, (8, columns))
     else:
-        out[state:] = two_rows(passes, (8, columns))
+        pack(out, total, passes)
 
 
 def rim_kernel(dims, ends, own, other, rim_own, rim_other, compact, taps, bias, out_sent, out_kept):
@@ -247,22 +247,35 @@
     return both.astype(BF16)
 
 
-def one_row(payload):
-    wide = payload[-8:].astype(F32)
-    return wide[0:1] + wide[1:2]
+def pack(out, state, passes):
+    rows, tiles = state.shape[0], state.shape[1] // 128
+    spread = [slice(k * 128, (k + 1) * 128) for k in range(tiles)]
+    for k, lanes in enumerate(spread):
+        out[k * rows : (k + 1) * rows] = state[:, lanes].astype(BF16)
+    top, rest = split(jnp.concatenate([passes[:, lanes] for lanes in spread], axis=0), 2)
+    out[tiles * rows : tiles * rows + tiles] = top
+    out[tiles * rows + tiles :] = rest
+
+
+def unpack(payload, rows, columns):
+    tiles = columns // 128
+    state = jnp.concatenate([payload[k * rows : (k + 1) * rows].astype(F32) for k in range(tiles)], axis=1)
+    first = tiles * rows
+    wide = payload[first : first + tiles].astype(F32) + payload[first + tiles :].astype(F32)
+    return state, jnp.concatenate([wide[k : k + 1] for k in range(tiles)], axis=1)
 
 
 def plane_kernel(state, own, own_rim, got, got_rim, out, far, base):
     upper = (lax.axis_index("seq") // 2) % 2 == 1
     mine = own[:state] + late(own_rim[...], state, own.shape[1])
-    theirs = got[:state].astype(F32) + late(got_rim[...], state, own.shape[1])
-    my_pass, their_pass = own[state : state + 1], one_row(got[...])
+    theirs, their_pass = unpack(got[...], state, own.shape[1])
+    theirs = theirs + late(got_rim[...], state, own.shape[1])
+    my_pass = own[state : state + 1]
     first, second = pick(upper, theirs, mine), pick(upper, mine, theirs)
     first_pass, later_pass = pick(upper, their_pass, my_pass), pick(upper, my_pass, their_pass)
     total = (later_pass * first + second).astype(BF16)
-    out[:state] = total
     far[...] = total
-    out[state:] = two_rows(my_pass * their_pass, (8, own.shape[1]))
+    pack(out, total.astype(F32), my_pass * their_pass)
     base[:state] = first
     base[state:] = jnp.broadcast_to(first_pass, (8, own.shape[1]))
 
@@ -272,17 +285,17 @@
     index = lax.axis_index("seq")
     plane = index // GROUPS
     upper = (index // 2) % 2 == 1
-    state = None
     for back in range(reach, 0, -1):
         even, odd = parts[2 * (back - 1) : 2 * back]
         source = plane - back
         is_even = (source + 2 * back) // back % 2 == 0
         there = source >= 0
         arrived = jnp.where(there, pick(is_even, even[...].astype(F32), odd[...].astype(F32)), 0.0)
-        if state is None:
-            state = arrived[:rows]
+        if back == reach:
+            state = arrived
         else:
-            state = arrived[:rows] + one_row(arrived) * state
+            fresh, passes = unpack(arrived, rows, base.shape[1])
+            state = fresh + passes * state
     later = base[rows : rows + 1] * state + base[:rows]
     out_own[...] = pick(upper, later, state).astype(BF16)
     out_sent[...] = pick(upper, state, later).astype(BF16)
@@ -475,7 +488,7 @@
     def params(mib):
         return pltpu.CompilerParams(vmem_limit_bytes=mib << 20)
 
-    packed = jax.ShapeDtypeStruct((state + 8, columns), BF16)
+    packed = jax.ShapeDtypeStruct(((state + 2) * (columns // 128), 128), BF16)
     packed_wide = jax.ShapeDtypeStruct((state + 8, columns), F32)
     piece = jax.ShapeDtypeStruct((state, columns), BF16)
     dims = (heads, width, inner, tok)

time: 46.3 us -> 45.9 us (level)
  no operation moved by 1% of the time
where the time goes in v6:
time: 45.9 us; the launch traced here: 45.7 us
  waiting for transfers between devices  17.6 us (38%)
  starting transfers between devices  16.7 us (36%)
  Pallas kernels  10.5 us (23%)
  local copies, waits for them, and re-layouts  0.66 us (1%)
    ppermute x13, waiting for transfers between devices, swap(): return lax.ppermute(block, 'seq', [*pairs, *((b, a) for a, b in pairs)])  17.6 us
    ppermute x13, starting transfers between devices, swap(): return lax.ppermute(block, 'seq', [*pairs, *((b, a) for a, b in pairs)])  16.7 us
    pallas_call x1, Pallas kernels, on_device(): pl.pallas_call(functools.partial(local_kernel, (heads, width, state, tok)...  3.53 us
    pallas_call x2, Pallas kernels, states(): pl.pallas_call(functools.partial(states_kernel, keep, dims, state), out_s...  1.85 us
    pallas_call x1, Pallas kernels, on_device(): pl.pallas_call(functools.partial(finish_near_kernel, width), out_shape=wh...  1.47 us
    pallas_call x1, Pallas kernels, on_device(): pl.pallas_call(functools.partial(load_kernel, (inner, PAIR * state)), out...  1.28 us
    pallas_call x1, Pallas kernels, on_device(): pl.pallas_call(functools.partial(finish_far_kernel, width), out_shape=who...  1.17 us
  transfers between devices with their start and end apart: 13, of which 5 were waited for; matrix products, arithmetic and copies ran while one was open for 0% of the time, Pallas kernels for 13%

profile of v6, /device:TPU:0, one launch (start us, length us, event | category | flops | bytes accessed | tf_op | source)
XLA Modules:
  0.0 45.7 jit_solution(10220918434440950989)
XLA Ops:
  0.0 0.5 %collective-permute-start = (bf16[64,4608]{1,0:T(8,128)(2,1)}, bf16[64,4608]{1,0:T(8,128)(2,1)S(1)}, u32[]{:S(2)}, u32[]{:S(2)}) collective-permute-start(bf16[64,4608]{1,0:T(8,128)(2,1)} %rows.1), channel_id=1, source_target_pairs={{0,1},{2,3},{4,5},{6,7},{8,9},{10,11},{12,13},{14,15},{1,0},{3,2},... | collective-permute-start | bytes 1769480 | tf_op jit(solution)/shard_map/ppermute | solution.py:446
  0.5 1.3 %load.1 = (bf16[64,4608]{1,0:T(8,128)(2,1)S(1)}, bf16[8,2304]{1,0:T(8,128)(2,1)S(1)}, bf16[64,64]{1,0:T(8,128)(2,1)S(1)}, f32[1,64]{1,0:T(1,128)S(1)}, f32[1,64]...) custom-call(s32[6]{0:T(128)} %lengths.1, bf16[64,4608]{1,0:T(8,128)(2,1)} %rows.1, ...), custom_call_target="tpu_custom_call" | custom-call | tf_op jit(solution)/shard_map/load/pallas_call | solution.py:471
  1.8 0.7 %collective-permute-start.1 = (bf16[8,2304]{1,0:T(8,128)(2,1)S(1)}, bf16[8,2304]{1,0:T(8,128)(2,1)S(1)}, u32[]{:S(2)}, u32[]{:S(2)}) collective-permute-start(bf16[8,2304]{1,0:T(8,128)(2,1)S(1)} %get-tuple-element.28), channel_id=1, source_target_pairs={{1,2},{3,4},{5,6},{7,8},{9,10},{11,12},{13,14},{2,1},{4,3},{6,5},{... | collective-permute-start | bytes 110600 | tf_op jit(solution)/shard_map/ppermute | solution.py:446
  2.5 0.6 %copy-done.1 = f32[64]{0:T(128)S(1)} copy-done((f32[64]{0:T(128)S(1)}, f32[64]{0:T(128)}, u32[]{:S(2)}) %copy-start.1) | copy-done | bytes 280
  3.1 3.5 %local_block.1 = (f32[64,4096]{1,0:T(8,128)S(1)}, f32[64,4096]{1,0:T(8,128)S(1)}, bf16[4,64,64]{2,1,0:T(8,128)(2,1)S(1)}, bf16[72,4096]{1,0:T(8,128)(2,1)S(1)}) custom-call(s32[6,128]{1,0:T(8,128)S(1)} %get-tuple-element.26.ends_ref.ends, bf16[64,4608]{1,0:T(8,128)(2,1)S(1)} %get-tuple-element.27.own, bf16[64,4608]{1,0:T(8,128)(2,1)S(1)} %collective-permute-done.other, ...), custom_call_target="tpu_custom_call" | custom-call | tf_op jit(solution)/shard_map/local_block/pallas_call | solution.py:536
  6.7 5.5 %collective-permute-start.2 = (bf16[72,4096]{1,0:T(8,128)(2,1)S(1)}, bf16[72,4096]{1,0:T(8,128)(2,1)S(1)}, u32[]{:S(2)}, u32[]{:S(2)}) collective-permute-start(bf16[72,4096]{1,0:T(8,128)(2,1)S(1)} %get-tuple-element.37), channel_id=1, source_target_pairs={{0,1},{2,3},{4,5},{6,7},{8,9},{10,11},{12,13},{14,15},{1,0},{3,2},... | collective-permute-start | bytes 1769480 | tf_op jit(solution)/shard_map/ppermute | solution.py:446
  12.3 1.6 %collective-permute-done.3.rest_1_ = bf16[64,64]{1,0:T(8,128)(2,1)S(1)} collective-permute-done((bf16[64,64]{1,0:T(8,128)(2,1)S(1)}, bf16[64,64]{1,0:T(8,128)(2,1)S(1)}, u32[]{:S(2)}, u32[]{:S(2)}) %collective-permute-start.3) | collective-permute-done | bytes 8224 | tf_op jit(solution)/shard_map/ppermute | solution.py:446
  13.9 1.0 %states_sent.1 = (bf16[528,128]{1,0:T(8,128)(2,1)S(1)}, f32[144,64]{1,0:T(8,128)S(1)}) custom-call(s32[6,128]{1,0:T(8,128)S(1)} %get-tuple-element.26.ends_ref.ends, bf16[64,4608]{1,0:T(8,128)(2,1)S(1)} %get-tuple-element.27.own, bf16[64,4608]{1,0:T(8,128)(2,1)S(1)} %collective-permute-done.other, bf16[64,64]{1,0:T(8,128)(2,1)S(1)} %get-tuple-element.29.raw.rest_0_, ...), custom_call_target="tpu_custom_call" | custom-call | tf_op jit(solution)/shard_map/states_sent/pallas_call | solution.py:498
  14.9 3.1 %collective-permute-start.5 = (bf16[528,128]{1,0:T(8,128)(2,1)S(1)}, bf16[528,128]{1,0:T(8,128)(2,1)S(1)}, u32[]{:S(2)}, u32[]{:S(2)}) collective-permute-start(bf16[528,128]{1,0:T(8,128)(2,1)S(1)} %get-tuple-element.40), channel_id=1, source_target_pairs={{0,2},{1,3},{4,6},{5,7},{8,10},{9,11},{12,14},{13,15},{2,0},{3,1},... | collective-permute-start | bytes 405512 | tf_op jit(solution)/shard_map/ppermute | solution.py:446
  18.1 1.1 %collective-permute-done.4.rim_other = bf16[8,2304]{1,0:T(8,128)(2,1)S(1)} collective-permute-done((bf16[8,2304]{1,0:T(8,128)(2,1)S(1)}, bf16[8,2304]{1,0:T(8,128)(2,1)S(1)}, u32[]{:S(2)}, u32[]{:S(2)}) %collective-permute-start.4) | collective-permute-done | bytes 36896 | tf_op jit(solution)/shard_map/ppermute | solution.py:446
  19.2 0.3 rim_terms.1
  19.7 0.8 %states_kept.1.own = f32[72,1024]{1,0:T(8,128)S(1)} custom-call(s32[6,128]{1,0:T(8,128)S(1)} %get-tuple-element.26.ends_ref.ends, bf16[64,4608]{1,0:T(8,128)(2,1)S(1)} %get-tuple-element.27.own, bf16[64,4608]{1,0:T(8,128)(2,1)S(1)} %collective-permute-done.other, f32[144,64]{1,0:T(8,128)S(1)} %get-tuple-element.38.rest_0_.compact, ...), custom_call_target="tpu_custom_call" | custom-call | tf_op jit(solution)/shard_map/states_kept/pallas_call | solution.py:498
  20.5 2.8 %collective-permute-done.6.got_rim = bf16[8,1152]{1,0:T(8,128)(2,1)S(1)} collective-permute-done((bf16[8,1152]{1,0:T(8,128)(2,1)S(1)}, bf16[8,1152]{1,0:T(8,128)(2,1)S(1)}, u32[]{:S(2)}, u32[]{:S(2)}) %collective-permute-start.6) | collective-permute-done | bytes 18464 | tf_op jit(solution)/shard_map/ppermute | solution.py:446
  23.3 0.3 plane_total.1
  23.6 1.6 %collective-permute-start.7 = (bf16[528,128]{1,0:T(8,128)(2,1)S(1)}, bf16[528,128]{1,0:T(8,128)(2,1)S(1)}, u32[]{:S(2)}, u32[]{:S(2)}) collective-permute-start(bf16[528,128]{1,0:T(8,128)(2,1)S(1)} %get-tuple-element.43), channel_id=1, source_target_pairs={{0,4},{1,5},{2,6},{3,7},{8,12},{9,13},{10,14},{11,15},{4,0},{5,1},... | collective-permute-start | bytes 405512 | tf_op jit(solution)/shard_map/ppermute | solution.py:446
  25.2 0.7 %collective-permute-start.8 = (bf16[528,128]{1,0:T(8,128)(2,1)S(1)}, bf16[528,128]{1,0:T(8,128)(2,1)S(1)}, u32[]{:S(2)}, u32[]{:S(2)}) collective-permute-start(bf16[528,128]{1,0:T(8,128)(2,1)S(1)} %get-tuple-element.43), channel_id=1, source_target_pairs={{4,8},{5,9},{6,10},{7,11},{8,4},{9,5},{10,6},{11,7},{20,24},{21,25... | collective-permute-start | bytes 405512 | tf_op jit(solution)/shard_map/ppermute | solution.py:446
  25.9 3.2 %collective-permute-start.9 = (bf16[64,1024]{1,0:T(8,128)(2,1)S(1)}, bf16[64,1024]{1,0:T(8,128)(2,1)S(1)}, u32[]{:S(2)}, u32[]{:S(2)}) collective-permute-start(bf16[64,1024]{1,0:T(8,128)(2,1)S(1)} %get-tuple-element.44), channel_id=1, source_target_pairs={{0,8},{1,9},{2,10},{3,11},{4,12},{5,13},{6,14},{7,15},{8,0},{9,1},... | collective-permute-start | bytes 393224 | tf_op jit(solution)/shard_map/ppermute | solution.py:446
  29.1 8.2 %collective-permute-done.9.rest_2_.rest_3_ = bf16[64,1024]{1,0:T(8,128)(2,1)S(1)} collective-permute-done((bf16[64,1024]{1,0:T(8,128)(2,1)S(1)}, bf16[64,1024]{1,0:T(8,128)(2,1)S(1)}, u32[]{:S(2)}, u32[]{:S(2)}) %collective-permute-start.9) | collective-permute-done | bytes 131104 | tf_op jit(solution)/shard_map/ppermute | solution.py:446
  37.3 0.2 arrive.1
  37.5 1.1 %collective-permute-start.10 = (bf16[64,1024]{1,0:T(8,128)(2,1)S(1)}, bf16[64,1024]{1,0:T(8,128)(2,1)S(1)}, u32[]{:S(2)}, u32[]{:S(2)}) collective-permute-start(bf16[64,1024]{1,0:T(8,128)(2,1)S(1)} %get-tuple-element.45), channel_id=1, source_target_pairs={{0,2},{1,3},{4,6},{5,7},{8,10},{9,11},{12,14},{13,15},{2,0},{3,1},... | collective-permute-start | bytes 393224 | tf_op jit(solution)/shard_map/ppermute | solution.py:446
  38.6 3.9 %collective-permute-done.10.x1 = bf16[64,1024]{1,0:T(8,128)(2,1)S(1)} collective-permute-done((bf16[64,1024]{1,0:T(8,128)(2,1)S(1)}, bf16[64,1024]{1,0:T(8,128)(2,1)S(1)}, u32[]{:S(2)}, u32[]{:S(2)}) %collective-permute-start.10) | collective-permute-done | bytes 131104 | tf_op jit(solution)/shard_map/ppermute | solution.py:446
  42.5 0.5 %finish_back.1.piece = bf16[64,1024]{1,0:T(8,128)(2,1)S(1)} custom-call(f32[64,4096]{1,0:T(8,128)S(1)} %get-tuple-element.34.a, f32[64,4096]{1,0:T(8,128)S(1)} %get-tuple-element.35.b, bf16[4,64,64]{2,1,0:T(8,128)(2,1)S(1)} %get-tuple-element.36.c, bf16[72,4096]{1,0:T(8,128)(2,1)S(1)} %collective-permute-done.2.prior, f32[1,4096]{1,0:T(1,128)S(1)} %bitcast.4, ...), custom_call_target="tpu_custom_call" | custom-call | tf_op jit(solution)/shard_map/finish_back/pallas_call | solution.py:567
  43.0 1.5 %finish_near.1.begun = bf16[64,4096]{1,0:T(8,128)(2,1)} custom-call(f32[64,4096]{1,0:T(8,128)S(1)} %get-tuple-element.34.a, f32[64,4096]{1,0:T(8,128)S(1)} %get-tuple-element.35.b, bf16[4,64,64]{2,1,0:T(8,128)(2,1)S(1)} %get-tuple-element.36.c, bf16[72,4096]{1,0:T(8,128)(2,1)S(1)} %collective-permute-done.2.prior, f32[1,4096]{1,0:T(1,128)S(1)} %bitcast.5, ...), custom_call_target="tpu_custom_call" | custom-call | tf_op jit(solution)/shard_map/finish_near/pallas_call | solution.py:563
  44.5 1.2 %finish_far.1 = bf16[64,4096]{1,0:T(8,128)(2,1)} custom-call(f32[64,4096]{1,0:T(8,128)S(1)} %get-tuple-element.34.a, f32[64,4096]{1,0:T(8,128)S(1)} %get-tuple-element.35.b, bf16[4,64,64]{2,1,0:T(8,128)(2,1)S(1)} %get-tuple-element.36.c, bf16[72,4096]{1,0:T(8,128)(2,1)S(1)} %collective-permute-done.2.prior, ...), custom_call_target="tpu_custom_call", output_to_operand_aliasing={{}: (7, {})} | custom-call | tf_op jit(solution)/shard_map/finish_far/pallas_call | solution.py:571
  (18 shorter events, 0.4 us)
Async XLA Ops:
  0.0 2.5 %collective-permute-start = (bf16[64,4608]{1,0:T(8,128)(2,1)}, bf16[64,4608]{1,0:T(8,128)(2,1)S(1)}, u32[]{:S(2)}, u32[]{:S(2)}) collective-permute-start(bf16[64,4608]{1,0:T(8,128)(2,1)} %rows.1), channel_id=1, source_target_pairs={{0,1},{2,3},{4,5},{6,7},{8,9},{10,11},{12,13},{14,15},{1,0},{3,2},... | collective-permute-start | bytes 1769480 | tf_op jit(solution)/shard_map/ppermute | solution.py:446
  1.8 0.7 %collective-permute-start.1 = (bf16[8,2304]{1,0:T(8,128)(2,1)S(1)}, bf16[8,2304]{1,0:T(8,128)(2,1)S(1)}, u32[]{:S(2)}, u32[]{:S(2)}) collective-permute-start(bf16[8,2304]{1,0:T(8,128)(2,1)S(1)} %get-tuple-element.28), channel_id=1, source_target_pairs={{1,2},{3,4},{5,6},{7,8},{9,10},{11,12},{13,14},{2,1},{4,3},{6,5},{... | collective-permute-start | bytes 110600 | tf_op jit(solution)/shard_map/ppermute | solution.py:446
  2.5 0.7 %copy-start.1 = (f32[64]{0:T(128)S(1)}, f32[64]{0:T(128)}, u32[]{:S(2)}) copy-start(f32[64]{0:T(128)} %param.17) | copy-start | bytes 772
  3.1 9.1 %copy-start.2 = (bf16[64,64]{1,0:T(8,128)(2,1)S(1)}, bf16[64,64]{1,0:T(8,128)(2,1)}, u32[]{:S(2)}) copy-start(bf16[64,64]{1,0:T(8,128)(2,1)} %raw.1) | copy-start | bytes 24580
  6.7 35.8 %collective-permute-start.2 = (bf16[72,4096]{1,0:T(8,128)(2,1)S(1)}, bf16[72,4096]{1,0:T(8,128)(2,1)S(1)}, u32[]{:S(2)}, u32[]{:S(2)}) collective-permute-start(bf16[72,4096]{1,0:T(8,128)(2,1)S(1)} %get-tuple-element.37), channel_id=1, source_target_pairs={{0,1},{2,3},{4,5},{6,7},{8,9},{10,11},{12,13},{14,15},{1,0},{3,2},... | collective-permute-start | bytes 1769480 | tf_op jit(solution)/shard_map/ppermute | solution.py:446
  12.2 1.7 %collective-permute-start.3 = (bf16[64,64]{1,0:T(8,128)(2,1)S(1)}, bf16[64,64]{1,0:T(8,128)(2,1)S(1)}, u32[]{:S(2)}, u32[]{:S(2)}) collective-permute-start(bf16[64,64]{1,0:T(8,128)(2,1)S(1)} %copy-done.2), channel_id=1, source_target_pairs={{0,1},{2,3},{4,5},{6,7},{8,9},{10,11},{12,13},{14,15},{1,0},{3,2},... | collective-permute-start | bytes 24584 | tf_op jit(solution)/shard_map/ppermute | solution.py:446
  14.9 8.4 %collective-permute-start.5 = (bf16[528,128]{1,0:T(8,128)(2,1)S(1)}, bf16[528,128]{1,0:T(8,128)(2,1)S(1)}, u32[]{:S(2)}, u32[]{:S(2)}) collective-permute-start(bf16[528,128]{1,0:T(8,128)(2,1)S(1)} %get-tuple-element.40), channel_id=1, source_target_pairs={{0,2},{1,3},{4,6},{5,7},{8,10},{9,11},{12,14},{13,15},{2,0},{3,1},... | collective-permute-start | bytes 405512 | tf_op jit(solution)/shard_map/ppermute | solution.py:446
  18.0 1.2 %collective-permute-start.4 = (bf16[8,2304]{1,0:T(8,128)(2,1)S(1)}, bf16[8,2304]{1,0:T(8,128)(2,1)S(1)}, u32[]{:S(2)}, u32[]{:S(2)}) collective-permute-start(bf16[8,2304]{1,0:T(8,128)(2,1)S(1)} %collective-permute-done.1.rim.rim_own), channel_id=1, source_target_pairs={{0,1},{2,3},{4,5},{6,7},{8,9},{10,11},{12,13},{14,15},{1,0},{3,2},... | collective-permute-start | bytes 110600 | tf_op jit(solution)/shard_map/ppermute | solution.py:446
  19.5 3.8 %collective-permute-start.6 = (bf16[8,1152]{1,0:T(8,128)(2,1)S(1)}, bf16[8,1152]{1,0:T(8,128)(2,1)S(1)}, u32[]{:S(2)}, u32[]{:S(2)}) collective-permute-start(bf16[8,1152]{1,0:T(8,128)(2,1)S(1)} %get-tuple-element.41), channel_id=1, source_target_pairs={{0,2},{1,3},{4,6},{5,7},{8,10},{9,11},{12,14},{13,15},{2,0},{3,1},... | collective-permute-start | bytes 55304 | tf_op jit(solution)/shard_map/ppermute | solution.py:446
  23.6 13.7 %collective-permute-start.7 = (bf16[528,128]{1,0:T(8,128)(2,1)S(1)}, bf16[528,128]{1,0:T(8,128)(2,1)S(1)}, u32[]{:S(2)}, u32[]{:S(2)}) collective-permute-start(bf16[528,128]{1,0:T(8,128)(2,1)S(1)} %get-tuple-element.43), channel_id=1, source_target_pairs={{0,4},{1,5},{2,6},{3,7},{8,12},{9,13},{10,14},{11,15},{4,0},{5,1},... | collective-permute-start | bytes 405512 | tf_op jit(solution)/shard_map/ppermute | solution.py:446
  25.2 12.0 %collective-permute-start.8 = (bf16[528,128]{1,0:T(8,128)(2,1)S(1)}, bf16[528,128]{1,0:T(8,128)(2,1)S(1)}, u32[]{:S(2)}, u32[]{:S(2)}) collective-permute-start(bf16[528,128]{1,0:T(8,128)(2,1)S(1)} %get-tuple-element.43), channel_id=1, source_target_pairs={{4,8},{5,9},{6,10},{7,11},{8,4},{9,5},{10,6},{11,7},{20,24},{21,25... | collective-permute-start | bytes 405512 | tf_op jit(solution)/shard_map/ppermute | solution.py:446
  25.9 11.4 %collective-permute-start.9 = (bf16[64,1024]{1,0:T(8,128)(2,1)S(1)}, bf16[64,1024]{1,0:T(8,128)(2,1)S(1)}, u32[]{:S(2)}, u32[]{:S(2)}) collective-permute-start(bf16[64,1024]{1,0:T(8,128)(2,1)S(1)} %get-tuple-element.44), channel_id=1, source_target_pairs={{0,8},{1,9},{2,10},{3,11},{4,12},{5,13},{6,14},{7,15},{8,0},{9,1},... | collective-permute-start | bytes 393224 | tf_op jit(solution)/shard_map/ppermute | solution.py:446
  37.3 5.2 %copy-start = (f32[4096]{0:T(1024)S(1)}, f32[4096]{0:T(1024)}, u32[]{:S(2)}) copy-start(f32[4096]{0:T(1024)} %param.18) | copy-start | bytes 49156
  37.5 5.0 %collective-permute-start.10 = (bf16[64,1024]{1,0:T(8,128)(2,1)S(1)}, bf16[64,1024]{1,0:T(8,128)(2,1)S(1)}, u32[]{:S(2)}, u32[]{:S(2)}) collective-permute-start(bf16[64,1024]{1,0:T(8,128)(2,1)S(1)} %get-tuple-element.45), channel_id=1, source_target_pairs={{0,2},{1,3},{4,6},{5,7},{8,10},{9,11},{12,14},{13,15},{2,0},{3,1},... | collective-permute-start | bytes 393224 | tf_op jit(solution)/shard_map/ppermute | solution.py:446
  38.6 4.5 %collective-permute-start.12 = (bf16[64,1024]{1,0:T(8,128)(2,1)S(1)}, bf16[64,1024]{1,0:T(8,128)(2,1)S(1)}, u32[]{:S(2)}, u32[]{:S(2)}) collective-permute-start(bf16[64,1024]{1,0:T(8,128)(2,1)S(1)} %get-tuple-element.46.x0), channel_id=1, source_target_pairs={{0,1},{2,3},{4,5},{6,7},{8,9},{10,11},{12,13},{14,15},{1,0},{3,2},... | collective-permute-start | bytes 393224 | tf_op jit(solution)/shard_map/ppermute | solution.py:446
  42.5 2.0 %collective-permute-start.11 = (bf16[64,1024]{1,0:T(8,128)(2,1)S(1)}, bf16[64,1024]{1,0:T(8,128)(2,1)S(1)}, u32[]{:S(2)}, u32[]{:S(2)}) collective-permute-start(bf16[64,1024]{1,0:T(8,128)(2,1)S(1)} %collective-permute-done.10.x1), channel_id=1, source_target_pairs={{0,1},{2,3},{4,5},{6,7},{8,9},{10,11},{12,13},{14,15},{1,0},{3,2},... | collective-permute-start | bytes 393224 | tf_op jit(solution)/shard_map/ppermute | solution.py:446

commit v7 on v6

--- a/solution.py
+++ b/solution.py
@@ -66,11 +66,11 @@
         column = lane + j * 128
         tiles.append(jnp.where((column >= start) & (column < start + width), 1.0, 0.0))
     once = jnp.concatenate(tiles, axis=1).astype(BF16)
-    return jnp.concatenate([once] * 3, axis=0)
+    return jnp.concatenate([once] * 2, axis=0)
 
 
 def widen(compact, chosen):
-    return dot(jnp.concatenate([p.astype(F32) for p in split(compact, 3)], axis=1).astype(BF16), chosen)
+    return dot(jnp.concatenate([p.astype(F32) for p in split(compact, 2)], axis=1).astype(BF16), chosen)
 
 
 def shifts(starts, first, places, count):
@@ -109,8 +109,12 @@
     inner, pair = dims
     moves = [
         (lengths, lens), (rows.at[tok - RIM :], rim), (raw, out_raw), (step_bias, out_bias), (rate_log, out_rate),
-        (taps, out_taps), (bias, out_conv), (rows, out_rows),
+        (taps, out_taps), (bias, out_conv),
     ]
+    core = lax.axis_index("seq") % 2
+    for at, size in ((core * (inner // PAIR), inner // PAIR), (inner + core * pair, pair)):
+        lanes = pl.ds(pl.multiple_of(at, size), size)
+        moves.append((rows.at[:, lanes], out_rows.at[:, lanes]))
     copies = [pltpu.make_async_copy(a, b, sems.at[k]) for k, (a, b) in enumerate(moves)]
     for copy in copies:
         copy.start()
@@ -301,11 +305,12 @@
     out_sent[...] = pick(upper, state, later).astype(BF16)
 
 
-def local_kernel(dims, ends_ref, own, other, rim, gate_hbm, raw, step_bias, rate_log, taps, bias, skip,
-                 a_out, b_out, c_out, s_out, gate, sem):
+def local_kernel(dims, ends_ref, own_hbm, other, rim, gate_hbm, raw, step_bias, rate_log, taps, bias, skip,
+                 a_out, b_out, c_out, s_out, gate, own, sems):
     heads, width, state, tok = dims
-    copy = pltpu.make_async_copy(gate_hbm, gate, sem)
-    copy.start()
+    copies = [pltpu.make_async_copy(own_hbm, own, sems.at[0]), pltpu.make_async_copy(gate_hbm, gate, sems.at[1])]
+    for copy in copies:
+        copy.start()
     index = lax.axis_index("seq")
     is_first = index % 2 == 0
     first = index * tok
@@ -333,11 +338,6 @@
         rows = jnp.concatenate([own[:, lanes], extra], axis=0)
         return convolve(moves, rows, taps[:, lanes], bias[lanes].reshape(1, lanes.stop - lanes.start)).astype(F32)
 
-    b_all, c_all = [], []
-    for j in range(2 * GROUPS * state // BLOCK):
-        pieces = mixed(slice(inner + j * BLOCK, inner + (j + 1) * BLOCK))
-        for k in range(BLOCK // state):
-            (b_all if len(b_all) < GROUPS else c_all).append(pieces[:, k * state : (k + 1) * state].astype(BF16))
     step, sums = log_sums(raw[...], step_bias[...], rate_log[...])
     ending_decay = jnp.exp(sums[tok - 1 :])
     passed = jnp.where(final[:, :heads] < first, ending_decay, 0.0)
@@ -348,7 +348,13 @@
     causal = (down >= across) & (across + first >= starts[:, :tok])
     here = position[:, :state] >= final[:, :state]
     entered = jnp.concatenate([starts] * (BLOCK // 128), axis=1) < first
-    copy.wait()
+    copies[0].wait()
+    b_all, c_all = [], []
+    for j in range(2 * GROUPS * state // BLOCK):
+        pieces = mixed(slice(inner + j * BLOCK, inner + (j + 1) * BLOCK))
+        for k in range(BLOCK // state):
+            (b_all if len(b_all) < GROUPS else c_all).append(pieces[:, k * state : (k + 1) * state].astype(BF16))
+    copies[1].wait()
     for g in range(GROUPS):
         wide = widen(whole[:, g * per : (g + 1) * per], chosen)
         b_rows, c_rows = b_all[g], c_all[g]
@@ -478,7 +484,7 @@
         ),
         in_specs=[HBM] * 7,
         out_specs=(VMEM,) * 8,
-        scratch_shapes=[pltpu.SMEM(doc_lengths.shape, jnp.int32), pltpu.VMEM((RIM, channels), BF16), pltpu.SemaphoreType.DMA((8,))],
+        scratch_shapes=[pltpu.SMEM(doc_lengths.shape, jnp.int32), pltpu.VMEM((RIM, channels), BF16), pltpu.SemaphoreType.DMA((9,))],
         compiler_params=pltpu.CompilerParams(vmem_limit_bytes=4 << 20),
         name="load",
     )(*map(hbm, (doc_lengths, mixer_in, step_raw, step_bias, rate_log, conv_weight, conv_bias)))
@@ -541,12 +547,12 @@
             jax.ShapeDtypeStruct((GROUPS, tok, state), BF16),
             jax.ShapeDtypeStruct((state + 8, inner), BF16),
         ),
-        in_specs=[VMEM] * 4 + [HBM] + [VMEM] * 6,
+        in_specs=[VMEM, HBM, VMEM, VMEM, HBM] + [VMEM] * 6,
         out_specs=(VMEM,) * 4,
-        scratch_shapes=[pltpu.VMEM((tok, inner), BF16), pltpu.SemaphoreType.DMA],
+        scratch_shapes=[pltpu.VMEM((tok, inner), BF16), pltpu.VMEM((tok, channels), BF16), pltpu.SemaphoreType.DMA((2,))],
         compiler_params=params(16),
         name="local_block",
-    )(ends, own, other, rim, hbm(gate_in), raw, step_bias, rate_log, taps, bias, skip_gain)
+    )(ends, hbm(mixer_in), other, rim, hbm(gate_in), raw, step_bias, rate_log, taps, bias, skip_gain)
     prior = swap(own_state, cores)
 
     x0, mine = pl.pallas_call(

time: 45.9 us -> 45.7 us (level)
    ppermute x13, starting transfers between devices: 16.7 us -> 16.3 us  [swap(): return lax.ppermute(block, 'seq', [*pairs, *((b, a) for a, b in pairs)])]
where the time goes in v7:
time: 45.7 us; the launch traced here: 45.5 us
  waiting for transfers between devices  18 us (39%)
  starting transfers between devices  16.3 us (36%)
  Pallas kernels  10.5 us (23%)
  local copies, waits for them, and re-layouts  0.66 us (1%)
    ppermute x13, waiting for transfers between devices, swap(): return lax.ppermute(block, 'seq', [*pairs, *((b, a) for a, b in pairs)])  18 us
    ppermute x13, starting transfers between devices, swap(): return lax.ppermute(block, 'seq', [*pairs, *((b, a) for a, b in pairs)])  16.3 us
    pallas_call x1, Pallas kernels, on_device(): pl.pallas_call(functools.partial(local_kernel, (heads, width, state, tok)...  3.61 us
    pallas_call x2, Pallas kernels, states(): pl.pallas_call(functools.partial(states_kernel, keep, dims, state), out_s...  1.86 us
    pallas_call x1, Pallas kernels, on_device(): pl.pallas_call(functools.partial(finish_near_kernel, width), out_shape=wh...  1.47 us
    pallas_call x1, Pallas kernels, on_device(): pl.pallas_call(functools.partial(load_kernel, (inner, PAIR * state)), out...  1.17 us
    pallas_call x1, Pallas kernels, on_device(): pl.pallas_call(functools.partial(finish_far_kernel, width), out_shape=who...  1.17 us
  transfers between devices with their start and end apart: 13, of which 5 were waited for; matrix products, arithmetic and copies ran while one was open for 0% of the time, Pallas kernels for 13%

profile of v7, /device:TPU:0, one launch (start us, length us, event | category | flops | bytes accessed | tf_op | source)
XLA Modules:
  0.0 45.5 jit_solution(4468109544031308832)
XLA Ops:
  0.0 0.5 %collective-permute-start = (bf16[64,4608]{1,0:T(8,128)(2,1)}, bf16[64,4608]{1,0:T(8,128)(2,1)S(1)}, u32[]{:S(2)}, u32[]{:S(2)}) collective-permute-start(bf16[64,4608]{1,0:T(8,128)(2,1)} %own_hbm.1), channel_id=1, source_target_pairs={{0,1},{2,3},{4,5},{6,7},{8,9},{10,11},{12,13},{14,15},{1,0},{3,2},... | collective-permute-start | bytes 1769480 | tf_op jit(solution)/shard_map/ppermute | solution.py:452
  0.5 1.2 %load.1 = (bf16[64,4608]{1,0:T(8,128)(2,1)S(1)}, bf16[8,2304]{1,0:T(8,128)(2,1)S(1)}, bf16[64,64]{1,0:T(8,128)(2,1)S(1)}, f32[1,64]{1,0:T(1,128)S(1)}, f32[1,64]...) custom-call(s32[6]{0:T(128)} %lengths.1, bf16[64,4608]{1,0:T(8,128)(2,1)} %own_hbm.1, ...), custom_call_target="tpu_custom_call" | custom-call | tf_op jit(solution)/shard_map/load/pallas_call | solution.py:477
  1.7 0.7 %collective-permute-start.1 = (bf16[8,2304]{1,0:T(8,128)(2,1)S(1)}, bf16[8,2304]{1,0:T(8,128)(2,1)S(1)}, u32[]{:S(2)}, u32[]{:S(2)}) collective-permute-start(bf16[8,2304]{1,0:T(8,128)(2,1)S(1)} %get-tuple-element.27), channel_id=1, source_target_pairs={{1,2},{3,4},{5,6},{7,8},{9,10},{11,12},{13,14},{2,1},{4,3},{6,5},{... | collective-permute-start | bytes 110600 | tf_op jit(solution)/shard_map/ppermute | solution.py:452
  2.4 0.6 %copy-done.1 = f32[64]{0:T(128)S(1)} copy-done((f32[64]{0:T(128)S(1)}, f32[64]{0:T(128)}, u32[]{:S(2)}) %copy-start.1) | copy-done | bytes 280
  3.0 3.6 %local_block.1 = (f32[64,4096]{1,0:T(8,128)S(1)}, f32[64,4096]{1,0:T(8,128)S(1)}, bf16[4,64,64]{2,1,0:T(8,128)(2,1)S(1)}, bf16[72,4096]{1,0:T(8,128)(2,1)S(1)}) custom-call(s32[6,128]{1,0:T(8,128)S(1)} %get-tuple-element.26.ends_ref.ends, bf16[64,4608]{1,0:T(8,128)(2,1)} %own_hbm.1, bf16[64,4608]{1,0:T(8,128)(2,1)S(1)} %collective-permute-done.other, ...), custom_call_target="tpu_custom_call" | custom-call | tf_op jit(solution)/shard_map/local_block/pallas_call | solution.py:542
  6.6 5.5 %collective-permute-start.2 = (bf16[72,4096]{1,0:T(8,128)(2,1)S(1)}, bf16[72,4096]{1,0:T(8,128)(2,1)S(1)}, u32[]{:S(2)}, u32[]{:S(2)}) collective-permute-start(bf16[72,4096]{1,0:T(8,128)(2,1)S(1)} %get-tuple-element.36), channel_id=1, source_target_pairs={{0,1},{2,3},{4,5},{6,7},{8,9},{10,11},{12,13},{14,15},{1,0},{3,2},... | collective-permute-start | bytes 1769480 | tf_op jit(solution)/shard_map/ppermute | solution.py:452
  12.3 1.6 %collective-permute-done.3.rest_1_ = bf16[64,64]{1,0:T(8,128)(2,1)S(1)} collective-permute-done((bf16[64,64]{1,0:T(8,128)(2,1)S(1)}, bf16[64,64]{1,0:T(8,128)(2,1)S(1)}, u32[]{:S(2)}, u32[]{:S(2)}) %collective-permute-start.3) | collective-permute-done | bytes 8224 | tf_op jit(solution)/shard_map/ppermute | solution.py:452
  13.8 1.0 %states_sent.1 = (bf16[528,128]{1,0:T(8,128)(2,1)S(1)}, f32[144,64]{1,0:T(8,128)S(1)}) custom-call(s32[6,128]{1,0:T(8,128)S(1)} %get-tuple-element.26.ends_ref.ends, bf16[64,4608]{1,0:T(8,128)(2,1)S(1)} %get-tuple-element.37.own, bf16[64,4608]{1,0:T(8,128)(2,1)S(1)} %collective-permute-done.other, bf16[64,64]{1,0:T(8,128)(2,1)S(1)} %get-tuple-element.28.raw.rest_0_, ...), custom_call_target="tpu_custom_call" | custom-call | tf_op jit(solution)/shard_map/states_sent/pallas_call | solution.py:504
  14.9 3.1 %collective-permute-start.5 = (bf16[528,128]{1,0:T(8,128)(2,1)S(1)}, bf16[528,128]{1,0:T(8,128)(2,1)S(1)}, u32[]{:S(2)}, u32[]{:S(2)}) collective-permute-start(bf16[528,128]{1,0:T(8,128)(2,1)S(1)} %get-tuple-element.40), channel_id=1, source_target_pairs={{0,2},{1,3},{4,6},{5,7},{8,10},{9,11},{12,14},{13,15},{2,0},{3,1},... | collective-permute-start | bytes 405512 | tf_op jit(solution)/shard_map/ppermute | solution.py:452
  18.1 1.1 %collective-permute-done.4.rim_other = bf16[8,2304]{1,0:T(8,128)(2,1)S(1)} collective-permute-done((bf16[8,2304]{1,0:T(8,128)(2,1)S(1)}, bf16[8,2304]{1,0:T(8,128)(2,1)S(1)}, u32[]{:S(2)}, u32[]{:S(2)}) %collective-permute-start.4) | collective-permute-done | bytes 36896 | tf_op jit(solution)/shard_map/ppermute | solution.py:452
  19.2 0.3 rim_terms.1
  19.5 0.2 collective-permute-start.6
  19.6 0.8 %states_kept.1.own = f32[72,1024]{1,0:T(8,128)S(1)} custom-call(s32[6,128]{1,0:T(8,128)S(1)} %get-tuple-element.26.ends_ref.ends, bf16[64,4608]{1,0:T(8,128)(2,1)S(1)} %get-tuple-element.37.own, bf16[64,4608]{1,0:T(8,128)(2,1)S(1)} %collective-permute-done.other, f32[144,64]{1,0:T(8,128)S(1)} %get-tuple-element.38.rest_0_.compact, ...), custom_call_target="tpu_custom_call" | custom-call | tf_op jit(solution)/shard_map/states_kept/pallas_call | solution.py:504
  20.5 2.8 %collective-permute-done.6.got_rim = bf16[8,1152]{1,0:T(8,128)(2,1)S(1)} collective-permute-done((bf16[8,1152]{1,0:T(8,128)(2,1)S(1)}, bf16[8,1152]{1,0:T(8,128)(2,1)S(1)}, u32[]{:S(2)}, u32[]{:S(2)}) %collective-permute-start.6) | collective-permute-done | bytes 18464 | tf_op jit(solution)/shard_map/ppermute | solution.py:452
  23.3 0.3 plane_total.1
  23.6 0.7 %collective-permute-start.8 = (bf16[528,128]{1,0:T(8,128)(2,1)S(1)}, bf16[528,128]{1,0:T(8,128)(2,1)S(1)}, u32[]{:S(2)}, u32[]{:S(2)}) collective-permute-start(bf16[528,128]{1,0:T(8,128)(2,1)S(1)} %get-tuple-element.43), channel_id=1, source_target_pairs={{4,8},{5,9},{6,10},{7,11},{8,4},{9,5},{10,6},{11,7},{20,24},{21,25... | collective-permute-start | bytes 405512 | tf_op jit(solution)/shard_map/ppermute | solution.py:452
  24.3 4.5 %collective-permute-start.7 = (bf16[528,128]{1,0:T(8,128)(2,1)S(1)}, bf16[528,128]{1,0:T(8,128)(2,1)S(1)}, u32[]{:S(2)}, u32[]{:S(2)}) collective-permute-start(bf16[528,128]{1,0:T(8,128)(2,1)S(1)} %get-tuple-element.43), channel_id=1, source_target_pairs={{0,4},{1,5},{2,6},{3,7},{8,12},{9,13},{10,14},{11,15},{4,0},{5,1},... | collective-permute-start | bytes 405512 | tf_op jit(solution)/shard_map/ppermute | solution.py:452
  28.7 8.4 %collective-permute-done.9.rest_2_.rest_3_ = bf16[64,1024]{1,0:T(8,128)(2,1)S(1)} collective-permute-done((bf16[64,1024]{1,0:T(8,128)(2,1)S(1)}, bf16[64,1024]{1,0:T(8,128)(2,1)S(1)}, u32[]{:S(2)}, u32[]{:S(2)}) %collective-permute-start.9) | collective-permute-done | bytes 131104 | tf_op jit(solution)/shard_map/ppermute | solution.py:452
  37.1 0.2 arrive.1
  37.3 1.0 %collective-permute-start.10 = (bf16[64,1024]{1,0:T(8,128)(2,1)S(1)}, bf16[64,1024]{1,0:T(8,128)(2,1)S(1)}, u32[]{:S(2)}, u32[]{:S(2)}) collective-permute-start(bf16[64,1024]{1,0:T(8,128)(2,1)S(1)} %get-tuple-element.45), channel_id=1, source_target_pairs={{0,2},{1,3},{4,6},{5,7},{8,10},{9,11},{12,14},{13,15},{2,0},{3,1},... | collective-permute-start | bytes 393224 | tf_op jit(solution)/shard_map/ppermute | solution.py:452
  38.3 4.0 %collective-permute-done.10.x1 = bf16[64,1024]{1,0:T(8,128)(2,1)S(1)} collective-permute-done((bf16[64,1024]{1,0:T(8,128)(2,1)S(1)}, bf16[64,1024]{1,0:T(8,128)(2,1)S(1)}, u32[]{:S(2)}, u32[]{:S(2)}) %collective-permute-start.10) | collective-permute-done | bytes 131104 | tf_op jit(solution)/shard_map/ppermute | solution.py:452
  42.4 0.5 %finish_back.1.piece = bf16[64,1024]{1,0:T(8,128)(2,1)S(1)} custom-call(f32[64,4096]{1,0:T(8,128)S(1)} %get-tuple-element.33.a, f32[64,4096]{1,0:T(8,128)S(1)} %get-tuple-element.34.b, bf16[4,64,64]{2,1,0:T(8,128)(2,1)S(1)} %get-tuple-element.35.c, bf16[72,4096]{1,0:T(8,128)(2,1)S(1)} %collective-permute-done.2.prior, f32[1,4096]{1,0:T(1,128)S(1)} %bitcast.4, ...), custom_call_target="tpu_custom_call" | custom-call | tf_op jit(solution)/shard_map/finish_back/pallas_call | solution.py:573
  42.9 1.5 %finish_near.1.begun = bf16[64,4096]{1,0:T(8,128)(2,1)} custom-call(f32[64,4096]{1,0:T(8,128)S(1)} %get-tuple-element.33.a, f32[64,4096]{1,0:T(8,128)S(1)} %get-tuple-element.34.b, bf16[4,64,64]{2,1,0:T(8,128)(2,1)S(1)} %get-tuple-element.35.c, bf16[72,4096]{1,0:T(8,128)(2,1)S(1)} %collective-permute-done.2.prior, f32[1,4096]{1,0:T(1,128)S(1)} %bitcast.5, ...), custom_call_target="tpu_custom_call" | custom-call | tf_op jit(solution)/shard_map/finish_near/pallas_call | solution.py:569
  44.4 1.2 %finish_far.1 = bf16[64,4096]{1,0:T(8,128)(2,1)} custom-call(f32[64,4096]{1,0:T(8,128)S(1)} %get-tuple-element.33.a, f32[64,4096]{1,0:T(8,128)S(1)} %get-tuple-element.34.b, bf16[4,64,64]{2,1,0:T(8,128)(2,1)S(1)} %get-tuple-element.35.c, bf16[72,4096]{1,0:T(8,128)(2,1)S(1)} %collective-permute-done.2.prior, ...), custom_call_target="tpu_custom_call", output_to_operand_aliasing={{}: (7, {})} | custom-call | tf_op jit(solution)/shard_map/finish_far/pallas_call | solution.py:577
  (18 shorter events, 0.2 us)
Async XLA Ops:
  0.0 2.4 %collective-permute-start = (bf16[64,4608]{1,0:T(8,128)(2,1)}, bf16[64,4608]{1,0:T(8,128)(2,1)S(1)}, u32[]{:S(2)}, u32[]{:S(2)}) collective-permute-start(bf16[64,4608]{1,0:T(8,128)(2,1)} %own_hbm.1), channel_id=1, source_target_pairs={{0,1},{2,3},{4,5},{6,7},{8,9},{10,11},{12,13},{14,15},{1,0},{3,2},... | collective-permute-start | bytes 1769480 | tf_op jit(solution)/shard_map/ppermute | solution.py:452
  1.7 0.7 %collective-permute-start.1 = (bf16[8,2304]{1,0:T(8,128)(2,1)S(1)}, bf16[8,2304]{1,0:T(8,128)(2,1)S(1)}, u32[]{:S(2)}, u32[]{:S(2)}) collective-permute-start(bf16[8,2304]{1,0:T(8,128)(2,1)S(1)} %get-tuple-element.27), channel_id=1, source_target_pairs={{1,2},{3,4},{5,6},{7,8},{9,10},{11,12},{13,14},{2,1},{4,3},{6,5},{... | collective-permute-start | bytes 110600 | tf_op jit(solution)/shard_map/ppermute | solution.py:452
  2.4 0.7 %copy-start.1 = (f32[64]{0:T(128)S(1)}, f32[64]{0:T(128)}, u32[]{:S(2)}) copy-start(f32[64]{0:T(128)} %param.17) | copy-start | bytes 772
  3.0 9.2 %copy-start.2 = (bf16[64,64]{1,0:T(8,128)(2,1)S(1)}, bf16[64,64]{1,0:T(8,128)(2,1)}, u32[]{:S(2)}) copy-start(bf16[64,64]{1,0:T(8,128)(2,1)} %raw.1) | copy-start | bytes 24580
  6.6 35.7 %collective-permute-start.2 = (bf16[72,4096]{1,0:T(8,128)(2,1)S(1)}, bf16[72,4096]{1,0:T(8,128)(2,1)S(1)}, u32[]{:S(2)}, u32[]{:S(2)}) collective-permute-start(bf16[72,4096]{1,0:T(8,128)(2,1)S(1)} %get-tuple-element.36), channel_id=1, source_target_pairs={{0,1},{2,3},{4,5},{6,7},{8,9},{10,11},{12,13},{14,15},{1,0},{3,2},... | collective-permute-start | bytes 1769480 | tf_op jit(solution)/shard_map/ppermute | solution.py:452
  12.2 1.7 %collective-permute-start.3 = (bf16[64,64]{1,0:T(8,128)(2,1)S(1)}, bf16[64,64]{1,0:T(8,128)(2,1)S(1)}, u32[]{:S(2)}, u32[]{:S(2)}) collective-permute-start(bf16[64,64]{1,0:T(8,128)(2,1)S(1)} %copy-done.2), channel_id=1, source_target_pairs={{0,1},{2,3},{4,5},{6,7},{8,9},{10,11},{12,13},{14,15},{1,0},{3,2},... | collective-permute-start | bytes 24584 | tf_op jit(solution)/shard_map/ppermute | solution.py:452
  14.9 8.4 %collective-permute-start.5 = (bf16[528,128]{1,0:T(8,128)(2,1)S(1)}, bf16[528,128]{1,0:T(8,128)(2,1)S(1)}, u32[]{:S(2)}, u32[]{:S(2)}) collective-permute-start(bf16[528,128]{1,0:T(8,128)(2,1)S(1)} %get-tuple-element.40), channel_id=1, source_target_pairs={{0,2},{1,3},{4,6},{5,7},{8,10},{9,11},{12,14},{13,15},{2,0},{3,1},... | collective-permute-start | bytes 405512 | tf_op jit(solution)/shard_map/ppermute | solution.py:452
  18.0 1.2 %collective-permute-start.4 = (bf16[8,2304]{1,0:T(8,128)(2,1)S(1)}, bf16[8,2304]{1,0:T(8,128)(2,1)S(1)}, u32[]{:S(2)}, u32[]{:S(2)}) collective-permute-start(bf16[8,2304]{1,0:T(8,128)(2,1)S(1)} %collective-permute-done.1.rim.rim_own), channel_id=1, source_target_pairs={{0,1},{2,3},{4,5},{6,7},{8,9},{10,11},{12,13},{14,15},{1,0},{3,2},... | collective-permute-start | bytes 110600 | tf_op jit(solution)/shard_map/ppermute | solution.py:452
  19.5 3.8 %collective-permute-start.6 = (bf16[8,1152]{1,0:T(8,128)(2,1)S(1)}, bf16[8,1152]{1,0:T(8,128)(2,1)S(1)}, u32[]{:S(2)}, u32[]{:S(2)}) collective-permute-start(bf16[8,1152]{1,0:T(8,128)(2,1)S(1)} %get-tuple-element.41), channel_id=1, source_target_pairs={{0,2},{1,3},{4,6},{5,7},{8,10},{9,11},{12,14},{13,15},{2,0},{3,1},... | collective-permute-start | bytes 55304 | tf_op jit(solution)/shard_map/ppermute | solution.py:452
  23.6 13.5 %collective-permute-start.8 = (bf16[528,128]{1,0:T(8,128)(2,1)S(1)}, bf16[528,128]{1,0:T(8,128)(2,1)S(1)}, u32[]{:S(2)}, u32[]{:S(2)}) collective-permute-start(bf16[528,128]{1,0:T(8,128)(2,1)S(1)} %get-tuple-element.43), channel_id=1, source_target_pairs={{4,8},{5,9},{6,10},{7,11},{8,4},{9,5},{10,6},{11,7},{20,24},{21,25... | collective-permute-start | bytes 405512 | tf_op jit(solution)/shard_map/ppermute | solution.py:452
  24.3 12.9 %collective-permute-start.7 = (bf16[528,128]{1,0:T(8,128)(2,1)S(1)}, bf16[528,128]{1,0:T(8,128)(2,1)S(1)}, u32[]{:S(2)}, u32[]{:S(2)}) collective-permute-start(bf16[528,128]{1,0:T(8,128)(2,1)S(1)} %get-tuple-element.43), channel_id=1, source_target_pairs={{0,4},{1,5},{2,6},{3,7},{8,12},{9,13},{10,14},{11,15},{4,0},{5,1},... | collective-permute-start | bytes 405512 | tf_op jit(solution)/shard_map/ppermute | solution.py:452
  28.7 8.4 %collective-permute-start.9 = (bf16[64,1024]{1,0:T(8,128)(2,1)S(1)}, bf16[64,1024]{1,0:T(8,128)(2,1)S(1)}, u32[]{:S(2)}, u32[]{:S(2)}) collective-permute-start(bf16[64,1024]{1,0:T(8,128)(2,1)S(1)} %get-tuple-element.44), channel_id=1, source_target_pairs={{0,8},{1,9},{2,10},{3,11},{4,12},{5,13},{6,14},{7,15},{8,0},{9,1},... | collective-permute-start | bytes 393224 | tf_op jit(solution)/shard_map/ppermute | solution.py:452
  37.1 5.2 %copy-start = (f32[4096]{0:T(1024)S(1)}, f32[4096]{0:T(1024)}, u32[]{:S(2)}) copy-start(f32[4096]{0:T(1024)} %param.18) | copy-start | bytes 49156
  37.3 5.0 %collective-permute-start.10 = (bf16[64,1024]{1,0:T(8,128)(2,1)S(1)}, bf16[64,1024]{1,0:T(8,128)(2,1)S(1)}, u32[]{:S(2)}, u32[]{:S(2)}) collective-permute-start(bf16[64,1024]{1,0:T(8,128)(2,1)S(1)} %get-tuple-element.45), channel_id=1, source_target_pairs={{0,2},{1,3},{4,6},{5,7},{8,10},{9,11},{12,14},{13,15},{2,0},{3,1},... | collective-permute-start | bytes 393224 | tf_op jit(solution)/shard_map/ppermute | solution.py:452
  38.3 4.5 %collective-permute-start.12 = (bf16[64,1024]{1,0:T(8,128)(2,1)S(1)}, bf16[64,1024]{1,0:T(8,128)(2,1)S(1)}, u32[]{:S(2)}, u32[]{:S(2)}) collective-permute-start(bf16[64,1024]{1,0:T(8,128)(2,1)S(1)} %get-tuple-element.46.x0), channel_id=1, source_target_pairs={{0,1},{2,3},{4,5},{6,7},{8,9},{10,11},{12,13},{14,15},{1,0},{3,2},... | collective-permute-start | bytes 393224 | tf_op jit(solution)/shard_map/ppermute | solution.py:452
  42.4 2.0 %collective-permute-start.11 = (bf16[64,1024]{1,0:T(8,128)(2,1)S(1)}, bf16[64,1024]{1,0:T(8,128)(2,1)S(1)}, u32[]{:S(2)}, u32[]{:S(2)}) collective-permute-start(bf16[64,1024]{1,0:T(8,128)(2,1)S(1)} %collective-permute-done.10.x1), channel_id=1, source_target_pairs={{0,1},{2,3},{4,5},{6,7},{8,9},{10,11},{12,13},{14,15},{1,0},{3,2},... | collective-permute-start | bytes 393224 | tf_op jit(solution)/shard_map/ppermute | solution.py:452
